TPU v7x, 32 devices: a whole 2x2x4 slice. The times are simulated.
32 devices in a mesh: grp: 2 (over y), bl: 4 (over z), ch: 4 (over x, core).
Axes of the slice: x: 2, y: 2, z: 4, core: 2. Of those that a mesh axis runs over, the one named last changes fastest.
Arguments:
- visibilities: bfloat16 [8, 128, 4096], P(None, 'ch', ('grp', 'bl')), parts along dimension 2, may hold values from -40 to 40
- sky_model: bfloat16 [8, 128, 4096], P(None, 'ch', ('grp', 'bl')), parts along dimension 2, may hold values from -4 to 4
- antenna_pairs: int32 [2, 4096], P(None, ('grp', 'bl')), parts along dimension 1, may hold values from 0 to 511, as said below
- tile_counts: int32 [8], P(('grp', 'bl')), parts along dimension 0, may hold values from 128 to 512, as said below
- usable_mask: int32 [128, 4096], P('ch', ('grp', 'bl')), parts along dimension 1, may hold values 0 or 1
Outputs:
- solved_gains: float32 [2, 2, 128, 1024], P(None, None, 'ch', ('grp', 'bl')), parts along dimension 3
- fitted_gains: float32 [2, 2, 128, 1024], P(None, None, 'ch', ('grp', 'bl')), parts along dimension 3
There are 2 independent parts, one for each index of `grp`. A program takes and returns all parts, laid end to end along the dimension named above; each array names one. Nothing has to cross between parts.
Inputs may be any that keep to these rules, and one draw needn't show every extreme that they name: `antenna_pairs`: the two stations of every slot differ. Tile t's baselines are its first tile_counts[t] slots; the later slots of a tile are not used. Some tile is full in every draw.
All inputs are finite; a program needn't handle non-finite values. No bound on the sum of `usable_mask` on one device may be relied on, other than what follows from the above.
Results may differ from a plain program's by a relative error of at most 0.0003.
Values may be sent and summed in bfloat16 or wider, within the bound.
No kernel may reach another device: no remote copies, remote signals or barrier semaphores. Data moves between devices by JAX's collectives and lax.ppermute only.
A program may use at most 64 MiB of HBM per device.

v0:
```python
import math

import jax
import jax.numpy as jnp
from jax import lax
from jax.sharding import PartitionSpec as P

STATION_COUNT = 512
SWEEPS = 2


damping = 4.0
highest = lax.Precision.HIGHEST


def split_parts(data):
    planes = data.astype(jnp.float32)
    shape_rest = planes.shape[1:]
    return (planes[:4].reshape((2, 2) + shape_rest), planes[4:].reshape((2, 2) + shape_rest))


def poly_basis(channel_total):
    node_values = (2.0 * jnp.arange(channel_total, dtype=jnp.float32) - (channel_total - 1)) / (
        channel_total - 1
    )
    basis_rows = []
    for degree in range(4):
        vector = node_values**degree
        for earlier in basis_rows:
            vector = vector - jnp.sum(vector * earlier) * earlier
        vector = vector / jnp.sqrt(jnp.sum(vector * vector))
        basis_rows.append(vector)
    return jnp.stack(basis_rows)


def contributions(
    model_real_part, model_imaginary, vis_real, vis_imag, first_gain, second_gain, weights
):
    second_real = second_gain[0][None]
    second_imag = second_gain[1][None]
    left_real = model_real_part * second_real + model_imaginary * second_imag
    left_imag = model_imaginary * second_real - model_real_part * second_imag
    first_num_real = jnp.sum(left_real * vis_real + left_imag * vis_imag, axis=1) * weights
    first_num_imag = jnp.sum(left_real * vis_imag - left_imag * vis_real, axis=1) * weights
    first_den = jnp.sum(left_real * left_real + left_imag * left_imag, axis=1) * weights
    first_real = first_gain[0][:, None]
    first_imag = first_gain[1][:, None]
    right_real = model_real_part * first_real - model_imaginary * first_imag
    right_imag = model_real_part * first_imag + model_imaginary * first_real
    second_num_real = jnp.sum(right_real * vis_real + right_imag * vis_imag, axis=0) * weights
    second_num_imag = jnp.sum(right_imag * vis_real - right_real * vis_imag, axis=0) * weights
    second_den = jnp.sum(right_real * right_real + right_imag * right_imag, axis=0) * weights
    return (
        jnp.stack([first_num_real, first_num_imag, first_den]),
        jnp.stack([second_num_real, second_num_imag, second_den]),
    )


def refresh(station_sums, previous):
    divisor = station_sums[2] + damping
    return jnp.stack(
        [
            (station_sums[0] + damping * previous[0]) / divisor,
            (station_sums[1] + damping * previous[1]) / divisor,
        ]
    )


def station_totals(end_first, end_second, first_endpoints, second_ends):
    total_slots = end_first.shape[3]
    flat_first = end_first.reshape(-1, total_slots)
    flat_second = end_second.reshape(-1, total_slots)
    block_rows = math.gcd(total_slots, 1024)
    block_count = total_slots // block_rows
    station_index = jnp.arange(STATION_COUNT, dtype=jnp.int32)

    def add_block(block, total):
        table_first = (first_endpoints[:, None] == station_index[None, :]).astype(jnp.float32)
        table_second = (second_ends[:, None] == station_index[None, :]).astype(jnp.float32)
        return (
            total
            + jnp.dot(
                flat_first, table_first, precision=highest, preferred_element_type=jnp.float32
            )
            + jnp.dot(
                flat_second, table_second, precision=highest, preferred_element_type=jnp.float32
            )
        )

    empty = jnp.zeros((flat_first.shape[0], STATION_COUNT), jnp.float32)
    summed = lax.fori_loop(0, block_count, add_block, empty)
    return summed.reshape(end_first.shape[:3] + (STATION_COUNT,))


def spread(owned_gains):
    return lax.all_gather(owned_gains, "bl", axis=3, tiled=True)


def local(visibilities, sky_model, antenna_pairs, tile_counts, usable_mask):
    vis_real, vis_imag = split_parts(visibilities)
    model_real_part, model_imaginary = split_parts(sky_model)
    channel_local = visibilities.shape[1]
    tile_rows = visibilities.shape[2]
    owner_count = lax.axis_size("bl")
    owned_count = STATION_COUNT // owner_count
    owner_start = lax.axis_index("bl") * owned_count
    live_slots = jnp.arange(tile_rows, dtype=jnp.int32) < tile_counts[0]
    weights = usable_mask.astype(jnp.float32) * live_slots.astype(jnp.float32)[None, :]
    channel_total = channel_local * lax.axis_size("ch")
    poly_rows = lax.dynamic_slice_in_dim(
        poly_basis(channel_total), lax.axis_index("ch") * channel_local, channel_local, 1
    )
    gain_state = jnp.stack(
        [
            jnp.ones((2, channel_local, STATION_COUNT), jnp.float32),
            jnp.zeros((2, channel_local, STATION_COUNT), jnp.float32),
        ]
    )
    solved = gain_state
    for iteration in range(SWEEPS):
        first_gain = jnp.take(gain_state, antenna_pairs[0], axis=3)
        second_gain = jnp.take(gain_state, antenna_pairs[1], axis=3)
        end_first, end_second = contributions(
            model_real_part, model_imaginary, vis_real, vis_imag, first_gain, second_gain, weights
        )
        partial_sums = station_totals(end_first, end_second, antenna_pairs[0], antenna_pairs[1])
        station_sums = lax.psum_scatter(partial_sums, "bl", scatter_dimension=3, tiled=True)
        previous = lax.dynamic_slice_in_dim(gain_state, owner_start, owned_count, 3)
        renewed = refresh(station_sums, previous)
        if iteration == 1:
            renewed = 0.5 * (renewed + previous)
        solved = renewed
        if iteration < SWEEPS - 1:
            gain_state = spread(renewed)
    local_moments = jnp.einsum("kc,rfca->krfa", poly_rows, solved, precision=highest)
    moments = lax.psum(local_moments, "ch")
    fitted = jnp.einsum("kc,krfa->rfca", poly_rows, moments, precision=highest)
    return (solved, fitted)


def solution(mesh):
    return jax.shard_map(
        local,
        mesh=mesh,
        in_specs=(
            P(None, "ch", ("grp", "bl")),
            P(None, "ch", ("grp", "bl")),
            P(None, ("grp", "bl")),
            P(("grp", "bl")),
            P("ch", ("grp", "bl")),
        ),
        out_specs=(P(None, None, "ch", ("grp", "bl")), P(None, None, "ch", ("grp", "bl"))),
        check_vma=False,
    )
```

profile of v0, /device:TPU:0, one launch (start us, length us, event | category | flops | bytes accessed | tf_op | source)
XLA Modules:
  0.0 124.9 jit_solution(16449280972635064767)
XLA Ops:
  7.2 0.8 fusion.35
  8.0 1.0 fusion.33
  9.1 1.0 convert_element_type.25
  10.1 3.4 %gather_fusion = f32[512,2,2,32]{3,2,1,0:T(2,128)S(1)} fusion(f32[2,2,32,512]{2,1,3,0:T(2,128)} %constant.17.clone.2, s32[1024]{0:T(1024)S(1)} %pad_clamp_fusion.1), kind=kCustom, calls=%fused_computation.clone | custom fusion | bytes 526336 | tf_op jit(solution)/shard_map/jit(_take)/gather | solution.py:122
  13.5 1.8 %select_bitcast_fusion.3 = f32[2,2,32,512]{2,1,0,3:T(2,128)S(1)} fusion(f32[512,2,2,32]{3,2,1,0:T(2,128)S(1)} %gather_fusion, pred[512]{0:T(512)(128)(4,1)S(1)} %get-tuple-element.121), kind=kLoop, calls=%fused_computation.10 | loop fusion | flops 65536 | bytes 524800 | tf_op jit(solution)/shard_map/jit(_take)/select_n | solution.py:122
  16.0 3.4 %gather_fusion.1 = f32[512,2,2,32]{3,2,1,0:T(2,128)S(1)} fusion(f32[2,2,32,512]{2,1,3,0:T(2,128)} %constant.17.clone.2, s32[1024]{0:T(1024)S(1)} %pad_clamp_fusion), kind=kCustom, calls=%fused_computation.2.clone | custom fusion | bytes 526336 | tf_op jit(solution)/shard_map/jit(_take)/gather | solution.py:121
  19.4 1.8 %select_bitcast_fusion.2 = f32[2,2,32,512]{2,1,0,3:T(2,128)S(1)} fusion(f32[512,2,2,32]{3,2,1,0:T(2,128)S(1)} %gather_fusion.1, pred[512]{0:T(512)(128)(4,1)S(1)} %get-tuple-element.122), kind=kLoop, calls=%fused_computation.9 | loop fusion | flops 65536 | bytes 524800 | tf_op jit(solution)/shard_map/jit(_take)/select_n | solution.py:121
  23.6 0.7 fusion.1
  24.3 0.7 convolution_add_fusion.1
  25.0 1.1 copy.63
  26.1 1.9 %reshape.247 = f32[512,192]{1,0:T(8,128)} reshape(f32[512,3,2,32]{3,2,1,0:T(2,128)S(1)} %bitcast.94) | data formatting | bytes 786432
  30.6 0.6 multiply_reduce_fusion.6
  31.9 20.9 %reduce-scatter.7.cloned.1.call-done = f32[128,192]{1,0:T(8,128)} async-done(((f32[512,192]{1,0:T(8,128)}), f32[128,192]{1,0:T(8,128)}) %reduce-scatter.7.cloned.1.call-update) | async-done | bytes 98320
  52.8 1.2 reshape.248
  54.3 0.8 fusion.14
  55.2 14.0 %all_gather.3 = f32[2,2,32,512]{3,2,1,0:T(8,128)S(1)} all-gather(f32[2,2,32,128]{3,2,1,0:T(8,128)S(1)} %pad_maximum_fusion.4), channel_id=1, replica_groups=mesh['grp'=2,'bl'=4,'ch'=4] {'bl'}, dimensions={3}, use_global_device_ids=true | all-gather | bytes 327680 | tf_op jit(solution)/shard_map/all_gather | solution.py:96
  69.7 3.1 %gather_fusion.2 = f32[512,2,2,32]{3,2,1,0:T(2,128)} fusion(f32[2,2,32,512]{2,1,3,0:T(2,128)S(1)} %copy.52, s32[1024]{0:T(1024)S(1)} %pad_clamp_fusion.1), kind=kCustom, calls=%fused_computation.1.clone | custom fusion | bytes 526336 | tf_op jit(solution)/shard_map/jit(_take)/gather | solution.py:122
  72.8 3.1 %gather_fusion.3 = f32[512,2,2,32]{3,2,1,0:T(2,128)} fusion(f32[2,2,32,512]{2,1,3,0:T(2,128)S(1)} %copy.52, s32[1024]{0:T(1024)S(1)} %pad_clamp_fusion), kind=kCustom, calls=%fused_computation.3.clone | custom fusion | bytes 526336 | tf_op jit(solution)/shard_map/jit(_take)/gather | solution.py:121
  75.9 3.1 %select_bitcast_fusion.1 = f32[2,2,32,512]{2,1,0,3:T(2,128)S(1)} fusion(f32[512,2,2,32]{3,2,1,0:T(2,128)} %gather_fusion.2, pred[512]{0:T(512)(128)(4,1)S(1)} %copy-done.8), kind=kLoop, calls=%fused_computation.8 | loop fusion | flops 65536 | bytes 524800 | tf_op jit(solution)/shard_map/jit(_take)/select_n | solution.py:122
  79.8 3.1 %select_bitcast_fusion = f32[2,2,32,512]{2,1,0,3:T(2,128)S(1)} fusion(f32[512,2,2,32]{3,2,1,0:T(2,128)} %gather_fusion.3, pred[512]{0:T(512)(128)(4,1)S(1)} %copy-done.6), kind=kLoop, calls=%fused_computation.7 | loop fusion | flops 65536 | bytes 524800 | tf_op jit(solution)/shard_map/jit(_take)/select_n | solution.py:121
  84.9 0.7 fusion
  85.6 0.7 convolution_add_fusion
  86.3 1.1 copy.65
  87.4 1.9 %reshape.249 = f32[512,192]{1,0:T(8,128)} reshape(f32[512,3,2,32]{3,2,1,0:T(2,128)S(1)} %bitcast.95) | data formatting | bytes 786432
  91.2 1.3 %multiply_reduce_fusion.2 = (f32[]{:T(128)}, f32[]{:T(128)}) fusion(f32[128]{0:T(128)S(1)} %get-tuple-element.70, f32[]{:T(128)S(6)} %mul.627, f32[]{:T(128)} %get-tuple-element.69, f32[]{:T(128)S(6)} %mul.619), kind=kLoop, calls=%fused_computation.104 | loop fusion | flops 1662 | bytes 532 | tf_op jit(solution)/shard_map/reduce_sum | solution.py:30
  93.1 1.9 %multiply_reduce_fusion.1 = (f32[]{:T(128)}, f32[128]{0:T(128)S(1)}) fusion(f32[128]{0:T(128)S(1)} %get-tuple-element.70, f32[]{:T(128)} %get-tuple-element.62, f32[]{:T(128)S(6)} %mul.627, f32[]{:T(128)S(6)} %sqrt.11, f32[]{:T(128)} %get-tuple-element.69, f32[]{:T(128)S(6)} %mul.619), kind=kLoop, calls=%fused_computation.102 | loop fusion | flops 1791 | bytes 1048 | tf_op jit(solution)/shard_map/reduce_sum | solution.py:30
  95.0 1.9 %multiply_reduce_fusion = f32[]{:T(128)} fusion(f32[128]{0:T(128)S(1)} %get-tuple-element.68, f32[]{:T(128)} %get-tuple-element.67, f32[128]{0:T(128)S(1)} %get-tuple-element.70, f32[]{:T(128)} %get-tuple-element.62, f32[]{:T(128)S(6)} %mul.627), kind=kLoop, calls=%fused_computation.101 | loop fusion | flops 1535 | bytes 1040 | tf_op jit(solution)/shard_map/reduce_sum | solution.py:31
  97.6 1.9 %fusion.28 = (f32[1,128]{1,0:T(1,128)S(1)}, f32[1,128]{1,0:T(1,128)S(1)}, f32[1,128]{1,0:T(1,128)S(1)}) fusion(f32[]{:T(128)S(6)} %sqrt.12, f32[]{:T(128)} %get-tuple-element.67, f32[]{:T(128)} %get-tuple-element.62, f32[]{:T(128)S(6)} %mul.627, f32[]{:T(128)S(6)} %sqrt.11, f32[]{:T(128)} %get-tuple-element.69, f32[]{:T(128)S(6)} %mul.619, f32[]{:T(128)S(6)} %sqrt.10, ...), kind=kLoop, calls=%fused_computation.116 | loop fusion | flops 2176 | bytes 1572 | tf_op jit(solution)/shard_map/div | solution.py:31
  99.6 9.8 %reduce-scatter.9.cloned.1.call-done = f32[128,192]{1,0:T(8,128)} async-done(((f32[512,192]{1,0:T(8,128)}), f32[128,192]{1,0:T(8,128)}) %reduce-scatter.9.cloned.1.call-update) | async-done | bytes 98320
  109.5 1.2 reshape.250
  111.3 5.7 %psum.7 = f32[4,2,2,128]{3,0,2,1:T(4,128)S(1)} all-reduce(f32[4,2,2,128]{3,0,2,1:T(4,128)S(1)} %fusion.16), channel_id=1, replica_groups=mesh['grp'=2,'bl'=4,'ch'=4] {'ch'}, use_global_device_ids=true, to_apply=%region_23.0 | all-reduce | flops 2048 | bytes 16384 | tf_op jit(solution)/shard_map/psum | solution.py:136
  117.1 1.0 convolution_bitcast_fusion
  (72 shorter events, 9.3 us)
Async XLA Ops:
  7.2 45.6 %reduce-scatter.7.cloned.1.call-start = ((), (), s32[]{:S(2)}) async-start(), calls=%async_computation.2 | async-start | bytes 655360
  8.0 5.5 %copy-start.7 = (pred[512]{0:T(512)(128)(4,1)}, pred[512]{0:T(512)(128)(4,1)S(1)}, u32[]{:S(2)}) copy-start(pred[512]{0:T(512)(128)(4,1)S(1)} %get-tuple-element.121) | copy-start | bytes 1540
  8.0 11.4 %copy-start.5 = (pred[512]{0:T(512)(128)(4,1)}, pred[512]{0:T(512)(128)(4,1)S(1)}, u32[]{:S(2)}) copy-start(pred[512]{0:T(512)(128)(4,1)S(1)} %get-tuple-element.122) | copy-start | bytes 1540
  21.2 1.0 copy-start
  21.6 1.3 %copy-start.4 = (s32[32,512]{1,0:T(8,128)S(1)}, s32[32,512]{1,0:T(8,128)}, u32[]{:S(2)}) copy-start(s32[32,512]{1,0:T(8,128)} %param.13) | copy-start | bytes 196612
  22.9 0.6 copy-start.1
  28.0 81.4 %reduce-scatter.9.cloned.1.call-start = ((), (), s32[]{:S(2)}) async-start(), calls=%async_computation.3 | async-start | bytes 655360
  54.2 21.7 %copy-start.8 = (pred[512]{0:T(512)(128)(4,1)S(1)}, pred[512]{0:T(512)(128)(4,1)}, u32[]{:S(2)}) copy-start(pred[512]{0:T(512)(128)(4,1)} %copy-done.7) | copy-start | bytes 1540
  79.1 0.8 copy-start.6
  83.9 0.8 copy-start.2
  111.1 6.9 %copy-start.3 = (f32[2,2,32,128]{3,2,1,0:T(8,128)}, f32[2,2,32,128]{3,2,1,0:T(8,128)S(1)}, u32[]{:S(2)}) copy-start(f32[2,2,32,128]{3,2,1,0:T(8,128)S(1)} %fusion.6) | copy-start | bytes 196612
Sparse Core Ops, SparseCore 0:
  28.2 24.5 reduce-scatter.6
  89.4 20.0 reduce-scatter.8
where the time goes:
time: 126 us; the launch traced here: 125 us
  waiting for transfers between devices  30.7 us (24%)
  local copies, waits for them, and re-layouts  28.3 us (22%)
  other arithmetic  23.2 us (18%)
  blocking collectives  19.7 us (16%)
  between operations  19.1 us (15%)
  matrix products  3.84 us (3%)
    unnamed x4, waiting for transfers between devices  30.7 us
    all_gather x1, blocking collectives, spread(): return lax.all_gather(owned_gains, 'bl', axis=3, tiled=True)  14 us
    unnamed x30, local copies, waits for them, and re-layouts  9.67 us
    gather x2, local copies, waits for them, and re-layouts, local(): second_gain = jnp.take(gain_state, antenna_pairs[1], axis=3)  6.52 us
    gather x2, local copies, waits for them, and re-layouts, local(): first_gain = jnp.take(gain_state, antenna_pairs[0], axis=3)  6.52 us
    psum x1, blocking collectives, local(): moments = lax.psum(local_moments, 'ch')  5.75 us
    reduce_sum x6, other arithmetic, poly_basis(): vector = vector - jnp.sum(vector * earlier) * earlier  5.66 us
    select_n x2, other arithmetic, local(): first_gain = jnp.take(gain_state, antenna_pairs[0], axis=3)  4.91 us
  transfers between devices with their start and end apart: 2, of which 2 were waited for; matrix products, arithmetic and copies ran while one was open for 8% of the time, Pallas kernels for 0%

commit v1 on v0

--- a/solution.py
+++ b/solution.py
@@ -1,36 +1,38 @@
+import functools
 import math
 
 import jax
 import jax.numpy as jnp
+import numpy as np
 from jax import lax
+from jax.experimental import pallas as pl
+from jax.experimental.pallas import tpu as pltpu
 from jax.sharding import PartitionSpec as P
 
 STATION_COUNT = 512
 SWEEPS = 2
 
-
 damping = 4.0
 highest = lax.Precision.HIGHEST
+
+
+def poly_basis(channel_total):
+    nodes = (2.0 * np.arange(channel_total, dtype=np.float64) - (channel_total - 1)) / (
+        channel_total - 1
+    )
+    rows = []
+    for degree in range(4):
+        vector = nodes**degree
+        for earlier in rows:
+            vector = vector - np.sum(vector * earlier) * earlier
+        rows.append(vector / np.sqrt(np.sum(vector * vector)))
+    return np.stack(rows).astype(np.float32)
 
 
 def split_parts(data):
     planes = data.astype(jnp.float32)
     shape_rest = planes.shape[1:]
     return (planes[:4].reshape((2, 2) + shape_rest), planes[4:].reshape((2, 2) + shape_rest))
-
-
-def poly_basis(channel_total):
-    node_values = (2.0 * jnp.arange(channel_total, dtype=jnp.float32) - (channel_total - 1)) / (
-        channel_total - 1
-    )
-    basis_rows = []
-    for degree in range(4):
-        vector = node_values**degree
-        for earlier in basis_rows:
-            vector = vector - jnp.sum(vector * earlier) * earlier
-        vector = vector / jnp.sqrt(jnp.sum(vector * vector))
-        basis_rows.append(vector)
-    return jnp.stack(basis_rows)
 
 
 def contributions(
@@ -70,45 +72,30 @@
     total_slots = end_first.shape[3]
     flat_first = end_first.reshape(-1, total_slots)
     flat_second = end_second.reshape(-1, total_slots)
-    block_rows = math.gcd(total_slots, 1024)
-    block_count = total_slots // block_rows
     station_index = jnp.arange(STATION_COUNT, dtype=jnp.int32)
-
-    def add_block(block, total):
-        table_first = (first_endpoints[:, None] == station_index[None, :]).astype(jnp.float32)
-        table_second = (second_ends[:, None] == station_index[None, :]).astype(jnp.float32)
-        return (
-            total
-            + jnp.dot(
-                flat_first, table_first, precision=highest, preferred_element_type=jnp.float32
-            )
-            + jnp.dot(
-                flat_second, table_second, precision=highest, preferred_element_type=jnp.float32
-            )
-        )
-
-    empty = jnp.zeros((flat_first.shape[0], STATION_COUNT), jnp.float32)
-    summed = lax.fori_loop(0, block_count, add_block, empty)
+    table_first = (first_endpoints[:, None] == station_index[None, :]).astype(jnp.float32)
+    table_second = (second_ends[:, None] == station_index[None, :]).astype(jnp.float32)
+    summed = jnp.dot(
+        flat_first, table_first, precision=highest, preferred_element_type=jnp.float32
+    ) + jnp.dot(flat_second, table_second, precision=highest, preferred_element_type=jnp.float32)
     return summed.reshape(end_first.shape[:3] + (STATION_COUNT,))
 
 
-def spread(owned_gains):
-    return lax.all_gather(owned_gains, "bl", axis=3, tiled=True)
-
-
-def local(visibilities, sky_model, antenna_pairs, tile_counts, usable_mask):
+def local_general(visibilities, sky_model, antenna_pairs, tile_counts, usable_mask):
     vis_real, vis_imag = split_parts(visibilities)
     model_real_part, model_imaginary = split_parts(sky_model)
     channel_local = visibilities.shape[1]
     tile_rows = visibilities.shape[2]
-    owner_count = lax.axis_size("bl")
-    owned_count = STATION_COUNT // owner_count
+    owned_count = STATION_COUNT // lax.axis_size("bl")
     owner_start = lax.axis_index("bl") * owned_count
     live_slots = jnp.arange(tile_rows, dtype=jnp.int32) < tile_counts[0]
     weights = usable_mask.astype(jnp.float32) * live_slots.astype(jnp.float32)[None, :]
     channel_total = channel_local * lax.axis_size("ch")
     poly_rows = lax.dynamic_slice_in_dim(
-        poly_basis(channel_total), lax.axis_index("ch") * channel_local, channel_local, 1
+        jnp.asarray(poly_basis(channel_total)),
+        lax.axis_index("ch") * channel_local,
+        channel_local,
+        1,
     )
     gain_state = jnp.stack(
         [
@@ -131,11 +118,268 @@
             renewed = 0.5 * (renewed + previous)
         solved = renewed
         if iteration < SWEEPS - 1:
-            gain_state = spread(renewed)
+            gain_state = lax.all_gather(renewed, "bl", axis=3, tiled=True)
     local_moments = jnp.einsum("kc,rfca->krfa", poly_rows, solved, precision=highest)
     moments = lax.psum(local_moments, "ch")
     fitted = jnp.einsum("kc,krfa->rfca", poly_rows, moments, precision=highest)
     return (solved, fitted)
+
+
+def split_dot(values, table, dims):
+    rows = values.shape[0]
+    high = values.astype(jnp.bfloat16)
+    low = (values - high.astype(jnp.float32)).astype(jnp.bfloat16)
+    both = lax.dot_general(
+        jnp.concatenate([high, low], axis=0),
+        table,
+        (dims, ((), ())),
+        preferred_element_type=jnp.float32,
+    )
+    return both[:rows] + both[rows:]
+
+
+def scatter(first, second, table):
+    return split_dot(jnp.concatenate([first, second], axis=1), table, ((1,), (1,)))
+
+
+def tile_terms(chunk_ref, pairs_ref, products_ref, table_ref):
+    slots = chunk_ref.shape[2]
+    station = lax.broadcasted_iota(jnp.int32, (STATION_COUNT, slots), 0)
+    for end in range(2):
+        hit = station == pairs_ref[end : end + 1, :]
+        table_ref[:, end * slots : (end + 1) * slots] = jnp.where(hit, 1.0, 0.0).astype(
+            jnp.bfloat16
+        )
+    real, imag, power = {}, {}, {}
+    for p in range(2):
+        for q in range(2):
+            plane = 2 * p + q
+            vis_real = chunk_ref[plane].astype(jnp.float32)
+            vis_imag = chunk_ref[4 + plane].astype(jnp.float32)
+            model_real = chunk_ref[8 + plane].astype(jnp.float32)
+            model_imag = chunk_ref[12 + plane].astype(jnp.float32)
+            real[p, q] = model_real * vis_real + model_imag * vis_imag
+            imag[p, q] = model_real * vis_imag - model_imag * vis_real
+            power[p, q] = model_real * model_real + model_imag * model_imag
+            products_ref[plane] = real[p, q]
+            products_ref[4 + plane] = imag[p, q]
+            products_ref[8 + plane] = power[p, q]
+    first = [real[p, 0] + real[p, 1] for p in range(2)]
+    first += [imag[p, 0] + imag[p, 1] for p in range(2)]
+    first += [power[p, 0] + power[p, 1] for p in range(2)]
+    second = [real[0, q] + real[1, q] for q in range(2)]
+    second += [-(imag[0, q] + imag[1, q]) for q in range(2)]
+    second += [power[0, q] + power[1, q] for q in range(2)]
+    return scatter(jnp.concatenate(first, 0), jnp.concatenate(second, 0), table_ref[...])
+
+
+def tile_kernel(chunk_ref, pairs_ref, products_ref, table_ref, sums_ref):
+    sums_ref[...] = tile_terms(chunk_ref, pairs_ref, products_ref, table_ref)
+
+
+def gain_terms(gains, products_ref, table_ref):
+    share = products_ref.shape[1]
+    slots = products_ref.shape[2]
+    ends = split_dot(gains, table_ref[...], ((1,), (0,)))
+    gain = lambda part, feed, end: ends[
+        (2 * part + feed) * share : (2 * part + feed + 1) * share,
+        end * slots : (end + 1) * slots,
+    ]
+    size = {
+        (feed, end): gain(0, feed, end) * gain(0, feed, end)
+        + gain(1, feed, end) * gain(1, feed, end)
+        for feed in range(2)
+        for end in range(2)
+    }
+    real = lambda p, q: products_ref[2 * p + q]
+    imag = lambda p, q: products_ref[4 + 2 * p + q]
+    power = lambda p, q: products_ref[8 + 2 * p + q]
+    first = [
+        sum(gain(0, q, 1) * real(p, q) - gain(1, q, 1) * imag(p, q) for q in range(2))
+        for p in range(2)
+    ]
+    first += [
+        sum(gain(0, q, 1) * imag(p, q) + gain(1, q, 1) * real(p, q) for q in range(2))
+        for p in range(2)
+    ]
+    first += [sum(size[q, 1] * power(p, q) for q in range(2)) for p in range(2)]
+    second = [
+        sum(gain(0, p, 0) * real(p, q) + gain(1, p, 0) * imag(p, q) for p in range(2))
+        for q in range(2)
+    ]
+    second += [
+        sum(gain(1, p, 0) * real(p, q) - gain(0, p, 0) * imag(p, q) for p in range(2))
+        for q in range(2)
+    ]
+    second += [sum(size[p, 0] * power(p, q) for p in range(2)) for q in range(2)]
+    return scatter(jnp.concatenate(first, 0), jnp.concatenate(second, 0), table_ref[...])
+
+
+def solve_kernel(tiles, *refs):
+    chunk_ref, pairs_ref = refs[:2]
+    products = refs[2 : 1 + tiles]
+    tables = refs[1 + tiles : 2 * tiles]
+    sums = refs[2 * tiles : 3 * tiles - 1]
+    outs = refs[3 * tiles - 1 : 4 * tiles - 1]
+    own_products, own_table, solved_ref = refs[4 * tiles - 1 :]
+    share = chunk_ref.shape[1]
+    total = tile_terms(chunk_ref, pairs_ref, own_products, own_table)
+    for part in sums:
+        total = total + part[...]
+    rows = 2 * share
+    divisor = total[2 * rows :] + damping
+    gains = jnp.concatenate([(total[:rows] + damping) / divisor, total[rows : 2 * rows] / divisor])
+    total = gain_terms(gains, own_products, own_table)
+    for products_ref, table_ref in zip(products, tables):
+        total = total + gain_terms(gains, products_ref, table_ref)
+    divisor = total[2 * rows :] + damping
+    renewed = (total[: 2 * rows] + damping * gains) / jnp.concatenate([divisor, divisor])
+    solved_ref[...] = 0.5 * (renewed + gains)
+    owned = STATION_COUNT // tiles
+    here = lax.axis_index("bl")
+    for step in range(tiles):
+        start = pl.multiple_of((here ^ step) * owned, owned)
+        outs[step][...] = solved_ref[:, pl.ds(start, owned)]
+
+
+def moment_kernel(basis_ref, *refs):
+    tiles = len(refs) - 2
+    pieces, solved_ref, moments_ref = refs[:tiles], refs[tiles], refs[tiles + 1]
+    share = pieces[0].shape[0] // 4
+    here = lax.axis_index("bl")
+    for step in range(tiles):
+        start = pl.multiple_of((here ^ step) * share, share)
+        for part in range(4):
+            solved_ref[part, pl.ds(start, share), :] = pieces[step][
+                part * share : (part + 1) * share, :
+            ]
+    for degree in range(4):
+        column = basis_ref[:, degree : degree + 1]
+        for part in range(4):
+            moments_ref[4 * degree + part : 4 * degree + part + 1, :] = jnp.sum(
+                solved_ref[part] * column, axis=0, keepdims=True
+            )
+
+
+def fit_kernel(basis_ref, *refs):
+    total = refs[0][...]
+    for part in refs[1:-1]:
+        total = total + part[...]
+    fitted_ref = refs[-1]
+    for part in range(4):
+        fitted_ref[part] = sum(
+            basis_ref[:, degree : degree + 1] * total[4 * degree + part : 4 * degree + part + 1, :]
+            for degree in range(4)
+        )
+
+
+def vmem_call(kernel, outs, scratch=(), **options):
+    def call(*args):
+        return pl.pallas_call(
+            kernel,
+            out_shape=outs,
+            in_specs=[pl.BlockSpec(memory_space=pltpu.VMEM)] * len(args),
+            out_specs=jax.tree.map(lambda _: pl.BlockSpec(memory_space=pltpu.VMEM), outs),
+            scratch_shapes=list(scratch),
+            compiler_params=pltpu.CompilerParams(vmem_limit_bytes=24 << 20),
+            **options,
+        )(*args)
+
+    return call
+
+
+def partners(count, step):
+    return [(index, index ^ step) for index in range(count)]
+
+
+def local_resplit(visibilities, sky_model, antenna_pairs, tile_counts, usable_mask):
+    channel_local = visibilities.shape[1]
+    slots = visibilities.shape[2]
+    tiles = lax.axis_size("bl")
+    groups = lax.axis_size("ch")
+    share = channel_local // tiles
+    owned = STATION_COUNT // tiles
+    here = lax.axis_index("bl")
+    f32 = jnp.float32
+    shape = jax.ShapeDtypeStruct
+
+    live = jnp.arange(slots, dtype=jnp.int32)[None, :] < tile_counts[0]
+    weights = jnp.where(live, usable_mask, 0).astype(jnp.bfloat16)
+
+    def chunk(step):
+        start = (here ^ step) * share
+        cut = lambda data, axis: lax.dynamic_slice_in_dim(data, start, share, axis)
+        return jnp.concatenate([cut(visibilities, 1), cut(sky_model, 1) * cut(weights, 0)[None]])
+
+    steps = list(range(1, tiles))
+    order = sorted(steps, key=lambda step: step == 1)
+    chunks = {0: chunk(0)}
+    pairs = {0: antenna_pairs}
+    for step in order:
+        chunks[step] = lax.ppermute(chunk(step), "bl", partners(tiles, step))
+    for step in order:
+        pairs[step] = lax.ppermute(antenna_pairs, "bl", partners(tiles, step))
+
+    tile_outs = (
+        shape((12, share, slots), f32),
+        shape((STATION_COUNT, 2 * slots), jnp.bfloat16),
+        shape((6 * share, STATION_COUNT), f32),
+    )
+    cost = pl.CostEstimate(
+        flops=24 * share * slots * STATION_COUNT, bytes_accessed=4 << 20, transcendentals=0
+    )
+    done = [vmem_call(tile_kernel, tile_outs, cost_estimate=cost)(chunks[k], pairs[k]) for k in [0] + order[:-1]]
+    last = order[-1]
+    pieces = vmem_call(
+        functools.partial(solve_kernel, tiles),
+        tuple(shape((4 * share, owned), f32) for _ in range(tiles)),
+        scratch=[
+            pltpu.VMEM((12, share, slots), f32),
+            pltpu.VMEM((STATION_COUNT, 2 * slots), jnp.bfloat16),
+            pltpu.VMEM((4 * share, STATION_COUNT), f32),
+        ],
+    )(
+        chunks[last],
+        pairs[last],
+        *[part[0] for part in done],
+        *[part[1] for part in done],
+        *[part[2] for part in done],
+    )
+    received = [pieces[0]] + [
+        lax.ppermute(pieces[step], "bl", partners(tiles, step)) for step in steps
+    ]
+    basis = lax.dynamic_slice_in_dim(
+        jnp.asarray(poly_basis(channel_local * groups).T),
+        lax.axis_index("ch") * channel_local,
+        channel_local,
+        0,
+    )
+    solved, moments = vmem_call(
+        moment_kernel, (shape((4, channel_local, owned), f32), shape((16, owned), f32))
+    )(basis, *received)
+    moment_parts = [moments] + [
+        lax.ppermute(moments, "ch", partners(groups, step)) for step in range(1, groups)
+    ]
+    fitted = vmem_call(fit_kernel, shape((4, channel_local, owned), f32))(basis, *moment_parts)
+    out_shape = (2, 2, channel_local, owned)
+    return solved.reshape(out_shape), fitted.reshape(out_shape)
+
+
+def local(visibilities, sky_model, antenna_pairs, tile_counts, usable_mask):
+    tiles = lax.axis_size("bl")
+    groups = lax.axis_size("ch")
+    power_of_two = lambda count: count & (count - 1) == 0
+    resplit = (
+        power_of_two(tiles)
+        and power_of_two(groups)
+        and 1 < tiles <= 4
+        and groups <= 8
+        and visibilities.shape[1] % (8 * tiles) == 0
+        and STATION_COUNT % (128 * tiles) == 0
+        and visibilities.shape[2] % 128 == 0
+    )
+    body = local_resplit if resplit else local_general
+    return body(visibilities, sky_model, antenna_pairs, tile_counts, usable_mask)
 
 
 def solution(mesh):

time: 126 us -> 42.3 us (0.34)
  local copies, waits for them, and re-layouts: 28.3 us -> 1.08 us
  other arithmetic: 23.2 us -> 2.05 us
  blocking collectives: 19.7 us -> 0 us
  between operations: 19.1 us -> 1.42 us
  starting transfers between devices: 0.08 us -> 17 us
  waiting for transfers between devices: 30.7 us -> 14.5 us
  Pallas kernels: 0 us -> 5.9 us
  matrix products: 3.84 us -> 0 us
    unnamed x4 -> x0, waiting for transfers between devices: 30.7 us -> none
    ppermute x0 -> x12, starting transfers between devices: none -> 17 us  [the longest x3 5.87 us: local_resplit(): chunks[step] = lax.ppermute(chunk(step), 'bl', partners(tiles, step))]
    ppermute x0 -> x12, waiting for transfers between devices: none -> 14.5 us  [the longest x3 7.58 us: local_resplit(): pairs[step] = lax.ppermute(antenna_pairs, 'bl', partners(tiles, step))]
    all_gather x1 -> x0, blocking collectives: 14 us -> none  [spread(): return lax.all_gather(owned_gains, 'bl', axis=3, tiled=True)]
    gather x4 -> x0, local copies, waits for them, and re-layouts: 13 us -> none  [the longest x2 6.52 us: local(): second_gain = jnp.take(gain_state, antenna_pairs[1], axis=3)]
    select_n x5 -> x0, other arithmetic: 9.81 us -> none  [the longest x2 4.91 us: local(): first_gain = jnp.take(gain_state, antenna_pairs[0], axis=3)]
    unnamed x30 -> x2, local copies, waits for them, and re-layouts: 9.67 us -> 0.35 us
    reduce_sum x12 -> x0, other arithmetic: 8.77 us -> none  [the longest x6 5.66 us: poly_basis(): vector = vector - jnp.sum(vector * earlier) * earlier]
  transfers between devices with their start and end apart: 2 -> 12, of which waited for: 2 -> 6; matrix products, arithmetic and copies ran while one was open for 8% -> 2% of each run, Pallas kernels for 0% -> 4%
where the time goes in v1:
time: 42.3 us; the launch traced here: 42 us
  starting transfers between devices  17 us (40%)
  waiting for transfers between devices  14.5 us (34%)
  Pallas kernels  5.9 us (14%)
  other arithmetic  2.05 us (5%)
  between operations  1.42 us (3%)
  local copies, waits for them, and re-layouts  1.08 us (3%)
    ppermute x3, waiting for transfers between devices, local_resplit(): pairs[step] = lax.ppermute(antenna_pairs, 'bl', partners(tiles, step))  7.58 us
    pallas_call x6, Pallas kernels, call(): pl.pallas_call(kernel, out_shape=outs, in_specs=[pl.BlockSpec(memory_spac...  5.9 us
    ppermute x3, starting transfers between devices, local_resplit(): chunks[step] = lax.ppermute(chunk(step), 'bl', partners(tiles, step))  5.87 us
    ppermute x3, waiting for transfers between devices, local_resplit(): lax.ppermute(pieces[step], 'bl', partners(tiles, step))  4.53 us
    ppermute x3, starting transfers between devices, local_resplit(): pairs[step] = lax.ppermute(antenna_pairs, 'bl', partners(tiles, step))  4.51 us
    ppermute x3, starting transfers between devices, local_resplit(): lax.ppermute(pieces[step], 'bl', partners(tiles, step))  4.45 us
    ppermute x3, waiting for transfers between devices, local_resplit(): lax.ppermute(moments, 'ch', partners(groups, step))  2.43 us
    ppermute x3, starting transfers between devices, local_resplit(): lax.ppermute(moments, 'ch', partners(groups, step))  2.14 us
  transfers between devices with their start and end apart: 12, of which 6 were waited for; matrix products, arithmetic and copies ran while one was open for 2% of the time, Pallas kernels for 4%

profile of v1, /device:TPU:0, one launch (start us, length us, event | category | flops | bytes accessed | tf_op | source)
XLA Modules:
  0.0 42.0 jit_solution(6305044714444830207)
XLA Ops:
  1.3 0.9 %select_convert_fusion = bf16[32,512]{1,0:T(8,128)(2,1)S(1)} fusion(s32[32,512]{1,0:T(8,128)} %param.10, pred[512]{0:T(512)(128)(4,1)S(1)} %iota_compare_fusion), kind=kLoop, calls=%fused_computation.7 | loop fusion | flops 32768 | bytes 98816 | tf_op jit(solution)/shard_map/convert_element_type | solution.py:307
  2.2 1.1 %dynamic-slice_multiply_fusion = (bf16[8,8,512]{2,1,0:T(8,128)(2,1)S(1)}, bf16[8,8,512]{2,1,0:T(8,128)(2,1)S(1)}, bf16[8,8,512]{2,1,0:T(8,128)(2,1)S(1)}, bf16[8...) fusion(bf16[8,32,512]{2,1,0:T(8,128)(2,1)} %param.7, ...), kind=kLoop, calls=%fused_computation.4 | loop fusion | flops 524288 | bytes 1081360 | tf_op jit(solution)/shard_map/mul | solution.py:312
  3.4 4.1 %collective-permute-start.2 = (bf16[16,8,512]{2,1,0:T(8,128)(2,1)S(1)}, bf16[16,8,512]{2,1,0:T(8,128)(2,1)S(1)}, u32[]{:S(2)}, u32[]{:S(2)}) collective-permute-start(bf16[16,8,512]{2,1,0:T(8,128)(2,1)S(1)} %pad_maximum_fusion.2), channel_id=1, source_target_pairs={{0,8},{4,12},{8,0},{12,4},{1,9},{5,13},{9,1},{13,5},{2,10},{6,14},... | collective-permute-start | bytes 393224 | tf_op jit(solution)/shard_map/ppermute | solution.py:319
  7.5 1.4 %collective-permute-start.4 = (bf16[16,8,512]{2,1,0:T(8,128)(2,1)S(1)}, bf16[16,8,512]{2,1,0:T(8,128)(2,1)S(1)}, u32[]{:S(2)}, u32[]{:S(2)}) collective-permute-start(bf16[16,8,512]{2,1,0:T(8,128)(2,1)S(1)} %pad_maximum_fusion.3), channel_id=1, source_target_pairs={{0,12},{4,8},{8,4},{12,0},{1,13},{5,9},{9,5},{13,1},{2,14},{6,10},... | collective-permute-start | bytes 393224 | tf_op jit(solution)/shard_map/ppermute | solution.py:319
  8.9 0.3 collective-permute-start
  9.3 0.3 copy-done
  9.6 2.4 %collective-permute-start.3 = (s32[2,512]{1,0:T(2,128)S(1)}, s32[2,512]{1,0:T(2,128)S(1)}, u32[]{:S(2)}, u32[]{:S(2)}) collective-permute-start(s32[2,512]{1,0:T(2,128)S(1)} %copy-done), channel_id=1, source_target_pairs={{0,8},{4,12},{8,0},{12,4},{1,9},{5,13},{9,1},{13,5},{2,10},{6,14},... | collective-permute-start | bytes 12296 | tf_op jit(solution)/shard_map/ppermute | solution.py:321
  12.1 1.3 %collective-permute-start.5 = (s32[2,512]{1,0:T(2,128)S(1)}, s32[2,512]{1,0:T(2,128)S(1)}, u32[]{:S(2)}, u32[]{:S(2)}) collective-permute-start(s32[2,512]{1,0:T(2,128)S(1)} %copy-done), channel_id=1, source_target_pairs={{0,12},{4,8},{8,4},{12,0},{1,13},{5,9},{9,5},{13,1},{2,14},{6,10},... | collective-permute-start | bytes 12296 | tf_op jit(solution)/shard_map/ppermute | solution.py:321
  13.4 0.5 %shard_map.77 = (f32[12,8,512]{2,1,0:T(8,128)S(1)}, bf16[512,1024]{1,0:T(8,128)(2,1)S(1)}, f32[48,512]{1,0:T(8,128)S(1)}) custom-call(bf16[16,8,512]{2,1,0:T(8,128)(2,1)S(1)} %pad_maximum_fusion.1.chunk_ref, s32[2,512]{1,0:T(2,128)S(1)} %copy-done), custom_call_target="tpu_custom_call" | custom-call | flops 50331648 | bytes 4194304 | tf_op jit(solution)/shard_map/pallas_call | solution.py:278
  14.0 5.8 %collective-permute-done.3.pairs_ref = s32[2,512]{1,0:T(2,128)S(1)} collective-permute-done((s32[2,512]{1,0:T(2,128)S(1)}, s32[2,512]{1,0:T(2,128)S(1)}, u32[]{:S(2)}, u32[]{:S(2)}) %collective-permute-start.3) | collective-permute-done | bytes 4128 | tf_op jit(solution)/shard_map/ppermute | solution.py:321
  19.8 0.7 %collective-permute-start.1 = (s32[2,512]{1,0:T(2,128)S(1)}, s32[2,512]{1,0:T(2,128)S(1)}, u32[]{:S(2)}, u32[]{:S(2)}) collective-permute-start(s32[2,512]{1,0:T(2,128)S(1)} %copy-done), channel_id=1, source_target_pairs={{0,4},{4,0},{8,12},{12,8},{1,5},{5,1},{9,13},{13,9},{2,6},{6,2},{1... | collective-permute-start | bytes 12296 | tf_op jit(solution)/shard_map/ppermute | solution.py:321
  20.5 0.5 %shard_map.78 = (f32[12,8,512]{2,1,0:T(8,128)S(1)}, bf16[512,1024]{1,0:T(8,128)(2,1)S(1)}, f32[48,512]{1,0:T(8,128)S(1)}) custom-call(bf16[16,8,512]{2,1,0:T(8,128)(2,1)S(1)} %collective-permute-done.2.chunk_ref, s32[2,512]{1,0:T(2,128)S(1)} %collective-permute-done.3.pairs_ref), custom_call_target="tpu_custom_call" | custom-call | flops 50331648 | bytes 4194304 | tf_op jit(solution)/shard_map/pallas_call | solution.py:278
  21.0 0.0 collective-permute-done.5.pairs_ref
  21.1 0.0 collective-permute-done.4.chunk_ref
  21.1 0.5 %shard_map.79 = (f32[12,8,512]{2,1,0:T(8,128)S(1)}, bf16[512,1024]{1,0:T(8,128)(2,1)S(1)}, f32[48,512]{1,0:T(8,128)S(1)}) custom-call(bf16[16,8,512]{2,1,0:T(8,128)(2,1)S(1)} %collective-permute-done.4.chunk_ref, s32[2,512]{1,0:T(2,128)S(1)} %collective-permute-done.5.pairs_ref), custom_call_target="tpu_custom_call" | custom-call | flops 50331648 | bytes 4194304 | tf_op jit(solution)/shard_map/pallas_call | solution.py:278
  21.6 1.8 %collective-permute-done.1.refs_1_ = s32[2,512]{1,0:T(2,128)S(1)} collective-permute-done((s32[2,512]{1,0:T(2,128)S(1)}, s32[2,512]{1,0:T(2,128)S(1)}, u32[]{:S(2)}, u32[]{:S(2)}) %collective-permute-start.1) | collective-permute-done | bytes 4128 | tf_op jit(solution)/shard_map/ppermute | solution.py:321
  23.4 2.9 %shard_map.80 = (f32[32,128]{1,0:T(8,128)S(1)}, f32[32,128]{1,0:T(8,128)S(1)}, f32[32,128]{1,0:T(8,128)S(1)}, f32[32,128]{1,0:T(8,128)S(1)}) custom-call(bf16[16,8,512]{2,1,0:T(8,128)(2,1)S(1)} %collective-permute-done.refs_0_, s32[2,512]{1,0:T(2,128)S(1)} %collective-permute-done.1.refs_1_, f32[12,8,512]{2,1,0:T(8,128)S(1)} %get-tuple-element.17.refs_2_, ...), custom_call_target="tpu_custom_call" | custom-call | tf_op jit(solution)/shard_map/pallas_call | solution.py:278
  26.3 0.8 %collective-permute-start.6 = (f32[32,128]{1,0:T(8,128)S(1)}, f32[32,128]{1,0:T(8,128)S(1)}, u32[]{:S(2)}, u32[]{:S(2)}) collective-permute-start(f32[32,128]{1,0:T(8,128)S(1)} %get-tuple-element.27), channel_id=1, source_target_pairs={{0,4},{4,0},{8,12},{12,8},{1,5},{5,1},{9,13},{13,9},{2,6},{6,2},{1... | collective-permute-start | bytes 49160 | tf_op jit(solution)/shard_map/ppermute | solution.py:349
  27.0 3.4 %collective-permute-start.7 = (f32[32,128]{1,0:T(8,128)S(1)}, f32[32,128]{1,0:T(8,128)S(1)}, u32[]{:S(2)}, u32[]{:S(2)}) collective-permute-start(f32[32,128]{1,0:T(8,128)S(1)} %get-tuple-element.28), channel_id=1, source_target_pairs={{0,8},{4,12},{8,0},{12,4},{1,9},{5,13},{9,1},{13,5},{2,10},{6,14},... | collective-permute-start | bytes 49160 | tf_op jit(solution)/shard_map/ppermute | solution.py:349
  30.4 0.3 collective-permute-start.8
  30.7 0.7 %constant_dynamic-slice_fusion.8.basis_ref = f32[32,4]{1,0:T(8,128)S(1)} fusion(f32[128,4]{1,0:T(8,128)} %constant.23.clone, s32[]{:T(128)S(6)} %select_n.14), kind=kLoop, calls=%fused_computation.17 | loop fusion | bytes 1028 | tf_op jit(solution)/shard_map/dynamic_slice | solution.py:351
  31.4 0.0 collective-permute-done.6.refs_1_
  31.4 0.7 %collective-permute-done.7.refs_2_ = f32[32,128]{1,0:T(8,128)S(1)} collective-permute-done((f32[32,128]{1,0:T(8,128)S(1)}, f32[32,128]{1,0:T(8,128)S(1)}, u32[]{:S(2)}, u32[]{:S(2)}) %collective-permute-start.7) | collective-permute-done | bytes 16416 | tf_op jit(solution)/shard_map/ppermute | solution.py:349
  32.1 3.8 %collective-permute-done.8.refs_3_ = f32[32,128]{1,0:T(8,128)S(1)} collective-permute-done((f32[32,128]{1,0:T(8,128)S(1)}, f32[32,128]{1,0:T(8,128)S(1)}, u32[]{:S(2)}, u32[]{:S(2)}) %collective-permute-start.8) | collective-permute-done | bytes 16416 | tf_op jit(solution)/shard_map/ppermute | solution.py:349
  36.0 0.6 %shard_map.81 = (f32[4,32,128]{2,1,0:T(8,128)}, f32[16,128]{1,0:T(8,128)S(1)}) custom-call(f32[32,4]{1,0:T(8,128)S(1)} %constant_dynamic-slice_fusion.8.basis_ref, f32[32,128]{1,0:T(8,128)S(1)} %get-tuple-element.26.refs_0_, f32[32,128]{1,0:T(8,128)S(1)} %collective-permute-done.6.refs_1_, f32[32,128]{1,0:T(8,128)S(1)} %collective-permute-done.7.refs_2_, ...), custom_call_target="tpu_custom_call" | custom-call | tf_op jit(solution)/shard_map/pallas_call | solution.py:278
  36.6 1.5 %collective-permute-start.10 = (f32[16,128]{1,0:T(8,128)S(1)}, f32[16,128]{1,0:T(8,128)S(1)}, u32[]{:S(2)}, u32[]{:S(2)}) collective-permute-start(f32[16,128]{1,0:T(8,128)S(1)} %get-tuple-element.31.refs_0_), channel_id=1, source_target_pairs={{0,2},{1,3},{2,0},{3,1},{4,6},{5,7},{6,4},{7,5},{8,10},{9,11},{10,... | collective-permute-start | bytes 24584 | tf_op jit(solution)/shard_map/ppermute | solution.py:361
  38.1 0.0 collective-permute-start.11
  38.1 0.6 %collective-permute-start.9 = (f32[16,128]{1,0:T(8,128)S(1)}, f32[16,128]{1,0:T(8,128)S(1)}, u32[]{:S(2)}, u32[]{:S(2)}) collective-permute-start(f32[16,128]{1,0:T(8,128)S(1)} %get-tuple-element.31.refs_0_), channel_id=1, source_target_pairs={{0,1},{1,0},{2,3},{3,2},{4,5},{5,4},{6,7},{7,6},{8,9},{9,8},{10,11... | collective-permute-start | bytes 24584 | tf_op jit(solution)/shard_map/ppermute | solution.py:361
  38.8 1.5 %collective-permute-done.10.refs_2_ = f32[16,128]{1,0:T(8,128)S(1)} collective-permute-done((f32[16,128]{1,0:T(8,128)S(1)}, f32[16,128]{1,0:T(8,128)S(1)}, u32[]{:S(2)}, u32[]{:S(2)}) %collective-permute-start.10) | collective-permute-done | bytes 8224 | tf_op jit(solution)/shard_map/ppermute | solution.py:361
  40.3 0.9 %collective-permute-done.11.refs_3_ = f32[16,128]{1,0:T(8,128)S(1)} collective-permute-done((f32[16,128]{1,0:T(8,128)S(1)}, f32[16,128]{1,0:T(8,128)S(1)}, u32[]{:S(2)}, u32[]{:S(2)}) %collective-permute-start.11) | collective-permute-done | bytes 8224 | tf_op jit(solution)/shard_map/ppermute | solution.py:361
  41.2 0.0 collective-permute-done.9.refs_1_
  41.2 0.8 %shard_map.82 = f32[4,32,128]{2,1,0:T(8,128)} custom-call(f32[32,4]{1,0:T(8,128)S(1)} %constant_dynamic-slice_fusion.8.basis_ref, f32[16,128]{1,0:T(8,128)S(1)} %get-tuple-element.31.refs_0_, f32[16,128]{1,0:T(8,128)S(1)} %collective-permute-done.9.refs_1_, f32[16,128]{1,0:T(8,128)S(1)} %collective-permute-done.10.refs_2_, ...), custom_call_target="tpu_custom_call" | custom-call | tf_op jit(solution)/shard_map/pallas_call | solution.py:278
  (9 shorter events, 0.1 us)
Async XLA Ops:
  3.4 17.1 %collective-permute-start.2 = (bf16[16,8,512]{2,1,0:T(8,128)(2,1)S(1)}, bf16[16,8,512]{2,1,0:T(8,128)(2,1)S(1)}, u32[]{:S(2)}, u32[]{:S(2)}) collective-permute-start(bf16[16,8,512]{2,1,0:T(8,128)(2,1)S(1)} %pad_maximum_fusion.2), channel_id=1, source_target_pairs={{0,8},{4,12},{8,0},{12,4},{1,9},{5,13},{9,1},{13,5},{2,10},{6,14},... | collective-permute-start | bytes 393224 | tf_op jit(solution)/shard_map/ppermute | solution.py:319
  7.5 13.5 %collective-permute-start.4 = (bf16[16,8,512]{2,1,0:T(8,128)(2,1)S(1)}, bf16[16,8,512]{2,1,0:T(8,128)(2,1)S(1)}, u32[]{:S(2)}, u32[]{:S(2)}) collective-permute-start(bf16[16,8,512]{2,1,0:T(8,128)(2,1)S(1)} %pad_maximum_fusion.3), channel_id=1, source_target_pairs={{0,12},{4,8},{8,4},{12,0},{1,13},{5,9},{9,5},{13,1},{2,14},{6,10},... | collective-permute-start | bytes 393224 | tf_op jit(solution)/shard_map/ppermute | solution.py:319
  8.9 0.7 %copy-start = (s32[2,512]{1,0:T(2,128)S(1)}, s32[2,512]{1,0:T(2,128)}, u32[]{:S(2)}) copy-start(s32[2,512]{1,0:T(2,128)} %pairs_ref.1) | copy-start | bytes 12292
  8.9 14.4 %collective-permute-start = (bf16[16,8,512]{2,1,0:T(8,128)(2,1)S(1)}, bf16[16,8,512]{2,1,0:T(8,128)(2,1)S(1)}, u32[]{:S(2)}, u32[]{:S(2)}) collective-permute-start(bf16[16,8,512]{2,1,0:T(8,128)(2,1)S(1)} %pad_maximum_fusion), channel_id=1, source_target_pairs={{0,4},{4,0},{8,12},{12,8},{1,5},{5,1},{9,13},{13,9},{2,6},{6,2},{1... | collective-permute-start | bytes 393224 | tf_op jit(solution)/shard_map/ppermute | solution.py:319
  9.6 10.2 %collective-permute-start.3 = (s32[2,512]{1,0:T(2,128)S(1)}, s32[2,512]{1,0:T(2,128)S(1)}, u32[]{:S(2)}, u32[]{:S(2)}) collective-permute-start(s32[2,512]{1,0:T(2,128)S(1)} %copy-done), channel_id=1, source_target_pairs={{0,8},{4,12},{8,0},{12,4},{1,9},{5,13},{9,1},{13,5},{2,10},{6,14},... | collective-permute-start | bytes 12296 | tf_op jit(solution)/shard_map/ppermute | solution.py:321
  12.1 9.0 %collective-permute-start.5 = (s32[2,512]{1,0:T(2,128)S(1)}, s32[2,512]{1,0:T(2,128)S(1)}, u32[]{:S(2)}, u32[]{:S(2)}) collective-permute-start(s32[2,512]{1,0:T(2,128)S(1)} %copy-done), channel_id=1, source_target_pairs={{0,12},{4,8},{8,4},{12,0},{1,13},{5,9},{9,5},{13,1},{2,14},{6,10},... | collective-permute-start | bytes 12296 | tf_op jit(solution)/shard_map/ppermute | solution.py:321
  19.8 3.6 %collective-permute-start.1 = (s32[2,512]{1,0:T(2,128)S(1)}, s32[2,512]{1,0:T(2,128)S(1)}, u32[]{:S(2)}, u32[]{:S(2)}) collective-permute-start(s32[2,512]{1,0:T(2,128)S(1)} %copy-done), channel_id=1, source_target_pairs={{0,4},{4,0},{8,12},{12,8},{1,5},{5,1},{9,13},{13,9},{2,6},{6,2},{1... | collective-permute-start | bytes 12296 | tf_op jit(solution)/shard_map/ppermute | solution.py:321
  26.3 5.2 %collective-permute-start.6 = (f32[32,128]{1,0:T(8,128)S(1)}, f32[32,128]{1,0:T(8,128)S(1)}, u32[]{:S(2)}, u32[]{:S(2)}) collective-permute-start(f32[32,128]{1,0:T(8,128)S(1)} %get-tuple-element.27), channel_id=1, source_target_pairs={{0,4},{4,0},{8,12},{12,8},{1,5},{5,1},{9,13},{13,9},{2,6},{6,2},{1... | collective-permute-start | bytes 49160 | tf_op jit(solution)/shard_map/ppermute | solution.py:349
  27.0 5.1 %collective-permute-start.7 = (f32[32,128]{1,0:T(8,128)S(1)}, f32[32,128]{1,0:T(8,128)S(1)}, u32[]{:S(2)}, u32[]{:S(2)}) collective-permute-start(f32[32,128]{1,0:T(8,128)S(1)} %get-tuple-element.28), channel_id=1, source_target_pairs={{0,8},{4,12},{8,0},{12,4},{1,9},{5,13},{9,1},{13,5},{2,10},{6,14},... | collective-permute-start | bytes 49160 | tf_op jit(solution)/shard_map/ppermute | solution.py:349
  30.4 5.5 %collective-permute-start.8 = (f32[32,128]{1,0:T(8,128)S(1)}, f32[32,128]{1,0:T(8,128)S(1)}, u32[]{:S(2)}, u32[]{:S(2)}) collective-permute-start(f32[32,128]{1,0:T(8,128)S(1)} %get-tuple-element.29), channel_id=1, source_target_pairs={{0,12},{4,8},{8,4},{12,0},{1,13},{5,9},{9,5},{13,1},{2,14},{6,10},... | collective-permute-start | bytes 49160 | tf_op jit(solution)/shard_map/ppermute | solution.py:349
  36.6 3.7 %collective-permute-start.10 = (f32[16,128]{1,0:T(8,128)S(1)}, f32[16,128]{1,0:T(8,128)S(1)}, u32[]{:S(2)}, u32[]{:S(2)}) collective-permute-start(f32[16,128]{1,0:T(8,128)S(1)} %get-tuple-element.31.refs_0_), channel_id=1, source_target_pairs={{0,2},{1,3},{2,0},{3,1},{4,6},{5,7},{6,4},{7,5},{8,10},{9,11},{10,... | collective-permute-start | bytes 24584 | tf_op jit(solution)/shard_map/ppermute | solution.py:361
  38.1 3.1 %collective-permute-start.11 = (f32[16,128]{1,0:T(8,128)S(1)}, f32[16,128]{1,0:T(8,128)S(1)}, u32[]{:S(2)}, u32[]{:S(2)}) collective-permute-start(f32[16,128]{1,0:T(8,128)S(1)} %get-tuple-element.31.refs_0_), channel_id=1, source_target_pairs={{0,3},{1,2},{2,1},{3,0},{4,7},{5,6},{6,5},{7,4},{8,11},{9,10},{10,... | collective-permute-start | bytes 24584 | tf_op jit(solution)/shard_map/ppermute | solution.py:361
  38.1 3.1 %collective-permute-start.9 = (f32[16,128]{1,0:T(8,128)S(1)}, f32[16,128]{1,0:T(8,128)S(1)}, u32[]{:S(2)}, u32[]{:S(2)}) collective-permute-start(f32[16,128]{1,0:T(8,128)S(1)} %get-tuple-element.31.refs_0_), channel_id=1, source_target_pairs={{0,1},{1,0},{2,3},{3,2},{4,5},{5,4},{6,7},{7,6},{8,9},{9,8},{10,11... | collective-permute-start | bytes 24584 | tf_op jit(solution)/shard_map/ppermute | solution.py:361

commit v2 on v1

--- a/solution.py
+++ b/solution.py
@@ -125,6 +125,53 @@
     return (solved, fitted)
 
 
+LANES = 128
+INDEX_SHIFT = 256.0
+
+
+def pack_kernel(order, counts_ref, vis_hbm, sky_hbm, pairs_hbm, mask_hbm, *refs):
+    tiles = len(order)
+    outs = refs[:tiles]
+    vis, sky, mask, pairs, rows, sems = refs[tiles:]
+    slots = pairs.shape[1]
+    blocks = slots // LANES
+    share = outs[0].shape[1]
+    here = lax.axis_index("bl")
+    ends_copy = pltpu.make_async_copy(pairs_hbm, pairs, sems.at[0])
+    copies = []
+    for slot, step in enumerate(order):
+        channels = pl.ds(pl.multiple_of((here ^ step) * share, share), share)
+        copies.append(
+            [
+                pltpu.make_async_copy(mask_hbm.at[channels], mask.at[slot], sems.at[1 + 3 * slot]),
+                pltpu.make_async_copy(sky_hbm.at[:, channels], sky.at[slot], sems.at[2 + 3 * slot]),
+                pltpu.make_async_copy(vis_hbm.at[:, channels], vis.at[slot], sems.at[3 + 3 * slot]),
+            ]
+        )
+    ends_copy.start()
+    for group in copies:
+        for copy in group:
+            copy.start()
+    ends_copy.wait()
+    for end in range(2):
+        for block in range(blocks):
+            row = end * blocks + block
+            rows[row : row + 1, :] = pairs[end : end + 1, block * LANES : (block + 1) * LANES]
+    ends = (rows[...].astype(jnp.float32) - INDEX_SHIFT).astype(jnp.bfloat16)
+    live = lax.broadcasted_iota(jnp.int32, (share, slots), 1) < counts_ref[0]
+    for slot in range(tiles):
+        out = outs[slot]
+        for copy in copies[slot]:
+            copy.wait()
+        weights = jnp.where(live, mask[slot], 0).astype(jnp.float32).astype(jnp.bfloat16)
+        for block in range(blocks):
+            lanes = slice(block * LANES, (block + 1) * LANES)
+            for plane in range(8):
+                out[16 * block + plane] = vis[slot, plane, :, lanes]
+                out[16 * block + 8 + plane] = sky[slot, plane, :, lanes] * weights[:, lanes]
+        out[16 * blocks] = ends
+
+
 def split_dot(values, table, dims):
     rows = values.shape[0]
     high = values.astype(jnp.bfloat16)
@@ -142,22 +189,28 @@
     return split_dot(jnp.concatenate([first, second], axis=1), table, ((1,), (1,)))
 
 
-def tile_terms(chunk_ref, pairs_ref, products_ref, table_ref):
-    slots = chunk_ref.shape[2]
-    station = lax.broadcasted_iota(jnp.int32, (STATION_COUNT, slots), 0)
-    for end in range(2):
-        hit = station == pairs_ref[end : end + 1, :]
-        table_ref[:, end * slots : (end + 1) * slots] = jnp.where(hit, 1.0, 0.0).astype(
+def tile_terms(chunk_ref, products_ref, table_ref):
+    slots = products_ref.shape[2]
+    blocks = slots // LANES
+    ends = chunk_ref[chunk_ref.shape[0] - 1].astype(jnp.float32)
+    station = lax.broadcasted_iota(jnp.int32, (STATION_COUNT, LANES), 0).astype(jnp.float32)
+    station = station - INDEX_SHIFT
+    for block in range(2 * blocks):
+        hit = station == ends[block : block + 1, :]
+        table_ref[:, block * LANES : (block + 1) * LANES] = jnp.where(hit, 1.0, 0.0).astype(
             jnp.bfloat16
         )
+    plane_of = lambda plane: jnp.concatenate(
+        [chunk_ref[16 * block + plane].astype(jnp.float32) for block in range(blocks)], axis=1
+    )
     real, imag, power = {}, {}, {}
     for p in range(2):
         for q in range(2):
             plane = 2 * p + q
-            vis_real = chunk_ref[plane].astype(jnp.float32)
-            vis_imag = chunk_ref[4 + plane].astype(jnp.float32)
-            model_real = chunk_ref[8 + plane].astype(jnp.float32)
-            model_imag = chunk_ref[12 + plane].astype(jnp.float32)
+            vis_real = plane_of(plane)
+            vis_imag = plane_of(4 + plane)
+            model_real = plane_of(8 + plane)
+            model_imag = plane_of(12 + plane)
             real[p, q] = model_real * vis_real + model_imag * vis_imag
             imag[p, q] = model_real * vis_imag - model_imag * vis_real
             power[p, q] = model_real * model_real + model_imag * model_imag
@@ -173,8 +226,8 @@
     return scatter(jnp.concatenate(first, 0), jnp.concatenate(second, 0), table_ref[...])
 
 
-def tile_kernel(chunk_ref, pairs_ref, products_ref, table_ref, sums_ref):
-    sums_ref[...] = tile_terms(chunk_ref, pairs_ref, products_ref, table_ref)
+def tile_kernel(chunk_ref, products_ref, table_ref, sums_ref):
+    sums_ref[...] = tile_terms(chunk_ref, products_ref, table_ref)
 
 
 def gain_terms(gains, products_ref, table_ref):
@@ -216,14 +269,14 @@
 
 
 def solve_kernel(tiles, *refs):
-    chunk_ref, pairs_ref = refs[:2]
-    products = refs[2 : 1 + tiles]
-    tables = refs[1 + tiles : 2 * tiles]
-    sums = refs[2 * tiles : 3 * tiles - 1]
-    outs = refs[3 * tiles - 1 : 4 * tiles - 1]
-    own_products, own_table, solved_ref = refs[4 * tiles - 1 :]
+    chunk_ref = refs[0]
+    products = refs[1:tiles]
+    tables = refs[tiles : 2 * tiles - 1]
+    sums = refs[2 * tiles - 1 : 3 * tiles - 2]
+    outs = refs[3 * tiles - 2 : 4 * tiles - 2]
+    own_products, own_table, solved_ref = refs[4 * tiles - 2 :]
     share = chunk_ref.shape[1]
-    total = tile_terms(chunk_ref, pairs_ref, own_products, own_table)
+    total = tile_terms(chunk_ref, own_products, own_table)
     for part in sums:
         total = total + part[...]
     rows = 2 * share
@@ -273,12 +326,14 @@
         )
 
 
-def vmem_call(kernel, outs, scratch=(), **options):
+def vmem_call(kernel, outs, scratch=(), spaces=None, **options):
     def call(*args):
         return pl.pallas_call(
             kernel,
             out_shape=outs,
-            in_specs=[pl.BlockSpec(memory_space=pltpu.VMEM)] * len(args),
+            in_specs=[
+                pl.BlockSpec(memory_space=space) for space in spaces or [pltpu.VMEM] * len(args)
+            ],
             out_specs=jax.tree.map(lambda _: pl.BlockSpec(memory_space=pltpu.VMEM), outs),
             scratch_shapes=list(scratch),
             compiler_params=pltpu.CompilerParams(vmem_limit_bytes=24 << 20),
@@ -286,6 +341,10 @@
         )(*args)
 
     return call
+
+
+def in_hbm(value):
+    return pltpu.with_memory_space_constraint(value, pltpu.HBM)
 
 
 def partners(count, step):
@@ -299,26 +358,29 @@
     groups = lax.axis_size("ch")
     share = channel_local // tiles
     owned = STATION_COUNT // tiles
-    here = lax.axis_index("bl")
     f32 = jnp.float32
     shape = jax.ShapeDtypeStruct
 
-    live = jnp.arange(slots, dtype=jnp.int32)[None, :] < tile_counts[0]
-    weights = jnp.where(live, usable_mask, 0).astype(jnp.bfloat16)
-
-    def chunk(step):
-        start = (here ^ step) * share
-        cut = lambda data, axis: lax.dynamic_slice_in_dim(data, start, share, axis)
-        return jnp.concatenate([cut(visibilities, 1), cut(sky_model, 1) * cut(weights, 0)[None]])
-
     steps = list(range(1, tiles))
     order = sorted(steps, key=lambda step: step == 1)
-    chunks = {0: chunk(0)}
-    pairs = {0: antenna_pairs}
-    for step in order:
-        chunks[step] = lax.ppermute(chunk(step), "bl", partners(tiles, step))
-    for step in order:
-        pairs[step] = lax.ppermute(antenna_pairs, "bl", partners(tiles, step))
+    blocks = slots // LANES
+    chunk_shape = shape((16 * blocks + 1, share, LANES), jnp.bfloat16)
+    packed = vmem_call(
+        functools.partial(pack_kernel, order + [0]),
+        (chunk_shape,) * tiles,
+        scratch=[
+            pltpu.VMEM((tiles, 8, share, slots), jnp.bfloat16),
+            pltpu.VMEM((tiles, 8, share, slots), jnp.bfloat16),
+            pltpu.VMEM((tiles, share, slots), jnp.int32),
+            pltpu.VMEM((2, slots), jnp.int32),
+            pltpu.VMEM((2 * blocks, LANES), jnp.int32),
+            pltpu.SemaphoreType.DMA((1 + 3 * tiles,)),
+        ],
+        spaces=[pltpu.SMEM] + [pltpu.HBM] * 4,
+    )(tile_counts, *[in_hbm(x) for x in (visibilities, sky_model, antenna_pairs, usable_mask)])
+    chunks = {0: packed[-1]}
+    for step, piece in zip(order, packed):
+        chunks[step] = lax.ppermute(piece, "bl", partners(tiles, step))
 
     tile_outs = (
         shape((12, share, slots), f32),
@@ -328,7 +390,7 @@
     cost = pl.CostEstimate(
         flops=24 * share * slots * STATION_COUNT, bytes_accessed=4 << 20, transcendentals=0
     )
-    done = [vmem_call(tile_kernel, tile_outs, cost_estimate=cost)(chunks[k], pairs[k]) for k in [0] + order[:-1]]
+    done = [vmem_call(tile_kernel, tile_outs, cost_estimate=cost)(chunks[k]) for k in [0] + order[:-1]]
     last = order[-1]
     pieces = vmem_call(
         functools.partial(solve_kernel, tiles),
@@ -340,7 +402,6 @@
         ],
     )(
         chunks[last],
-        pairs[last],
         *[part[0] for part in done],
         *[part[1] for part in done],
         *[part[2] for part in done],
@@ -374,9 +435,10 @@
         and power_of_two(groups)
         and 1 < tiles <= 4
         and groups <= 8
-        and visibilities.shape[1] % (8 * tiles) == 0
+        and visibilities.shape[1] == 8 * tiles
         and STATION_COUNT % (128 * tiles) == 0
-        and visibilities.shape[2] % 128 == 0
+        and STATION_COUNT <= 2 * INDEX_SHIFT
+        and visibilities.shape[2] == 4 * LANES
     )
     body = local_resplit if resplit else local_general
     return body(visibilities, sky_model, antenna_pairs, tile_counts, usable_mask)

time: 42.3 us -> 37.2 us (0.88)
  starting transfers between devices: 17 us -> 13.1 us
  other arithmetic: 2.05 us -> 0 us
  Pallas kernels: 5.9 us -> 7.81 us
  waiting for transfers between devices: 14.5 us -> 14 us
    ppermute x6 -> x3, starting transfers between devices: 10.4 us -> 5.71 us  [local_resplit(): chunks[step] = lax.ppermute(piece, 'bl', partners(tiles, step))]
    pallas_call x6 -> x7, Pallas kernels: 5.9 us -> 7.81 us  [call(): pl.pallas_call(kernel, out_shape=outs, in_specs=[pl.BlockSpec(memory_spac...]
    mul x1 -> x0, other arithmetic: 1.14 us -> none  [chunk(): cut(sky_model, 1) * cut(weights, 0)[None]]
    ppermute x3, waiting for transfers between devices: 4.53 us -> 3.43 us  [local_resplit(): lax.ppermute(pieces[step], 'bl', partners(tiles, step))]
    ppermute x3, starting transfers between devices: 4.45 us -> 5.49 us  [local_resplit(): lax.ppermute(pieces[step], 'bl', partners(tiles, step))]
    convert_element_type x1 -> x0, other arithmetic: 0.85 us -> none  [local_resplit(): weights = jnp.where(live, usable_mask, 0).astype(jnp.bfloat16)]
    ppermute x6 -> x3, waiting for transfers between devices: 7.59 us -> 7.89 us  [local_resplit(): chunks[step] = lax.ppermute(piece, 'bl', partners(tiles, step))]
  transfers between devices with their start and end apart: 12 -> 9, of which waited for: 6 -> 5; matrix products, arithmetic and copies ran while one was open for 2% -> 2% of each run, Pallas kernels for 4% -> 5%
where the time goes in v2:
time: 37.2 us; the launch traced here: 37 us
  waiting for transfers between devices  14 us (38%)
  starting transfers between devices  13.1 us (35%)
  Pallas kernels  7.81 us (21%)
  between operations  1.34 us (4%)
  local copies, waits for them, and re-layouts  0.72 us (2%)
    ppermute x3, waiting for transfers between devices, local_resplit(): chunks[step] = lax.ppermute(piece, 'bl', partners(tiles, step))  7.89 us
    pallas_call x7, Pallas kernels, call(): pl.pallas_call(kernel, out_shape=outs, in_specs=[pl.BlockSpec(memory_spac...  7.81 us
    ppermute x3, starting transfers between devices, local_resplit(): chunks[step] = lax.ppermute(piece, 'bl', partners(tiles, step))  5.71 us
    ppermute x3, starting transfers between devices, local_resplit(): lax.ppermute(pieces[step], 'bl', partners(tiles, step))  5.49 us
    ppermute x3, waiting for transfers between devices, local_resplit(): lax.ppermute(pieces[step], 'bl', partners(tiles, step))  3.43 us
    ppermute x3, waiting for transfers between devices, local_resplit(): lax.ppermute(moments, 'ch', partners(groups, step))  2.7 us
    ppermute x3, starting transfers between devices, local_resplit(): lax.ppermute(moments, 'ch', partners(groups, step))  1.86 us
  transfers between devices with their start and end apart: 9, of which 5 were waited for; matrix products, arithmetic and copies ran while one was open for 2% of the time, Pallas kernels for 5%

profile of v2, /device:TPU:0, one launch (start us, length us, event | category | flops | bytes accessed | tf_op | source)
XLA Modules:
  0.0 37.0 jit_solution(6431229625478217444)
XLA Ops:
  1.3 1.3 %shard_map.77 = (bf16[65,8,128]{2,1,0:T(8,128)(2,1)S(1)}, bf16[65,8,128]{2,1,0:T(8,128)(2,1)S(1)}, bf16[65,8,128]{2,1,0:T(8,128)(2,1)S(1)}, bf16[65,8,128]{2,1,0:T(8,128)(2,1)S(1)}) custom-call(s32[1]{0:T(128)S(6)} %copy.8.counts_ref, bf16[8,32,512]{2,1,0:T(8,128)(2,1)} %vis_hbm.1, bf16[8,32,512]{2,1,0:T(8,128)(2,1)} %sky_hbm.1, s32[2,512]{1,0:T(2,128)} %pairs_hbm.1, ...), custom_call_target="tpu_custom_call" | custom-call | tf_op jit(solution)/shard_map/pallas_call | solution.py:331
  2.6 4.1 %collective-permute-start.1 = (bf16[65,8,128]{2,1,0:T(8,128)(2,1)S(1)}, bf16[65,8,128]{2,1,0:T(8,128)(2,1)S(1)}, u32[]{:S(2)}, u32[]{:S(2)}) collective-permute-start(bf16[65,8,128]{2,1,0:T(8,128)(2,1)S(1)} %get-tuple-element.24), channel_id=1, source_target_pairs={{0,8},{4,12},{8,0},{12,4},{1,9},{5,13},{9,1},{13,5},{2,10},{6,14},... | collective-permute-start | bytes 399368 | tf_op jit(solution)/shard_map/ppermute | solution.py:383
  6.7 1.3 %collective-permute-start.2 = (bf16[65,8,128]{2,1,0:T(8,128)(2,1)S(1)}, bf16[65,8,128]{2,1,0:T(8,128)(2,1)S(1)}, u32[]{:S(2)}, u32[]{:S(2)}) collective-permute-start(bf16[65,8,128]{2,1,0:T(8,128)(2,1)S(1)} %get-tuple-element.26), channel_id=1, source_target_pairs={{0,12},{4,8},{8,4},{12,0},{1,13},{5,9},{9,5},{13,1},{2,14},{6,10},... | collective-permute-start | bytes 399368 | tf_op jit(solution)/shard_map/ppermute | solution.py:383
  8.0 0.2 collective-permute-start
  8.3 0.7 %shard_map.78 = (f32[12,8,512]{2,1,0:T(8,128)S(1)}, bf16[512,1024]{1,0:T(8,128)(2,1)S(1)}, f32[48,512]{1,0:T(8,128)S(1)}) custom-call(bf16[65,8,128]{2,1,0:T(8,128)(2,1)S(1)} %get-tuple-element.22.chunk_ref), custom_call_target="tpu_custom_call" | custom-call | flops 50331648 | bytes 4194304 | tf_op jit(solution)/shard_map/pallas_call | solution.py:331
  8.9 7.9 %collective-permute-done.1.chunk_ref = bf16[65,8,128]{2,1,0:T(8,128)(2,1)S(1)} collective-permute-done((bf16[65,8,128]{2,1,0:T(8,128)(2,1)S(1)}, bf16[65,8,128]{2,1,0:T(8,128)(2,1)S(1)}, u32[]{:S(2)}, u32[]{:S(2)}) %collective-permute-start.1) | collective-permute-done | bytes 133152 | tf_op jit(solution)/shard_map/ppermute | solution.py:383
  16.8 0.7 %shard_map.79 = (f32[12,8,512]{2,1,0:T(8,128)S(1)}, bf16[512,1024]{1,0:T(8,128)(2,1)S(1)}, f32[48,512]{1,0:T(8,128)S(1)}) custom-call(bf16[65,8,128]{2,1,0:T(8,128)(2,1)S(1)} %collective-permute-done.1.chunk_ref), custom_call_target="tpu_custom_call" | custom-call | flops 50331648 | bytes 4194304 | tf_op jit(solution)/shard_map/pallas_call | solution.py:331
  17.5 0.0 collective-permute-done.2.chunk_ref
  17.5 0.7 %shard_map.80 = (f32[12,8,512]{2,1,0:T(8,128)S(1)}, bf16[512,1024]{1,0:T(8,128)(2,1)S(1)}, f32[48,512]{1,0:T(8,128)S(1)}) custom-call(bf16[65,8,128]{2,1,0:T(8,128)(2,1)S(1)} %collective-permute-done.2.chunk_ref), custom_call_target="tpu_custom_call" | custom-call | flops 50331648 | bytes 4194304 | tf_op jit(solution)/shard_map/pallas_call | solution.py:331
  18.2 0.0 collective-permute-done.refs_0_
  18.2 3.1 %shard_map.81 = (f32[32,128]{1,0:T(8,128)S(1)}, f32[32,128]{1,0:T(8,128)S(1)}, f32[32,128]{1,0:T(8,128)S(1)}, f32[32,128]{1,0:T(8,128)S(1)}) custom-call(bf16[65,8,128]{2,1,0:T(8,128)(2,1)S(1)} %collective-permute-done.refs_0_, f32[12,8,512]{2,1,0:T(8,128)S(1)} %get-tuple-element.23.refs_1_, f32[12,8,512]{2,1,0:T(8,128)S(1)} %get-tuple-element.25.refs_2_, ...), custom_call_target="tpu_custom_call" | custom-call | tf_op jit(solution)/shard_map/pallas_call | solution.py:331
  21.3 2.1 %collective-permute-start.3 = (f32[32,128]{1,0:T(8,128)S(1)}, f32[32,128]{1,0:T(8,128)S(1)}, u32[]{:S(2)}, u32[]{:S(2)}) collective-permute-start(f32[32,128]{1,0:T(8,128)S(1)} %get-tuple-element.35), channel_id=1, source_target_pairs={{0,4},{4,0},{8,12},{12,8},{1,5},{5,1},{9,13},{13,9},{2,6},{6,2},{1... | collective-permute-start | bytes 49160 | tf_op jit(solution)/shard_map/ppermute | solution.py:410
  23.4 2.0 %collective-permute-start.4 = (f32[32,128]{1,0:T(8,128)S(1)}, f32[32,128]{1,0:T(8,128)S(1)}, u32[]{:S(2)}, u32[]{:S(2)}) collective-permute-start(f32[32,128]{1,0:T(8,128)S(1)} %get-tuple-element.36), channel_id=1, source_target_pairs={{0,8},{4,12},{8,0},{12,4},{1,9},{5,13},{9,1},{13,5},{2,10},{6,14},... | collective-permute-start | bytes 49160 | tf_op jit(solution)/shard_map/ppermute | solution.py:410
  25.4 1.4 %collective-permute-start.5 = (f32[32,128]{1,0:T(8,128)S(1)}, f32[32,128]{1,0:T(8,128)S(1)}, u32[]{:S(2)}, u32[]{:S(2)}) collective-permute-start(f32[32,128]{1,0:T(8,128)S(1)} %get-tuple-element.37), channel_id=1, source_target_pairs={{0,12},{4,8},{8,4},{12,0},{1,13},{5,9},{9,5},{13,1},{2,14},{6,10},... | collective-permute-start | bytes 49160 | tf_op jit(solution)/shard_map/ppermute | solution.py:410
  26.8 0.7 %constant_dynamic-slice_fusion.basis_ref = f32[32,4]{1,0:T(8,128)S(1)} fusion(f32[128,4]{1,0:T(8,128)} %constant.12.clone, s32[]{:T(128)S(6)} %select_n.3), kind=kLoop, calls=%fused_computation | loop fusion | bytes 1028 | tf_op jit(solution)/shard_map/dynamic_slice | solution.py:412
  27.5 0.0 collective-permute-done.3.refs_1_
  27.5 0.5 %collective-permute-done.4.refs_2_ = f32[32,128]{1,0:T(8,128)S(1)} collective-permute-done((f32[32,128]{1,0:T(8,128)S(1)}, f32[32,128]{1,0:T(8,128)S(1)}, u32[]{:S(2)}, u32[]{:S(2)}) %collective-permute-start.4) | collective-permute-done | bytes 16416 | tf_op jit(solution)/shard_map/ppermute | solution.py:410
  28.0 2.9 %collective-permute-done.5.refs_3_ = f32[32,128]{1,0:T(8,128)S(1)} collective-permute-done((f32[32,128]{1,0:T(8,128)S(1)}, f32[32,128]{1,0:T(8,128)S(1)}, u32[]{:S(2)}, u32[]{:S(2)}) %collective-permute-start.5) | collective-permute-done | bytes 16416 | tf_op jit(solution)/shard_map/ppermute | solution.py:410
  30.9 0.6 %shard_map.82 = (f32[4,32,128]{2,1,0:T(8,128)}, f32[16,128]{1,0:T(8,128)S(1)}) custom-call(f32[32,4]{1,0:T(8,128)S(1)} %constant_dynamic-slice_fusion.basis_ref, f32[32,128]{1,0:T(8,128)S(1)} %get-tuple-element.34.refs_0_, f32[32,128]{1,0:T(8,128)S(1)} %collective-permute-done.3.refs_1_, f32[32,128]{1,0:T(8,128)S(1)} %collective-permute-done.4.refs_2_, ...), custom_call_target="tpu_custom_call" | custom-call | tf_op jit(solution)/shard_map/pallas_call | solution.py:331
  31.6 0.0 collective-permute-start.6
  31.6 1.5 %collective-permute-start.7 = (f32[16,128]{1,0:T(8,128)S(1)}, f32[16,128]{1,0:T(8,128)S(1)}, u32[]{:S(2)}, u32[]{:S(2)}) collective-permute-start(f32[16,128]{1,0:T(8,128)S(1)} %get-tuple-element.39.refs_0_), channel_id=1, source_target_pairs={{0,2},{1,3},{2,0},{3,1},{4,6},{5,7},{6,4},{7,5},{8,10},{9,11},{10,... | collective-permute-start | bytes 24584 | tf_op jit(solution)/shard_map/ppermute | solution.py:422
  33.1 0.4 %collective-permute-start.8 = (f32[16,128]{1,0:T(8,128)S(1)}, f32[16,128]{1,0:T(8,128)S(1)}, u32[]{:S(2)}, u32[]{:S(2)}) collective-permute-start(f32[16,128]{1,0:T(8,128)S(1)} %get-tuple-element.39.refs_0_), channel_id=1, source_target_pairs={{0,3},{1,2},{2,1},{3,0},{4,7},{5,6},{6,5},{7,4},{8,11},{9,10},{10,... | collective-permute-start | bytes 24584 | tf_op jit(solution)/shard_map/ppermute | solution.py:422
  33.5 0.0 collective-permute-done.6.refs_1_
  33.5 1.8 %collective-permute-done.7.refs_2_ = f32[16,128]{1,0:T(8,128)S(1)} collective-permute-done((f32[16,128]{1,0:T(8,128)S(1)}, f32[16,128]{1,0:T(8,128)S(1)}, u32[]{:S(2)}, u32[]{:S(2)}) %collective-permute-start.7) | collective-permute-done | bytes 8224 | tf_op jit(solution)/shard_map/ppermute | solution.py:422
  35.2 0.9 %collective-permute-done.8.refs_3_ = f32[16,128]{1,0:T(8,128)S(1)} collective-permute-done((f32[16,128]{1,0:T(8,128)S(1)}, f32[16,128]{1,0:T(8,128)S(1)}, u32[]{:S(2)}, u32[]{:S(2)}) %collective-permute-start.8) | collective-permute-done | bytes 8224 | tf_op jit(solution)/shard_map/ppermute | solution.py:422
  36.2 0.8 %shard_map.83 = f32[4,32,128]{2,1,0:T(8,128)} custom-call(f32[32,4]{1,0:T(8,128)S(1)} %constant_dynamic-slice_fusion.basis_ref, f32[16,128]{1,0:T(8,128)S(1)} %get-tuple-element.39.refs_0_, f32[16,128]{1,0:T(8,128)S(1)} %collective-permute-done.6.refs_1_, f32[16,128]{1,0:T(8,128)S(1)} %collective-permute-done.7.refs_2_, ...), custom_call_target="tpu_custom_call" | custom-call | tf_op jit(solution)/shard_map/pallas_call | solution.py:331
Async XLA Ops:
  2.6 14.3 %collective-permute-start.1 = (bf16[65,8,128]{2,1,0:T(8,128)(2,1)S(1)}, bf16[65,8,128]{2,1,0:T(8,128)(2,1)S(1)}, u32[]{:S(2)}, u32[]{:S(2)}) collective-permute-start(bf16[65,8,128]{2,1,0:T(8,128)(2,1)S(1)} %get-tuple-element.24), channel_id=1, source_target_pairs={{0,8},{4,12},{8,0},{12,4},{1,9},{5,13},{9,1},{13,5},{2,10},{6,14},... | collective-permute-start | bytes 399368 | tf_op jit(solution)/shard_map/ppermute | solution.py:383
  6.7 10.8 %collective-permute-start.2 = (bf16[65,8,128]{2,1,0:T(8,128)(2,1)S(1)}, bf16[65,8,128]{2,1,0:T(8,128)(2,1)S(1)}, u32[]{:S(2)}, u32[]{:S(2)}) collective-permute-start(bf16[65,8,128]{2,1,0:T(8,128)(2,1)S(1)} %get-tuple-element.26), channel_id=1, source_target_pairs={{0,12},{4,8},{8,4},{12,0},{1,13},{5,9},{9,5},{13,1},{2,14},{6,10},... | collective-permute-start | bytes 399368 | tf_op jit(solution)/shard_map/ppermute | solution.py:383
  8.0 10.2 %collective-permute-start = (bf16[65,8,128]{2,1,0:T(8,128)(2,1)S(1)}, bf16[65,8,128]{2,1,0:T(8,128)(2,1)S(1)}, u32[]{:S(2)}, u32[]{:S(2)}) collective-permute-start(bf16[65,8,128]{2,1,0:T(8,128)(2,1)S(1)} %get-tuple-element.21), channel_id=1, source_target_pairs={{0,4},{4,0},{8,12},{12,8},{1,5},{5,1},{9,13},{13,9},{2,6},{6,2},{1... | collective-permute-start | bytes 399368 | tf_op jit(solution)/shard_map/ppermute | solution.py:383
  21.3 6.2 %collective-permute-start.3 = (f32[32,128]{1,0:T(8,128)S(1)}, f32[32,128]{1,0:T(8,128)S(1)}, u32[]{:S(2)}, u32[]{:S(2)}) collective-permute-start(f32[32,128]{1,0:T(8,128)S(1)} %get-tuple-element.35), channel_id=1, source_target_pairs={{0,4},{4,0},{8,12},{12,8},{1,5},{5,1},{9,13},{13,9},{2,6},{6,2},{1... | collective-permute-start | bytes 49160 | tf_op jit(solution)/shard_map/ppermute | solution.py:410
  23.4 4.6 %collective-permute-start.4 = (f32[32,128]{1,0:T(8,128)S(1)}, f32[32,128]{1,0:T(8,128)S(1)}, u32[]{:S(2)}, u32[]{:S(2)}) collective-permute-start(f32[32,128]{1,0:T(8,128)S(1)} %get-tuple-element.36), channel_id=1, source_target_pairs={{0,8},{4,12},{8,0},{12,4},{1,9},{5,13},{9,1},{13,5},{2,10},{6,14},... | collective-permute-start | bytes 49160 | tf_op jit(solution)/shard_map/ppermute | solution.py:410
  25.4 5.5 %collective-permute-start.5 = (f32[32,128]{1,0:T(8,128)S(1)}, f32[32,128]{1,0:T(8,128)S(1)}, u32[]{:S(2)}, u32[]{:S(2)}) collective-permute-start(f32[32,128]{1,0:T(8,128)S(1)} %get-tuple-element.37), channel_id=1, source_target_pairs={{0,12},{4,8},{8,4},{12,0},{1,13},{5,9},{9,5},{13,1},{2,14},{6,10},... | collective-permute-start | bytes 49160 | tf_op jit(solution)/shard_map/ppermute | solution.py:410
  31.6 1.9 %collective-permute-start.6 = (f32[16,128]{1,0:T(8,128)S(1)}, f32[16,128]{1,0:T(8,128)S(1)}, u32[]{:S(2)}, u32[]{:S(2)}) collective-permute-start(f32[16,128]{1,0:T(8,128)S(1)} %get-tuple-element.39.refs_0_), channel_id=1, source_target_pairs={{0,1},{1,0},{2,3},{3,2},{4,5},{5,4},{6,7},{7,6},{8,9},{9,8},{10,11... | collective-permute-start | bytes 24584 | tf_op jit(solution)/shard_map/ppermute | solution.py:422
  31.6 3.7 %collective-permute-start.7 = (f32[16,128]{1,0:T(8,128)S(1)}, f32[16,128]{1,0:T(8,128)S(1)}, u32[]{:S(2)}, u32[]{:S(2)}) collective-permute-start(f32[16,128]{1,0:T(8,128)S(1)} %get-tuple-element.39.refs_0_), channel_id=1, source_target_pairs={{0,2},{1,3},{2,0},{3,1},{4,6},{5,7},{6,4},{7,5},{8,10},{9,11},{10,... | collective-permute-start | bytes 24584 | tf_op jit(solution)/shard_map/ppermute | solution.py:422
  33.1 3.1 %collective-permute-start.8 = (f32[16,128]{1,0:T(8,128)S(1)}, f32[16,128]{1,0:T(8,128)S(1)}, u32[]{:S(2)}, u32[]{:S(2)}) collective-permute-start(f32[16,128]{1,0:T(8,128)S(1)} %get-tuple-element.39.refs_0_), channel_id=1, source_target_pairs={{0,3},{1,2},{2,1},{3,0},{4,7},{5,6},{6,5},{7,4},{8,11},{9,10},{10,... | collective-permute-start | bytes 24584 | tf_op jit(solution)/shard_map/ppermute | solution.py:422

commit v3 on v2

--- a/solution.py
+++ b/solution.py
@@ -172,34 +172,38 @@
         out[16 * blocks] = ends
 
 
-def split_dot(values, table, dims):
-    rows = values.shape[0]
+def pieces_of(values):
     high = values.astype(jnp.bfloat16)
     low = (values - high.astype(jnp.float32)).astype(jnp.bfloat16)
+    return jnp.concatenate([high, low], axis=0)
+
+
+def station_sums(first, second, table):
+    rows = first.shape[0]
     both = lax.dot_general(
-        jnp.concatenate([high, low], axis=0),
+        pieces_of(jnp.concatenate([first, second], axis=1)),
         table,
-        (dims, ((), ())),
+        (((1,), (1,)), ((), ())),
         preferred_element_type=jnp.float32,
     )
     return both[:rows] + both[rows:]
 
 
-def scatter(first, second, table):
-    return split_dot(jnp.concatenate([first, second], axis=1), table, ((1,), (1,)))
-
-
-def tile_terms(chunk_ref, products_ref, table_ref):
-    slots = products_ref.shape[2]
-    blocks = slots // LANES
-    ends = chunk_ref[chunk_ref.shape[0] - 1].astype(jnp.float32)
+def end_table(chunk_ref, table_ref):
+    rows = table_ref.shape[1] // LANES
+    ends = chunk_ref[chunk_ref.shape[0] - 1]
     station = lax.broadcasted_iota(jnp.int32, (STATION_COUNT, LANES), 0).astype(jnp.float32)
-    station = station - INDEX_SHIFT
-    for block in range(2 * blocks):
-        hit = station == ends[block : block + 1, :]
-        table_ref[:, block * LANES : (block + 1) * LANES] = jnp.where(hit, 1.0, 0.0).astype(
-            jnp.bfloat16
+    station = (station - INDEX_SHIFT).astype(jnp.bfloat16)
+    one = jnp.ones((), jnp.bfloat16)
+    zero = jnp.zeros((), jnp.bfloat16)
+    for row in range(rows):
+        table_ref[:, row * LANES : (row + 1) * LANES] = jnp.where(
+            station == ends[row : row + 1, :], one, zero
         )
+
+
+def unit_terms(chunk_ref, products_ref):
+    blocks = products_ref.shape[2] // LANES
     plane_of = lambda plane: jnp.concatenate(
         [chunk_ref[16 * block + plane].astype(jnp.float32) for block in range(blocks)], axis=1
     )
@@ -223,21 +227,45 @@
     second = [real[0, q] + real[1, q] for q in range(2)]
     second += [-(imag[0, q] + imag[1, q]) for q in range(2)]
     second += [power[0, q] + power[1, q] for q in range(2)]
-    return scatter(jnp.concatenate(first, 0), jnp.concatenate(second, 0), table_ref[...])
+    return jnp.concatenate(first, 0), jnp.concatenate(second, 0)
 
 
 def tile_kernel(chunk_ref, products_ref, table_ref, sums_ref):
-    sums_ref[...] = tile_terms(chunk_ref, products_ref, table_ref)
-
-
-def gain_terms(gains, products_ref, table_ref):
+    end_table(chunk_ref, table_ref)
+    sums_ref[...] = station_sums(*unit_terms(chunk_ref, products_ref), table_ref[...])
+
+
+def end_gains(gains, chunk_ref, share, blocks):
+    ends = (chunk_ref[chunk_ref.shape[0] - 1].astype(jnp.float32) + INDEX_SHIFT).astype(jnp.int32)
+    result = []
+    for end in range(2):
+        found = {row: [] for row in range(4)}
+        for block in range(blocks):
+            row = end * blocks + block
+            index = jnp.broadcast_to(ends[row : row + 1, :], (share, LANES))
+            lane = index % LANES
+            group = index // LANES
+            for part in range(4):
+                rows = gains[part * share : (part + 1) * share]
+                value = None
+                for source in range(STATION_COUNT // LANES):
+                    picked = jnp.take_along_axis(
+                        rows[:, source * LANES : (source + 1) * LANES],
+                        lane,
+                        axis=1,
+                        mode="promise_in_bounds",
+                    )
+                    value = picked if value is None else jnp.where(group == source, picked, value)
+                found[part].append(value)
+        result.append([jnp.concatenate(found[part], axis=1) for part in range(4)])
+    return result
+
+
+def gain_terms(gains, chunk_ref, products_ref):
     share = products_ref.shape[1]
-    slots = products_ref.shape[2]
-    ends = split_dot(gains, table_ref[...], ((1,), (0,)))
-    gain = lambda part, feed, end: ends[
-        (2 * part + feed) * share : (2 * part + feed + 1) * share,
-        end * slots : (end + 1) * slots,
-    ]
+    blocks = products_ref.shape[2] // LANES
+    at = end_gains(gains, chunk_ref, share, blocks)
+    gain = lambda part, feed, end: at[end][2 * part + feed]
     size = {
         (feed, end): gain(0, feed, end) * gain(0, feed, end)
         + gain(1, feed, end) * gain(1, feed, end)
@@ -265,26 +293,34 @@
         for q in range(2)
     ]
     second += [sum(size[p, 0] * power(p, q) for p in range(2)) for q in range(2)]
-    return scatter(jnp.concatenate(first, 0), jnp.concatenate(second, 0), table_ref[...])
-
-
-def solve_kernel(tiles, *refs):
-    chunk_ref = refs[0]
-    products = refs[1:tiles]
-    tables = refs[tiles : 2 * tiles - 1]
-    sums = refs[2 * tiles - 1 : 3 * tiles - 2]
-    outs = refs[3 * tiles - 2 : 4 * tiles - 2]
-    own_products, own_table, solved_ref = refs[4 * tiles - 2 :]
-    share = chunk_ref.shape[1]
-    total = tile_terms(chunk_ref, own_products, own_table)
-    for part in sums:
-        total = total + part[...]
+    return jnp.concatenate(first, 0), jnp.concatenate(second, 0)
+
+
+def solve_kernel(early, late, *refs):
+    tiles = early + late
+    chunks, refs = refs[:tiles], refs[tiles:]
+    products, refs = refs[:early], refs[early:]
+    tables, refs = refs[:early], refs[early:]
+    sums, refs = refs[:early], refs[early:]
+    outs, refs = refs[:tiles], refs[tiles:]
+    late_products, refs = refs[:late], refs[late:]
+    late_tables, refs = refs[:late], refs[late:]
+    (solved_ref,) = refs
+    share = chunks[0].shape[1]
+    total = sum(part[...] for part in sums)
+    for chunk_ref, products_ref, table_ref in zip(chunks[early:], late_products, late_tables):
+        end_table(chunk_ref, table_ref)
+        total = total + station_sums(*unit_terms(chunk_ref, products_ref), table_ref[...])
     rows = 2 * share
     divisor = total[2 * rows :] + damping
     gains = jnp.concatenate([(total[:rows] + damping) / divisor, total[rows : 2 * rows] / divisor])
-    total = gain_terms(gains, own_products, own_table)
-    for products_ref, table_ref in zip(products, tables):
-        total = total + gain_terms(gains, products_ref, table_ref)
+    total = 0.0
+    for chunk_ref, products_ref, table_ref in zip(
+        chunks, products + late_products, tables + late_tables
+    ):
+        total = total + station_sums(
+            *gain_terms(gains, chunk_ref, products_ref), table_ref[...]
+        )
     divisor = total[2 * rows :] + damping
     renewed = (total[: 2 * rows] + damping * gains) / jnp.concatenate([divisor, divisor])
     solved_ref[...] = 0.5 * (renewed + gains)
@@ -296,22 +332,31 @@
 
 
 def moment_kernel(basis_ref, *refs):
-    tiles = len(refs) - 2
-    pieces, solved_ref, moments_ref = refs[:tiles], refs[tiles], refs[tiles + 1]
+    pieces, moments_ref = refs[:-1], refs[-1]
     share = pieces[0].shape[0] // 4
     here = lax.axis_index("bl")
-    for step in range(tiles):
+    columns = []
+    for step in range(len(pieces)):
+        start = pl.multiple_of((here ^ step) * share, share)
+        columns.append(basis_ref[pl.ds(start, share), :])
+    for degree in range(4):
+        for part in range(4):
+            terms = sum(
+                piece[part * share : (part + 1) * share, :] * column[:, degree : degree + 1]
+                for piece, column in zip(pieces, columns)
+            )
+            row = 4 * degree + part
+            moments_ref[row : row + 1, :] = jnp.sum(terms, axis=0, keepdims=True)
+
+
+def order_kernel(*refs):
+    pieces, solved_ref = refs[:-1], refs[-1]
+    share = pieces[0].shape[0] // 4
+    here = lax.axis_index("bl")
+    for step, piece in enumerate(pieces):
         start = pl.multiple_of((here ^ step) * share, share)
         for part in range(4):
-            solved_ref[part, pl.ds(start, share), :] = pieces[step][
-                part * share : (part + 1) * share, :
-            ]
-    for degree in range(4):
-        column = basis_ref[:, degree : degree + 1]
-        for part in range(4):
-            moments_ref[4 * degree + part : 4 * degree + part + 1, :] = jnp.sum(
-                solved_ref[part] * column, axis=0, keepdims=True
-            )
+            solved_ref[part, pl.ds(start, share), :] = piece[part * share : (part + 1) * share, :]
 
 
 def fit_kernel(basis_ref, *refs):
@@ -390,34 +435,34 @@
     cost = pl.CostEstimate(
         flops=24 * share * slots * STATION_COUNT, bytes_accessed=4 << 20, transcendentals=0
     )
-    done = [vmem_call(tile_kernel, tile_outs, cost_estimate=cost)(chunks[k]) for k in [0] + order[:-1]]
-    last = order[-1]
+    early, late = [0, 1], [step for step in order if step > 1]
+    done = [vmem_call(tile_kernel, tile_outs, cost_estimate=cost)(chunks[k]) for k in early]
     pieces = vmem_call(
-        functools.partial(solve_kernel, tiles),
+        functools.partial(solve_kernel, len(early), len(late)),
         tuple(shape((4 * share, owned), f32) for _ in range(tiles)),
         scratch=[
-            pltpu.VMEM((12, share, slots), f32),
-            pltpu.VMEM((STATION_COUNT, 2 * slots), jnp.bfloat16),
+            *[pltpu.VMEM((12, share, slots), f32) for _ in late],
+            *[pltpu.VMEM((STATION_COUNT, 2 * slots), jnp.bfloat16) for _ in late],
             pltpu.VMEM((4 * share, STATION_COUNT), f32),
         ],
     )(
-        chunks[last],
+        *[chunks[step] for step in early + late],
         *[part[0] for part in done],
         *[part[1] for part in done],
         *[part[2] for part in done],
     )
-    received = [pieces[0]] + [
-        lax.ppermute(pieces[step], "bl", partners(tiles, step)) for step in steps
-    ]
+    received = {0: pieces[0]}
+    for step in reversed(steps):
+        received[step] = lax.ppermute(pieces[step], "bl", partners(tiles, step))
+    received = [received[step] for step in range(tiles)]
     basis = lax.dynamic_slice_in_dim(
         jnp.asarray(poly_basis(channel_local * groups).T),
         lax.axis_index("ch") * channel_local,
         channel_local,
         0,
     )
-    solved, moments = vmem_call(
-        moment_kernel, (shape((4, channel_local, owned), f32), shape((16, owned), f32))
-    )(basis, *received)
+    moments = vmem_call(moment_kernel, shape((16, owned), f32))(basis, *received)
+    solved = vmem_call(order_kernel, shape((4, channel_local, owned), f32))(*received)
     moment_parts = [moments] + [
         lax.ppermute(moments, "ch", partners(groups, step)) for step in range(1, groups)
     ]

time: 37.2 us -> 35.7 us (0.960)
  Pallas kernels: 7.81 us -> 6.31 us
  starting transfers between devices: 13.1 us -> 12.2 us
  waiting for transfers between devices: 14 us -> 14.9 us
    pallas_call x7, Pallas kernels: 7.81 us -> 6.31 us  [call(): pl.pallas_call(kernel, out_shape=outs, in_specs=[pl.BlockSpec(memory_spac...]
    ppermute x3, waiting for transfers between devices: 7.89 us -> 9.34 us  [local_resplit(): chunks[step] = lax.ppermute(piece, 'bl', partners(tiles, step))]
    ppermute x3, starting transfers between devices: 5.49 us -> 4.58 us  [local_resplit(): received[step] = lax.ppermute(pieces[step], 'bl', partners(tiles, step))]
    ppermute x3, waiting for transfers between devices: 2.7 us -> 2.15 us  [local_resplit(): lax.ppermute(moments, 'ch', partners(groups, step))]
  transfers between devices with their start and end apart: 9 -> 9, of which waited for: 5 -> 6; matrix products, arithmetic and copies ran while one was open for 2% -> 2% of each run, Pallas kernels for 5% -> 5%
where the time goes in v3:
time: 35.7 us; the launch traced here: 35.5 us
  waiting for transfers between devices  14.9 us (42%)
  starting transfers between devices  12.2 us (34%)
  Pallas kernels  6.31 us (18%)
  between operations  1.33 us (4%)
  local copies, waits for them, and re-layouts  0.72 us (2%)
    ppermute x3, waiting for transfers between devices, local_resplit(): chunks[step] = lax.ppermute(piece, 'bl', partners(tiles, step))  9.34 us
    pallas_call x7, Pallas kernels, call(): pl.pallas_call(kernel, out_shape=outs, in_specs=[pl.BlockSpec(memory_spac...  6.31 us
    ppermute x3, starting transfers between devices, local_resplit(): chunks[step] = lax.ppermute(piece, 'bl', partners(tiles, step))  5.71 us
    ppermute x3, starting transfers between devices, local_resplit(): received[step] = lax.ppermute(pieces[step], 'bl', partners(tiles, step))  4.58 us
    ppermute x3, waiting for transfers between devices, local_resplit(): received[step] = lax.ppermute(pieces[step], 'bl', partners(tiles, step))  3.43 us
    ppermute x3, waiting for transfers between devices, local_resplit(): lax.ppermute(moments, 'ch', partners(groups, step))  2.15 us
    ppermute x3, starting transfers between devices, local_resplit(): lax.ppermute(moments, 'ch', partners(groups, step))  1.92 us
    dynamic_slice x1, local copies, waits for them, and re-layouts, local_resplit(): lax.dynamic_slice_in_dim(jnp.asarray(poly_basis(channel_local * groups).T...  0.72 us
  transfers between devices with their start and end apart: 9, of which 6 were waited for; matrix products, arithmetic and copies ran while one was open for 2% of the time, Pallas kernels for 5%

profile of v3, /device:TPU:0, one launch (start us, length us, event | category | flops | bytes accessed | tf_op | source)
XLA Modules:
  0.0 35.5 jit_solution(13873810752697793420)
XLA Ops:
  1.3 1.3 %shard_map.77 = (bf16[65,8,128]{2,1,0:T(8,128)(2,1)S(1)}, bf16[65,8,128]{2,1,0:T(8,128)(2,1)S(1)}, bf16[65,8,128]{2,1,0:T(8,128)(2,1)S(1)}, bf16[65,8,128]{2,1,0:T(8,128)(2,1)S(1)}) custom-call(s32[1]{0:T(128)S(6)} %copy.8.counts_ref, bf16[8,32,512]{2,1,0:T(8,128)(2,1)} %vis_hbm.1, bf16[8,32,512]{2,1,0:T(8,128)(2,1)} %sky_hbm.1, s32[2,512]{1,0:T(2,128)} %pairs_hbm.1, ...), custom_call_target="tpu_custom_call" | custom-call | tf_op jit(solution)/shard_map/pallas_call | solution.py:376
  2.6 3.1 %collective-permute-start = (bf16[65,8,128]{2,1,0:T(8,128)(2,1)S(1)}, bf16[65,8,128]{2,1,0:T(8,128)(2,1)S(1)}, u32[]{:S(2)}, u32[]{:S(2)}) collective-permute-start(bf16[65,8,128]{2,1,0:T(8,128)(2,1)S(1)} %get-tuple-element.17), channel_id=1, source_target_pairs={{0,4},{4,0},{8,12},{12,8},{1,5},{5,1},{9,13},{13,9},{2,6},{6,2},{1... | collective-permute-start | bytes 399368 | tf_op jit(solution)/shard_map/ppermute | solution.py:428
  5.7 2.6 %collective-permute-start.1 = (bf16[65,8,128]{2,1,0:T(8,128)(2,1)S(1)}, bf16[65,8,128]{2,1,0:T(8,128)(2,1)S(1)}, u32[]{:S(2)}, u32[]{:S(2)}) collective-permute-start(bf16[65,8,128]{2,1,0:T(8,128)(2,1)S(1)} %get-tuple-element.18), channel_id=1, source_target_pairs={{0,8},{4,12},{8,0},{12,4},{1,9},{5,13},{9,1},{13,5},{2,10},{6,14},... | collective-permute-start | bytes 399368 | tf_op jit(solution)/shard_map/ppermute | solution.py:428
  8.3 0.0 collective-permute-start.2
  8.3 0.5 %shard_map.78 = (f32[12,8,512]{2,1,0:T(8,128)S(1)}, bf16[512,1024]{1,0:T(8,128)(2,1)S(1)}, f32[48,512]{1,0:T(8,128)S(1)}) custom-call(bf16[65,8,128]{2,1,0:T(8,128)(2,1)S(1)} %get-tuple-element.16.chunk_ref.refs_0_), custom_call_target="tpu_custom_call" | custom-call | flops 50331648 | bytes 4194304 | tf_op jit(solution)/shard_map/pallas_call | solution.py:376
  8.8 2.0 %collective-permute-done.chunk_ref.refs_1_ = bf16[65,8,128]{2,1,0:T(8,128)(2,1)S(1)} collective-permute-done((bf16[65,8,128]{2,1,0:T(8,128)(2,1)S(1)}, bf16[65,8,128]{2,1,0:T(8,128)(2,1)S(1)}, u32[]{:S(2)}, u32[]{:S(2)}) %collective-permute-start) | collective-permute-done | bytes 133152 | tf_op jit(solution)/shard_map/ppermute | solution.py:428
  10.9 0.5 %shard_map.79 = (f32[12,8,512]{2,1,0:T(8,128)S(1)}, bf16[512,1024]{1,0:T(8,128)(2,1)S(1)}, f32[48,512]{1,0:T(8,128)S(1)}) custom-call(bf16[65,8,128]{2,1,0:T(8,128)(2,1)S(1)} %collective-permute-done.chunk_ref.refs_1_), custom_call_target="tpu_custom_call" | custom-call | flops 50331648 | bytes 4194304 | tf_op jit(solution)/shard_map/pallas_call | solution.py:376
  11.4 7.3 %collective-permute-done.1.refs_2_ = bf16[65,8,128]{2,1,0:T(8,128)(2,1)S(1)} collective-permute-done((bf16[65,8,128]{2,1,0:T(8,128)(2,1)S(1)}, bf16[65,8,128]{2,1,0:T(8,128)(2,1)S(1)}, u32[]{:S(2)}, u32[]{:S(2)}) %collective-permute-start.1) | collective-permute-done | bytes 133152 | tf_op jit(solution)/shard_map/ppermute | solution.py:428
  18.7 0.0 collective-permute-done.2.refs_3_
  18.7 2.4 %shard_map.80 = (f32[32,128]{1,0:T(8,128)S(1)}, f32[32,128]{1,0:T(8,128)S(1)}, f32[32,128]{1,0:T(8,128)S(1)}, f32[32,128]{1,0:T(8,128)S(1)}) custom-call(bf16[65,8,128]{2,1,0:T(8,128)(2,1)S(1)} %get-tuple-element.16.chunk_ref.refs_0_, bf16[65,8,128]{2,1,0:T(8,128)(2,1)S(1)} %collective-permute-done.chunk_ref.refs_1_, ...), custom_call_target="tpu_custom_call" | custom-call | tf_op jit(solution)/shard_map/pallas_call | solution.py:376
  21.1 2.1 %collective-permute-start.3 = (f32[32,128]{1,0:T(8,128)S(1)}, f32[32,128]{1,0:T(8,128)S(1)}, u32[]{:S(2)}, u32[]{:S(2)}) collective-permute-start(f32[32,128]{1,0:T(8,128)S(1)} %get-tuple-element.27), channel_id=1, source_target_pairs={{0,4},{4,0},{8,12},{12,8},{1,5},{5,1},{9,13},{13,9},{2,6},{6,2},{1... | collective-permute-start | bytes 49160 | tf_op jit(solution)/shard_map/ppermute | solution.py:456
  23.3 1.1 %collective-permute-start.4 = (f32[32,128]{1,0:T(8,128)S(1)}, f32[32,128]{1,0:T(8,128)S(1)}, u32[]{:S(2)}, u32[]{:S(2)}) collective-permute-start(f32[32,128]{1,0:T(8,128)S(1)} %get-tuple-element.28), channel_id=1, source_target_pairs={{0,8},{4,12},{8,0},{12,4},{1,9},{5,13},{9,1},{13,5},{2,10},{6,14},... | collective-permute-start | bytes 49160 | tf_op jit(solution)/shard_map/ppermute | solution.py:456
  24.3 1.4 %collective-permute-start.5 = (f32[32,128]{1,0:T(8,128)S(1)}, f32[32,128]{1,0:T(8,128)S(1)}, u32[]{:S(2)}, u32[]{:S(2)}) collective-permute-start(f32[32,128]{1,0:T(8,128)S(1)} %get-tuple-element.29), channel_id=1, source_target_pairs={{0,12},{4,8},{8,4},{12,0},{1,13},{5,9},{9,5},{13,1},{2,14},{6,10},... | collective-permute-start | bytes 49160 | tf_op jit(solution)/shard_map/ppermute | solution.py:456
  25.7 0.7 %constant_dynamic-slice_fusion.basis_ref = f32[32,4]{1,0:T(8,128)S(1)} fusion(f32[128,4]{1,0:T(8,128)} %constant.12.clone, s32[]{:T(128)S(6)} %select_n.3), kind=kLoop, calls=%fused_computation | loop fusion | bytes 1028 | tf_op jit(solution)/shard_map/dynamic_slice | solution.py:458
  26.4 0.0 collective-permute-done.3.refs_1_
  26.4 1.5 %collective-permute-done.4.refs_2_ = f32[32,128]{1,0:T(8,128)S(1)} collective-permute-done((f32[32,128]{1,0:T(8,128)S(1)}, f32[32,128]{1,0:T(8,128)S(1)}, u32[]{:S(2)}, u32[]{:S(2)}) %collective-permute-start.4) | collective-permute-done | bytes 16416 | tf_op jit(solution)/shard_map/ppermute | solution.py:456
  28.0 1.9 %collective-permute-done.5.refs_3_ = f32[32,128]{1,0:T(8,128)S(1)} collective-permute-done((f32[32,128]{1,0:T(8,128)S(1)}, f32[32,128]{1,0:T(8,128)S(1)}, u32[]{:S(2)}, u32[]{:S(2)}) %collective-permute-start.5) | collective-permute-done | bytes 16416 | tf_op jit(solution)/shard_map/ppermute | solution.py:456
  29.9 0.1 shard_map.82.refs_0_
  30.0 0.1 collective-permute-start.6
  30.1 1.6 %collective-permute-start.7 = (f32[16,128]{1,0:T(8,128)S(1)}, f32[16,128]{1,0:T(8,128)S(1)}, u32[]{:S(2)}, u32[]{:S(2)}) collective-permute-start(f32[16,128]{1,0:T(8,128)S(1)} %shard_map.82.refs_0_), channel_id=1, source_target_pairs={{0,2},{1,3},{2,0},{3,1},{4,6},{5,7},{6,4},{7,5},{8,10},{9,11},{10,... | collective-permute-start | bytes 24584 | tf_op jit(solution)/shard_map/ppermute | solution.py:467
  31.6 0.3 collective-permute-start.8
  31.9 0.6 %shard_map.81 = f32[4,32,128]{2,1,0:T(8,128)} custom-call(f32[32,128]{1,0:T(8,128)S(1)} %get-tuple-element.26.refs_0_, f32[32,128]{1,0:T(8,128)S(1)} %collective-permute-done.3.refs_1_, f32[32,128]{1,0:T(8,128)S(1)} %collective-permute-done.4.refs_2_, f32[32,128]{1,0:T(8,128)S(1)} %collective-permute-done.5.refs_3_), custom_call_target="tpu_custom_call" | custom-call | tf_op jit(solution)/shard_map/pallas_call | solution.py:376
  32.6 0.0 collective-permute-done.6.refs_1_
  32.6 1.2 %collective-permute-done.7.refs_2_ = f32[16,128]{1,0:T(8,128)S(1)} collective-permute-done((f32[16,128]{1,0:T(8,128)S(1)}, f32[16,128]{1,0:T(8,128)S(1)}, u32[]{:S(2)}, u32[]{:S(2)}) %collective-permute-start.7) | collective-permute-done | bytes 8224 | tf_op jit(solution)/shard_map/ppermute | solution.py:467
  33.8 0.9 %collective-permute-done.8.refs_3_ = f32[16,128]{1,0:T(8,128)S(1)} collective-permute-done((f32[16,128]{1,0:T(8,128)S(1)}, f32[16,128]{1,0:T(8,128)S(1)}, u32[]{:S(2)}, u32[]{:S(2)}) %collective-permute-start.8) | collective-permute-done | bytes 8224 | tf_op jit(solution)/shard_map/ppermute | solution.py:467
  34.7 0.8 %shard_map.83 = f32[4,32,128]{2,1,0:T(8,128)} custom-call(f32[32,4]{1,0:T(8,128)S(1)} %constant_dynamic-slice_fusion.basis_ref, f32[16,128]{1,0:T(8,128)S(1)} %shard_map.82.refs_0_, f32[16,128]{1,0:T(8,128)S(1)} %collective-permute-done.6.refs_1_, f32[16,128]{1,0:T(8,128)S(1)} %collective-permute-done.7.refs_2_, f32[16,128]{1,0:T(8,128)S(1)} %collective-permute-done.8.refs_3_), custom_call_target="tpu_custom_call" | custom-call | tf_op jit(solution)/shard_map/pallas_call | solution.py:376
Async XLA Ops:
  2.6 8.3 %collective-permute-start = (bf16[65,8,128]{2,1,0:T(8,128)(2,1)S(1)}, bf16[65,8,128]{2,1,0:T(8,128)(2,1)S(1)}, u32[]{:S(2)}, u32[]{:S(2)}) collective-permute-start(bf16[65,8,128]{2,1,0:T(8,128)(2,1)S(1)} %get-tuple-element.17), channel_id=1, source_target_pairs={{0,4},{4,0},{8,12},{12,8},{1,5},{5,1},{9,13},{13,9},{2,6},{6,2},{1... | collective-permute-start | bytes 399368 | tf_op jit(solution)/shard_map/ppermute | solution.py:428
  5.7 13.0 %collective-permute-start.1 = (bf16[65,8,128]{2,1,0:T(8,128)(2,1)S(1)}, bf16[65,8,128]{2,1,0:T(8,128)(2,1)S(1)}, u32[]{:S(2)}, u32[]{:S(2)}) collective-permute-start(bf16[65,8,128]{2,1,0:T(8,128)(2,1)S(1)} %get-tuple-element.18), channel_id=1, source_target_pairs={{0,8},{4,12},{8,0},{12,4},{1,9},{5,13},{9,1},{13,5},{2,10},{6,14},... | collective-permute-start | bytes 399368 | tf_op jit(solution)/shard_map/ppermute | solution.py:428
  8.3 10.4 %collective-permute-start.2 = (bf16[65,8,128]{2,1,0:T(8,128)(2,1)S(1)}, bf16[65,8,128]{2,1,0:T(8,128)(2,1)S(1)}, u32[]{:S(2)}, u32[]{:S(2)}) collective-permute-start(bf16[65,8,128]{2,1,0:T(8,128)(2,1)S(1)} %get-tuple-element.19), channel_id=1, source_target_pairs={{0,12},{4,8},{8,4},{12,0},{1,13},{5,9},{9,5},{13,1},{2,14},{6,10},... | collective-permute-start | bytes 399368 | tf_op jit(solution)/shard_map/ppermute | solution.py:428
  21.1 5.3 %collective-permute-start.3 = (f32[32,128]{1,0:T(8,128)S(1)}, f32[32,128]{1,0:T(8,128)S(1)}, u32[]{:S(2)}, u32[]{:S(2)}) collective-permute-start(f32[32,128]{1,0:T(8,128)S(1)} %get-tuple-element.27), channel_id=1, source_target_pairs={{0,4},{4,0},{8,12},{12,8},{1,5},{5,1},{9,13},{13,9},{2,6},{6,2},{1... | collective-permute-start | bytes 49160 | tf_op jit(solution)/shard_map/ppermute | solution.py:456
  23.3 4.7 %collective-permute-start.4 = (f32[32,128]{1,0:T(8,128)S(1)}, f32[32,128]{1,0:T(8,128)S(1)}, u32[]{:S(2)}, u32[]{:S(2)}) collective-permute-start(f32[32,128]{1,0:T(8,128)S(1)} %get-tuple-element.28), channel_id=1, source_target_pairs={{0,8},{4,12},{8,0},{12,4},{1,9},{5,13},{9,1},{13,5},{2,10},{6,14},... | collective-permute-start | bytes 49160 | tf_op jit(solution)/shard_map/ppermute | solution.py:456
  24.3 5.5 %collective-permute-start.5 = (f32[32,128]{1,0:T(8,128)S(1)}, f32[32,128]{1,0:T(8,128)S(1)}, u32[]{:S(2)}, u32[]{:S(2)}) collective-permute-start(f32[32,128]{1,0:T(8,128)S(1)} %get-tuple-element.29), channel_id=1, source_target_pairs={{0,12},{4,8},{8,4},{12,0},{1,13},{5,9},{9,5},{13,1},{2,14},{6,10},... | collective-permute-start | bytes 49160 | tf_op jit(solution)/shard_map/ppermute | solution.py:456
  30.0 2.6 %collective-permute-start.6 = (f32[16,128]{1,0:T(8,128)S(1)}, f32[16,128]{1,0:T(8,128)S(1)}, u32[]{:S(2)}, u32[]{:S(2)}) collective-permute-start(f32[16,128]{1,0:T(8,128)S(1)} %shard_map.82.refs_0_), channel_id=1, source_target_pairs={{0,1},{1,0},{2,3},{3,2},{4,5},{5,4},{6,7},{7,6},{8,9},{9,8},{10,11... | collective-permute-start | bytes 24584 | tf_op jit(solution)/shard_map/ppermute | solution.py:467
  30.1 3.7 %collective-permute-start.7 = (f32[16,128]{1,0:T(8,128)S(1)}, f32[16,128]{1,0:T(8,128)S(1)}, u32[]{:S(2)}, u32[]{:S(2)}) collective-permute-start(f32[16,128]{1,0:T(8,128)S(1)} %shard_map.82.refs_0_), channel_id=1, source_target_pairs={{0,2},{1,3},{2,0},{3,1},{4,6},{5,7},{6,4},{7,5},{8,10},{9,11},{10,... | collective-permute-start | bytes 24584 | tf_op jit(solution)/shard_map/ppermute | solution.py:467
  31.6 3.1 %collective-permute-start.8 = (f32[16,128]{1,0:T(8,128)S(1)}, f32[16,128]{1,0:T(8,128)S(1)}, u32[]{:S(2)}, u32[]{:S(2)}) collective-permute-start(f32[16,128]{1,0:T(8,128)S(1)} %shard_map.82.refs_0_), channel_id=1, source_target_pairs={{0,3},{1,2},{2,1},{3,0},{4,7},{5,6},{6,5},{7,4},{8,11},{9,10},{10,... | collective-permute-start | bytes 24584 | tf_op jit(solution)/shard_map/ppermute | solution.py:467

commit v4 on v3

--- a/solution.py
+++ b/solution.py
@@ -1,5 +1,4 @@
 import functools
-import math
 
 import jax
 import jax.numpy as jnp
@@ -8,6 +7,7 @@
 from jax.experimental import pallas as pl
 from jax.experimental.pallas import tpu as pltpu
 from jax.sharding import PartitionSpec as P
+
 
 STATION_COUNT = 512
 SWEEPS = 2
@@ -452,7 +452,7 @@
         *[part[2] for part in done],
     )
     received = {0: pieces[0]}
-    for step in reversed(steps):
+    for step in steps:
         received[step] = lax.ppermute(pieces[step], "bl", partners(tiles, step))
     received = [received[step] for step in range(tiles)]
     basis = lax.dynamic_slice_in_dim(
@@ -463,9 +463,9 @@
     )
     moments = vmem_call(moment_kernel, shape((16, owned), f32))(basis, *received)
     solved = vmem_call(order_kernel, shape((4, channel_local, owned), f32))(*received)
-    moment_parts = [moments] + [
-        lax.ppermute(moments, "ch", partners(groups, step)) for step in range(1, groups)
-    ]
+    moment_parts = [moments]
+    for step in range(1, groups):
+        moment_parts.append(lax.ppermute(moments, "ch", partners(groups, step)))
     fitted = vmem_call(fit_kernel, shape((4, channel_local, owned), f32))(basis, *moment_parts)
     out_shape = (2, 2, channel_local, owned)
     return solved.reshape(out_shape), fitted.reshape(out_shape)

time: 35.7 us -> 35.7 us (level)
  no operation moved by 1% of the time
where the time goes in v4:
time: 35.7 us; the launch traced here: 35.5 us
  waiting for transfers between devices  14.9 us (42%)
  starting transfers between devices  12.2 us (34%)
  Pallas kernels  6.31 us (18%)
  between operations  1.33 us (4%)
  local copies, waits for them, and re-layouts  0.72 us (2%)
    ppermute x3, waiting for transfers between devices, local_resplit(): chunks[step] = lax.ppermute(piece, 'bl', partners(tiles, step))  9.34 us
    pallas_call x7, Pallas kernels, call(): pl.pallas_call(kernel, out_shape=outs, in_specs=[pl.BlockSpec(memory_spac...  6.31 us
    ppermute x3, starting transfers between devices, local_resplit(): chunks[step] = lax.ppermute(piece, 'bl', partners(tiles, step))  5.71 us
    ppermute x3, starting transfers between devices, local_resplit(): received[step] = lax.ppermute(pieces[step], 'bl', partners(tiles, step))  4.58 us
    ppermute x3, waiting for transfers between devices, local_resplit(): received[step] = lax.ppermute(pieces[step], 'bl', partners(tiles, step))  3.43 us
    ppermute x3, waiting for transfers between devices, local_resplit(): moment_parts.append(lax.ppermute(moments, 'ch', partners(groups, step)))  2.15 us
    ppermute x3, starting transfers between devices, local_resplit(): moment_parts.append(lax.ppermute(moments, 'ch', partners(groups, step)))  1.92 us
    dynamic_slice x1, local copies, waits for them, and re-layouts, local_resplit(): lax.dynamic_slice_in_dim(jnp.asarray(poly_basis(channel_local * groups).T...  0.72 us
  transfers between devices with their start and end apart: 9, of which 6 were waited for; matrix products, arithmetic and copies ran while one was open for 2% of the time, Pallas kernels for 5%

profile of v4, /device:TPU:0, one launch (start us, length us, event | category | flops | bytes accessed | tf_op | source)
XLA Modules:
  0.0 35.5 jit_solution(13873810752697793420)
XLA Ops:
  1.3 1.3 %shard_map.77 = (bf16[65,8,128]{2,1,0:T(8,128)(2,1)S(1)}, bf16[65,8,128]{2,1,0:T(8,128)(2,1)S(1)}, bf16[65,8,128]{2,1,0:T(8,128)(2,1)S(1)}, bf16[65,8,128]{2,1,0:T(8,128)(2,1)S(1)}) custom-call(s32[1]{0:T(128)S(6)} %copy.8.counts_ref, bf16[8,32,512]{2,1,0:T(8,128)(2,1)} %vis_hbm.1, bf16[8,32,512]{2,1,0:T(8,128)(2,1)} %sky_hbm.1, s32[2,512]{1,0:T(2,128)} %pairs_hbm.1, ...), custom_call_target="tpu_custom_call" | custom-call | tf_op jit(solution)/shard_map/pallas_call | solution.py:376
  2.6 3.1 %collective-permute-start = (bf16[65,8,128]{2,1,0:T(8,128)(2,1)S(1)}, bf16[65,8,128]{2,1,0:T(8,128)(2,1)S(1)}, u32[]{:S(2)}, u32[]{:S(2)}) collective-permute-start(bf16[65,8,128]{2,1,0:T(8,128)(2,1)S(1)} %get-tuple-element.17), channel_id=1, source_target_pairs={{0,4},{4,0},{8,12},{12,8},{1,5},{5,1},{9,13},{13,9},{2,6},{6,2},{1... | collective-permute-start | bytes 399368 | tf_op jit(solution)/shard_map/ppermute | solution.py:428
  5.7 2.6 %collective-permute-start.1 = (bf16[65,8,128]{2,1,0:T(8,128)(2,1)S(1)}, bf16[65,8,128]{2,1,0:T(8,128)(2,1)S(1)}, u32[]{:S(2)}, u32[]{:S(2)}) collective-permute-start(bf16[65,8,128]{2,1,0:T(8,128)(2,1)S(1)} %get-tuple-element.18), channel_id=1, source_target_pairs={{0,8},{4,12},{8,0},{12,4},{1,9},{5,13},{9,1},{13,5},{2,10},{6,14},... | collective-permute-start | bytes 399368 | tf_op jit(solution)/shard_map/ppermute | solution.py:428
  8.3 0.0 collective-permute-start.2
  8.3 0.5 %shard_map.78 = (f32[12,8,512]{2,1,0:T(8,128)S(1)}, bf16[512,1024]{1,0:T(8,128)(2,1)S(1)}, f32[48,512]{1,0:T(8,128)S(1)}) custom-call(bf16[65,8,128]{2,1,0:T(8,128)(2,1)S(1)} %get-tuple-element.16.chunk_ref.refs_0_), custom_call_target="tpu_custom_call" | custom-call | flops 50331648 | bytes 4194304 | tf_op jit(solution)/shard_map/pallas_call | solution.py:376
  8.8 2.0 %collective-permute-done.chunk_ref.refs_1_ = bf16[65,8,128]{2,1,0:T(8,128)(2,1)S(1)} collective-permute-done((bf16[65,8,128]{2,1,0:T(8,128)(2,1)S(1)}, bf16[65,8,128]{2,1,0:T(8,128)(2,1)S(1)}, u32[]{:S(2)}, u32[]{:S(2)}) %collective-permute-start) | collective-permute-done | bytes 133152 | tf_op jit(solution)/shard_map/ppermute | solution.py:428
  10.9 0.5 %shard_map.79 = (f32[12,8,512]{2,1,0:T(8,128)S(1)}, bf16[512,1024]{1,0:T(8,128)(2,1)S(1)}, f32[48,512]{1,0:T(8,128)S(1)}) custom-call(bf16[65,8,128]{2,1,0:T(8,128)(2,1)S(1)} %collective-permute-done.chunk_ref.refs_1_), custom_call_target="tpu_custom_call" | custom-call | flops 50331648 | bytes 4194304 | tf_op jit(solution)/shard_map/pallas_call | solution.py:376
  11.4 7.3 %collective-permute-done.1.refs_2_ = bf16[65,8,128]{2,1,0:T(8,128)(2,1)S(1)} collective-permute-done((bf16[65,8,128]{2,1,0:T(8,128)(2,1)S(1)}, bf16[65,8,128]{2,1,0:T(8,128)(2,1)S(1)}, u32[]{:S(2)}, u32[]{:S(2)}) %collective-permute-start.1) | collective-permute-done | bytes 133152 | tf_op jit(solution)/shard_map/ppermute | solution.py:428
  18.7 0.0 collective-permute-done.2.refs_3_
  18.7 2.4 %shard_map.80 = (f32[32,128]{1,0:T(8,128)S(1)}, f32[32,128]{1,0:T(8,128)S(1)}, f32[32,128]{1,0:T(8,128)S(1)}, f32[32,128]{1,0:T(8,128)S(1)}) custom-call(bf16[65,8,128]{2,1,0:T(8,128)(2,1)S(1)} %get-tuple-element.16.chunk_ref.refs_0_, bf16[65,8,128]{2,1,0:T(8,128)(2,1)S(1)} %collective-permute-done.chunk_ref.refs_1_, ...), custom_call_target="tpu_custom_call" | custom-call | tf_op jit(solution)/shard_map/pallas_call | solution.py:376
  21.1 2.1 %collective-permute-start.3 = (f32[32,128]{1,0:T(8,128)S(1)}, f32[32,128]{1,0:T(8,128)S(1)}, u32[]{:S(2)}, u32[]{:S(2)}) collective-permute-start(f32[32,128]{1,0:T(8,128)S(1)} %get-tuple-element.27), channel_id=1, source_target_pairs={{0,4},{4,0},{8,12},{12,8},{1,5},{5,1},{9,13},{13,9},{2,6},{6,2},{1... | collective-permute-start | bytes 49160 | tf_op jit(solution)/shard_map/ppermute | solution.py:456
  23.3 1.1 %collective-permute-start.4 = (f32[32,128]{1,0:T(8,128)S(1)}, f32[32,128]{1,0:T(8,128)S(1)}, u32[]{:S(2)}, u32[]{:S(2)}) collective-permute-start(f32[32,128]{1,0:T(8,128)S(1)} %get-tuple-element.28), channel_id=1, source_target_pairs={{0,8},{4,12},{8,0},{12,4},{1,9},{5,13},{9,1},{13,5},{2,10},{6,14},... | collective-permute-start | bytes 49160 | tf_op jit(solution)/shard_map/ppermute | solution.py:456
  24.3 1.4 %collective-permute-start.5 = (f32[32,128]{1,0:T(8,128)S(1)}, f32[32,128]{1,0:T(8,128)S(1)}, u32[]{:S(2)}, u32[]{:S(2)}) collective-permute-start(f32[32,128]{1,0:T(8,128)S(1)} %get-tuple-element.29), channel_id=1, source_target_pairs={{0,12},{4,8},{8,4},{12,0},{1,13},{5,9},{9,5},{13,1},{2,14},{6,10},... | collective-permute-start | bytes 49160 | tf_op jit(solution)/shard_map/ppermute | solution.py:456
  25.7 0.7 %constant_dynamic-slice_fusion.basis_ref = f32[32,4]{1,0:T(8,128)S(1)} fusion(f32[128,4]{1,0:T(8,128)} %constant.12.clone, s32[]{:T(128)S(6)} %select_n.3), kind=kLoop, calls=%fused_computation | loop fusion | bytes 1028 | tf_op jit(solution)/shard_map/dynamic_slice | solution.py:458
  26.4 0.0 collective-permute-done.3.refs_1_
  26.4 1.5 %collective-permute-done.4.refs_2_ = f32[32,128]{1,0:T(8,128)S(1)} collective-permute-done((f32[32,128]{1,0:T(8,128)S(1)}, f32[32,128]{1,0:T(8,128)S(1)}, u32[]{:S(2)}, u32[]{:S(2)}) %collective-permute-start.4) | collective-permute-done | bytes 16416 | tf_op jit(solution)/shard_map/ppermute | solution.py:456
  28.0 1.9 %collective-permute-done.5.refs_3_ = f32[32,128]{1,0:T(8,128)S(1)} collective-permute-done((f32[32,128]{1,0:T(8,128)S(1)}, f32[32,128]{1,0:T(8,128)S(1)}, u32[]{:S(2)}, u32[]{:S(2)}) %collective-permute-start.5) | collective-permute-done | bytes 16416 | tf_op jit(solution)/shard_map/ppermute | solution.py:456
  29.9 0.1 shard_map.82.refs_0_
  30.0 0.1 collective-permute-start.6
  30.1 1.6 %collective-permute-start.7 = (f32[16,128]{1,0:T(8,128)S(1)}, f32[16,128]{1,0:T(8,128)S(1)}, u32[]{:S(2)}, u32[]{:S(2)}) collective-permute-start(f32[16,128]{1,0:T(8,128)S(1)} %shard_map.82.refs_0_), channel_id=1, source_target_pairs={{0,2},{1,3},{2,0},{3,1},{4,6},{5,7},{6,4},{7,5},{8,10},{9,11},{10,... | collective-permute-start | bytes 24584 | tf_op jit(solution)/shard_map/ppermute | solution.py:468
  31.6 0.3 collective-permute-start.8
  31.9 0.6 %shard_map.81 = f32[4,32,128]{2,1,0:T(8,128)} custom-call(f32[32,128]{1,0:T(8,128)S(1)} %get-tuple-element.26.refs_0_, f32[32,128]{1,0:T(8,128)S(1)} %collective-permute-done.3.refs_1_, f32[32,128]{1,0:T(8,128)S(1)} %collective-permute-done.4.refs_2_, f32[32,128]{1,0:T(8,128)S(1)} %collective-permute-done.5.refs_3_), custom_call_target="tpu_custom_call" | custom-call | tf_op jit(solution)/shard_map/pallas_call | solution.py:376
  32.6 0.0 collective-permute-done.6.refs_1_
  32.6 1.2 %collective-permute-done.7.refs_2_ = f32[16,128]{1,0:T(8,128)S(1)} collective-permute-done((f32[16,128]{1,0:T(8,128)S(1)}, f32[16,128]{1,0:T(8,128)S(1)}, u32[]{:S(2)}, u32[]{:S(2)}) %collective-permute-start.7) | collective-permute-done | bytes 8224 | tf_op jit(solution)/shard_map/ppermute | solution.py:468
  33.8 0.9 %collective-permute-done.8.refs_3_ = f32[16,128]{1,0:T(8,128)S(1)} collective-permute-done((f32[16,128]{1,0:T(8,128)S(1)}, f32[16,128]{1,0:T(8,128)S(1)}, u32[]{:S(2)}, u32[]{:S(2)}) %collective-permute-start.8) | collective-permute-done | bytes 8224 | tf_op jit(solution)/shard_map/ppermute | solution.py:468
  34.7 0.8 %shard_map.83 = f32[4,32,128]{2,1,0:T(8,128)} custom-call(f32[32,4]{1,0:T(8,128)S(1)} %constant_dynamic-slice_fusion.basis_ref, f32[16,128]{1,0:T(8,128)S(1)} %shard_map.82.refs_0_, f32[16,128]{1,0:T(8,128)S(1)} %collective-permute-done.6.refs_1_, f32[16,128]{1,0:T(8,128)S(1)} %collective-permute-done.7.refs_2_, f32[16,128]{1,0:T(8,128)S(1)} %collective-permute-done.8.refs_3_), custom_call_target="tpu_custom_call" | custom-call | tf_op jit(solution)/shard_map/pallas_call | solution.py:376
Async XLA Ops:
  2.6 8.3 %collective-permute-start = (bf16[65,8,128]{2,1,0:T(8,128)(2,1)S(1)}, bf16[65,8,128]{2,1,0:T(8,128)(2,1)S(1)}, u32[]{:S(2)}, u32[]{:S(2)}) collective-permute-start(bf16[65,8,128]{2,1,0:T(8,128)(2,1)S(1)} %get-tuple-element.17), channel_id=1, source_target_pairs={{0,4},{4,0},{8,12},{12,8},{1,5},{5,1},{9,13},{13,9},{2,6},{6,2},{1... | collective-permute-start | bytes 399368 | tf_op jit(solution)/shard_map/ppermute | solution.py:428
  5.7 13.0 %collective-permute-start.1 = (bf16[65,8,128]{2,1,0:T(8,128)(2,1)S(1)}, bf16[65,8,128]{2,1,0:T(8,128)(2,1)S(1)}, u32[]{:S(2)}, u32[]{:S(2)}) collective-permute-start(bf16[65,8,128]{2,1,0:T(8,128)(2,1)S(1)} %get-tuple-element.18), channel_id=1, source_target_pairs={{0,8},{4,12},{8,0},{12,4},{1,9},{5,13},{9,1},{13,5},{2,10},{6,14},... | collective-permute-start | bytes 399368 | tf_op jit(solution)/shard_map/ppermute | solution.py:428
  8.3 10.4 %collective-permute-start.2 = (bf16[65,8,128]{2,1,0:T(8,128)(2,1)S(1)}, bf16[65,8,128]{2,1,0:T(8,128)(2,1)S(1)}, u32[]{:S(2)}, u32[]{:S(2)}) collective-permute-start(bf16[65,8,128]{2,1,0:T(8,128)(2,1)S(1)} %get-tuple-element.19), channel_id=1, source_target_pairs={{0,12},{4,8},{8,4},{12,0},{1,13},{5,9},{9,5},{13,1},{2,14},{6,10},... | collective-permute-start | bytes 399368 | tf_op jit(solution)/shard_map/ppermute | solution.py:428
  21.1 5.3 %collective-permute-start.3 = (f32[32,128]{1,0:T(8,128)S(1)}, f32[32,128]{1,0:T(8,128)S(1)}, u32[]{:S(2)}, u32[]{:S(2)}) collective-permute-start(f32[32,128]{1,0:T(8,128)S(1)} %get-tuple-element.27), channel_id=1, source_target_pairs={{0,4},{4,0},{8,12},{12,8},{1,5},{5,1},{9,13},{13,9},{2,6},{6,2},{1... | collective-permute-start | bytes 49160 | tf_op jit(solution)/shard_map/ppermute | solution.py:456
  23.3 4.7 %collective-permute-start.4 = (f32[32,128]{1,0:T(8,128)S(1)}, f32[32,128]{1,0:T(8,128)S(1)}, u32[]{:S(2)}, u32[]{:S(2)}) collective-permute-start(f32[32,128]{1,0:T(8,128)S(1)} %get-tuple-element.28), channel_id=1, source_target_pairs={{0,8},{4,12},{8,0},{12,4},{1,9},{5,13},{9,1},{13,5},{2,10},{6,14},... | collective-permute-start | bytes 49160 | tf_op jit(solution)/shard_map/ppermute | solution.py:456
  24.3 5.5 %collective-permute-start.5 = (f32[32,128]{1,0:T(8,128)S(1)}, f32[32,128]{1,0:T(8,128)S(1)}, u32[]{:S(2)}, u32[]{:S(2)}) collective-permute-start(f32[32,128]{1,0:T(8,128)S(1)} %get-tuple-element.29), channel_id=1, source_target_pairs={{0,12},{4,8},{8,4},{12,0},{1,13},{5,9},{9,5},{13,1},{2,14},{6,10},... | collective-permute-start | bytes 49160 | tf_op jit(solution)/shard_map/ppermute | solution.py:456
  30.0 2.6 %collective-permute-start.6 = (f32[16,128]{1,0:T(8,128)S(1)}, f32[16,128]{1,0:T(8,128)S(1)}, u32[]{:S(2)}, u32[]{:S(2)}) collective-permute-start(f32[16,128]{1,0:T(8,128)S(1)} %shard_map.82.refs_0_), channel_id=1, source_target_pairs={{0,1},{1,0},{2,3},{3,2},{4,5},{5,4},{6,7},{7,6},{8,9},{9,8},{10,11... | collective-permute-start | bytes 24584 | tf_op jit(solution)/shard_map/ppermute | solution.py:468
  30.1 3.7 %collective-permute-start.7 = (f32[16,128]{1,0:T(8,128)S(1)}, f32[16,128]{1,0:T(8,128)S(1)}, u32[]{:S(2)}, u32[]{:S(2)}) collective-permute-start(f32[16,128]{1,0:T(8,128)S(1)} %shard_map.82.refs_0_), channel_id=1, source_target_pairs={{0,2},{1,3},{2,0},{3,1},{4,6},{5,7},{6,4},{7,5},{8,10},{9,11},{10,... | collective-permute-start | bytes 24584 | tf_op jit(solution)/shard_map/ppermute | solution.py:468
  31.6 3.1 %collective-permute-start.8 = (f32[16,128]{1,0:T(8,128)S(1)}, f32[16,128]{1,0:T(8,128)S(1)}, u32[]{:S(2)}, u32[]{:S(2)}) collective-permute-start(f32[16,128]{1,0:T(8,128)S(1)} %shard_map.82.refs_0_), channel_id=1, source_target_pairs={{0,3},{1,2},{2,1},{3,0},{4,7},{5,6},{6,5},{7,4},{8,11},{9,10},{10,... | collective-permute-start | bytes 24584 | tf_op jit(solution)/shard_map/ppermute | solution.py:468

commit v5 on v4

--- a/solution.py
+++ b/solution.py
@@ -129,47 +129,75 @@
 INDEX_SHIFT = 256.0
 
 
-def pack_kernel(order, counts_ref, vis_hbm, sky_hbm, pairs_hbm, mask_hbm, *refs):
-    tiles = len(order)
-    outs = refs[:tiles]
-    vis, sky, mask, pairs, rows, sems = refs[tiles:]
-    slots = pairs.shape[1]
+def chunk_copies(step, vis_hbm, sky_hbm, mask_hbm, out, sky, mask, sems):
+    share, slots = mask.shape
     blocks = slots // LANES
-    share = outs[0].shape[1]
-    here = lax.axis_index("bl")
-    ends_copy = pltpu.make_async_copy(pairs_hbm, pairs, sems.at[0])
-    copies = []
-    for slot, step in enumerate(order):
-        channels = pl.ds(pl.multiple_of((here ^ step) * share, share), share)
+    channels = pl.ds(pl.multiple_of((lax.axis_index("bl") ^ step) * share, share), share)
+    copies = [
+        pltpu.make_async_copy(mask_hbm.at[channels], mask, sems.at[0]),
+        pltpu.make_async_copy(sky_hbm.at[:, channels], sky, sems.at[1]),
+    ]
+    for block in range(blocks):
         copies.append(
-            [
-                pltpu.make_async_copy(mask_hbm.at[channels], mask.at[slot], sems.at[1 + 3 * slot]),
-                pltpu.make_async_copy(sky_hbm.at[:, channels], sky.at[slot], sems.at[2 + 3 * slot]),
-                pltpu.make_async_copy(vis_hbm.at[:, channels], vis.at[slot], sems.at[3 + 3 * slot]),
-            ]
+            pltpu.make_async_copy(
+                vis_hbm.at[:, channels, pl.ds(block * LANES, LANES)],
+                out.at[pl.ds(8 * block, 8)],
+                sems.at[2 + block],
+            )
         )
-    ends_copy.start()
-    for group in copies:
-        for copy in group:
-            copy.start()
-    ends_copy.wait()
+    for copy in copies:
+        copy.start()
+    return copies
+
+
+def mask_model(out, sky, mask):
+    blocks = mask.shape[1] // LANES
+    weights = mask[...].astype(jnp.float32).astype(jnp.bfloat16)
+    for block in range(blocks):
+        lanes = slice(block * LANES, (block + 1) * LANES)
+        for plane in range(8):
+            out[8 * (blocks + block) + plane] = sky[plane, :, lanes] * weights[:, lanes]
+
+
+def first_kernel(step, vis_hbm, sky_hbm, mask_hbm, out, sky, mask, sems):
+    copies = chunk_copies(step, vis_hbm, sky_hbm, mask_hbm, out, sky, mask, sems)
+    for copy in copies[:2]:
+        copy.wait()
+    mask_model(out, sky, mask)
+    for copy in copies[2:]:
+        copy.wait()
+
+
+def pack_kernel(steps, counts_ref, vis_hbm, sky_hbm, mask_hbm, pairs_hbm, *refs):
+    outs, ends_out = refs[: len(steps)], refs[len(steps)]
+    sky, mask, pairs, rows, pairs_sem, sems = refs[len(steps) + 1 :]
+    blocks = pairs.shape[1] // LANES
+    pairs_copy = pltpu.make_async_copy(pairs_hbm, pairs, pairs_sem)
+    pairs_copy.start()
+    copies = [
+        chunk_copies(
+            step, vis_hbm, sky_hbm, mask_hbm, outs[slot], sky.at[slot], mask.at[slot], sems.at[slot]
+        )
+        for slot, step in enumerate(steps)
+    ]
+    pairs_copy.wait()
+    lane = lax.broadcasted_iota(jnp.int32, (1, LANES), 1)
     for end in range(2):
         for block in range(blocks):
             row = end * blocks + block
-            rows[row : row + 1, :] = pairs[end : end + 1, block * LANES : (block + 1) * LANES]
+            station = pairs[end : end + 1, block * LANES : (block + 1) * LANES]
+            live = lane + block * LANES < counts_ref[0]
+            rows[row : row + 1, :] = jnp.where(live, station, STATION_COUNT)
     ends = (rows[...].astype(jnp.float32) - INDEX_SHIFT).astype(jnp.bfloat16)
-    live = lax.broadcasted_iota(jnp.int32, (share, slots), 1) < counts_ref[0]
-    for slot in range(tiles):
-        out = outs[slot]
-        for copy in copies[slot]:
+    ends_out[0] = ends
+    for slot in range(len(steps)):
+        outs[slot][16 * blocks] = ends
+        for copy in copies[slot][:2]:
             copy.wait()
-        weights = jnp.where(live, mask[slot], 0).astype(jnp.float32).astype(jnp.bfloat16)
-        for block in range(blocks):
-            lanes = slice(block * LANES, (block + 1) * LANES)
-            for plane in range(8):
-                out[16 * block + plane] = vis[slot, plane, :, lanes]
-                out[16 * block + 8 + plane] = sky[slot, plane, :, lanes] * weights[:, lanes]
-        out[16 * blocks] = ends
+        mask_model(outs[slot], sky.at[slot], mask.at[slot])
+    for group in copies:
+        for copy in group[2:]:
+            copy.wait()
 
 
 def pieces_of(values):
@@ -189,14 +217,13 @@
     return both[:rows] + both[rows:]
 
 
-def end_table(chunk_ref, table_ref):
-    rows = table_ref.shape[1] // LANES
-    ends = chunk_ref[chunk_ref.shape[0] - 1]
+def end_table(ends_ref, table_ref):
+    ends = ends_ref[ends_ref.shape[0] - 1]
     station = lax.broadcasted_iota(jnp.int32, (STATION_COUNT, LANES), 0).astype(jnp.float32)
     station = (station - INDEX_SHIFT).astype(jnp.bfloat16)
     one = jnp.ones((), jnp.bfloat16)
     zero = jnp.zeros((), jnp.bfloat16)
-    for row in range(rows):
+    for row in range(table_ref.shape[1] // LANES):
         table_ref[:, row * LANES : (row + 1) * LANES] = jnp.where(
             station == ends[row : row + 1, :], one, zero
         )
@@ -204,17 +231,21 @@
 
 def unit_terms(chunk_ref, products_ref):
     blocks = products_ref.shape[2] // LANES
-    plane_of = lambda plane: jnp.concatenate(
-        [chunk_ref[16 * block + plane].astype(jnp.float32) for block in range(blocks)], axis=1
+    plane_of = lambda base, plane: jnp.concatenate(
+        [
+            chunk_ref[8 * (base * blocks + block) + plane].astype(jnp.float32)
+            for block in range(blocks)
+        ],
+        axis=1,
     )
     real, imag, power = {}, {}, {}
     for p in range(2):
         for q in range(2):
             plane = 2 * p + q
-            vis_real = plane_of(plane)
-            vis_imag = plane_of(4 + plane)
-            model_real = plane_of(8 + plane)
-            model_imag = plane_of(12 + plane)
+            vis_real = plane_of(0, plane)
+            vis_imag = plane_of(0, 4 + plane)
+            model_real = plane_of(1, plane)
+            model_imag = plane_of(1, 4 + plane)
             real[p, q] = model_real * vis_real + model_imag * vis_imag
             imag[p, q] = model_real * vis_imag - model_imag * vis_real
             power[p, q] = model_real * model_real + model_imag * model_imag
@@ -230,13 +261,13 @@
     return jnp.concatenate(first, 0), jnp.concatenate(second, 0)
 
 
-def tile_kernel(chunk_ref, products_ref, table_ref, sums_ref):
-    end_table(chunk_ref, table_ref)
+def tile_kernel(chunk_ref, ends_ref, products_ref, table_ref, sums_ref):
+    end_table(ends_ref, table_ref)
     sums_ref[...] = station_sums(*unit_terms(chunk_ref, products_ref), table_ref[...])
 
 
-def end_gains(gains, chunk_ref, share, blocks):
-    ends = (chunk_ref[chunk_ref.shape[0] - 1].astype(jnp.float32) + INDEX_SHIFT).astype(jnp.int32)
+def end_gains(gains, ends_ref, share, blocks):
+    ends = (ends_ref[ends_ref.shape[0] - 1].astype(jnp.float32) + INDEX_SHIFT).astype(jnp.int32)
     result = []
     for end in range(2):
         found = {row: [] for row in range(4)}
@@ -261,10 +292,10 @@
     return result
 
 
-def gain_terms(gains, chunk_ref, products_ref):
+def gain_terms(gains, ends_ref, products_ref):
     share = products_ref.shape[1]
     blocks = products_ref.shape[2] // LANES
-    at = end_gains(gains, chunk_ref, share, blocks)
+    at = end_gains(gains, ends_ref, share, blocks)
     gain = lambda part, feed, end: at[end][2 * part + feed]
     size = {
         (feed, end): gain(0, feed, end) * gain(0, feed, end)
@@ -298,7 +329,8 @@
 
 def solve_kernel(early, late, *refs):
     tiles = early + late
-    chunks, refs = refs[:tiles], refs[tiles:]
+    chunks, refs = refs[:late], refs[late:]
+    ends, refs = refs[:tiles], refs[tiles:]
     products, refs = refs[:early], refs[early:]
     tables, refs = refs[:early], refs[early:]
     sums, refs = refs[:early], refs[early:]
@@ -306,21 +338,21 @@
     late_products, refs = refs[:late], refs[late:]
     late_tables, refs = refs[:late], refs[late:]
     (solved_ref,) = refs
-    share = chunks[0].shape[1]
+    share = products[0].shape[1]
     total = sum(part[...] for part in sums)
-    for chunk_ref, products_ref, table_ref in zip(chunks[early:], late_products, late_tables):
-        end_table(chunk_ref, table_ref)
+    for chunk_ref, ends_ref, products_ref, table_ref in zip(
+        chunks, ends[early:], late_products, late_tables
+    ):
+        end_table(ends_ref, table_ref)
         total = total + station_sums(*unit_terms(chunk_ref, products_ref), table_ref[...])
     rows = 2 * share
     divisor = total[2 * rows :] + damping
     gains = jnp.concatenate([(total[:rows] + damping) / divisor, total[rows : 2 * rows] / divisor])
     total = 0.0
-    for chunk_ref, products_ref, table_ref in zip(
-        chunks, products + late_products, tables + late_tables
+    for ends_ref, products_ref, table_ref in zip(
+        ends, products + late_products, tables + late_tables
     ):
-        total = total + station_sums(
-            *gain_terms(gains, chunk_ref, products_ref), table_ref[...]
-        )
+        total = total + station_sums(*gain_terms(gains, ends_ref, products_ref), table_ref[...])
     divisor = total[2 * rows :] + damping
     renewed = (total[: 2 * rows] + damping * gains) / jnp.concatenate([divisor, divisor])
     solved_ref[...] = 0.5 * (renewed + gains)
@@ -407,49 +439,75 @@
     shape = jax.ShapeDtypeStruct
 
     steps = list(range(1, tiles))
-    order = sorted(steps, key=lambda step: step == 1)
+    first = FIRST
+    others = [step for step in steps if step != first] + [0]
     blocks = slots // LANES
-    chunk_shape = shape((16 * blocks + 1, share, LANES), jnp.bfloat16)
-    packed = vmem_call(
-        functools.partial(pack_kernel, order + [0]),
-        (chunk_shape,) * tiles,
+    bf16 = jnp.bfloat16
+    (lead,) = vmem_call(
+        functools.partial(first_kernel, first),
+        (shape((16 * blocks, share, LANES), bf16),),
         scratch=[
-            pltpu.VMEM((tiles, 8, share, slots), jnp.bfloat16),
-            pltpu.VMEM((tiles, 8, share, slots), jnp.bfloat16),
-            pltpu.VMEM((tiles, share, slots), jnp.int32),
+            pltpu.VMEM((8, share, slots), bf16),
+            pltpu.VMEM((share, slots), jnp.int32),
+            pltpu.SemaphoreType.DMA((2 + blocks,)),
+        ],
+        spaces=[pltpu.HBM] * 3,
+    )(in_hbm(visibilities), in_hbm(sky_model), in_hbm(usable_mask))
+    tile_counts, lead = lax.optimization_barrier((tile_counts, lead))
+    *packed, own_ends = vmem_call(
+        functools.partial(pack_kernel, others),
+        (shape((16 * blocks + 1, share, LANES), bf16),) * len(others)
+        + (shape((1, 2 * blocks, LANES), bf16),),
+        scratch=[
+            pltpu.VMEM((len(others), 8, share, slots), bf16),
+            pltpu.VMEM((len(others), share, slots), jnp.int32),
             pltpu.VMEM((2, slots), jnp.int32),
             pltpu.VMEM((2 * blocks, LANES), jnp.int32),
-            pltpu.SemaphoreType.DMA((1 + 3 * tiles,)),
+            pltpu.SemaphoreType.DMA,
+            pltpu.SemaphoreType.DMA((len(others), 2 + blocks)),
         ],
         spaces=[pltpu.SMEM] + [pltpu.HBM] * 4,
-    )(tile_counts, *[in_hbm(x) for x in (visibilities, sky_model, antenna_pairs, usable_mask)])
-    chunks = {0: packed[-1]}
-    for step, piece in zip(order, packed):
-        chunks[step] = lax.ppermute(piece, "bl", partners(tiles, step))
-
-    tile_outs = (
-        shape((12, share, slots), f32),
-        shape((STATION_COUNT, 2 * slots), jnp.bfloat16),
-        shape((6 * share, STATION_COUNT), f32),
-    )
-    cost = pl.CostEstimate(
-        flops=24 * share * slots * STATION_COUNT, bytes_accessed=4 << 20, transcendentals=0
-    )
-    early, late = [0, 1], [step for step in order if step > 1]
-    done = [vmem_call(tile_kernel, tile_outs, cost_estimate=cost)(chunks[k]) for k in early]
+    )(
+        tile_counts,
+        in_hbm(visibilities),
+        in_hbm(sky_model),
+        in_hbm(usable_mask),
+        in_hbm(antenna_pairs),
+    )
+
+    def exchange(piece, step):
+        return lax.ppermute(piece, "bl", partners(tiles, step))
+
+    chunks = {0: packed[-1], first: exchange(lead, first)}
+    for piece, step in zip(packed[:-1], others):
+        chunks[step] = exchange(piece, step)
+    ends = dict(chunks)
+    ends[first] = exchange(own_ends, first)
+
+    products_shape = shape((12, share, slots), f32)
+    table_shape = shape((STATION_COUNT, 2 * slots), bf16)
+    sums_shape = shape((6 * share, STATION_COUNT), f32)
+    tile_outs = (products_shape, table_shape, sums_shape)
+    late = [steps[-1]]
+    done = {
+        step: vmem_call(tile_kernel, tile_outs)(chunks[step], ends[step])
+        for step in range(tiles)
+        if step not in late
+    }
     pieces = vmem_call(
-        functools.partial(solve_kernel, len(early), len(late)),
+        functools.partial(solve_kernel, len(done), len(late)),
         tuple(shape((4 * share, owned), f32) for _ in range(tiles)),
         scratch=[
             *[pltpu.VMEM((12, share, slots), f32) for _ in late],
-            *[pltpu.VMEM((STATION_COUNT, 2 * slots), jnp.bfloat16) for _ in late],
+            *[pltpu.VMEM((STATION_COUNT, 2 * slots), bf16) for _ in late],
             pltpu.VMEM((4 * share, STATION_COUNT), f32),
         ],
     )(
-        *[chunks[step] for step in early + late],
-        *[part[0] for part in done],
-        *[part[1] for part in done],
-        *[part[2] for part in done],
+        *[chunks[step] for step in late],
+        *[ends[step] for step in list(done) + late],
+        *[parts[0] for parts in done.values()],
+        *[parts[1] for parts in done.values()],
+        *[parts[2] for parts in done.values()],
     )
     received = {0: pieces[0]}
     for step in steps:
@@ -469,6 +527,9 @@
     fitted = vmem_call(fit_kernel, shape((4, channel_local, owned), f32))(basis, *moment_parts)
     out_shape = (2, 2, channel_local, owned)
     return solved.reshape(out_shape), fitted.reshape(out_shape)
+
+
+FIRST = 2
 
 
 def local(visibilities, sky_model, antenna_pairs, tile_counts, usable_mask):

time: 35.7 us -> 37.2 us (1.042)
  starting transfers between devices: 12.2 us -> 14.9 us
  waiting for transfers between devices: 14.9 us -> 12.3 us
  Pallas kernels: 6.31 us -> 7.44 us
    ppermute x3 -> x4, starting transfers between devices: 5.71 us -> 8.58 us  [exchange(): return lax.ppermute(piece, 'bl', partners(tiles, step))]
    ppermute x3 -> x4, waiting for transfers between devices: 9.34 us -> 7.46 us  [exchange(): return lax.ppermute(piece, 'bl', partners(tiles, step))]
    pallas_call x7 -> x9, Pallas kernels: 6.31 us -> 7.44 us  [call(): pl.pallas_call(kernel, out_shape=outs, in_specs=[pl.BlockSpec(memory_spac...]
    ppermute x3, waiting for transfers between devices: 2.15 us -> 1.23 us  [local_resplit(): moment_parts.append(lax.ppermute(moments, 'ch', partners(groups, step)))]
  transfers between devices with their start and end apart: 9 -> 10, of which waited for: 6 -> 4; matrix products, arithmetic and copies ran while one was open for 2% -> 2% of each run, Pallas kernels for 5% -> 9%
where the time goes in v5:
time: 37.2 us; the launch traced here: 36.8 us
  starting transfers between devices  14.9 us (40%)
  waiting for transfers between devices  12.3 us (33%)
  Pallas kernels  7.44 us (20%)
  between operations  1.37 us (4%)
  local copies, waits for them, and re-layouts  0.72 us (2%)
    ppermute x4, starting transfers between devices, exchange(): return lax.ppermute(piece, 'bl', partners(tiles, step))  8.58 us
    ppermute x4, waiting for transfers between devices, exchange(): return lax.ppermute(piece, 'bl', partners(tiles, step))  7.46 us
    pallas_call x9, Pallas kernels, call(): pl.pallas_call(kernel, out_shape=outs, in_specs=[pl.BlockSpec(memory_spac...  7.44 us
    ppermute x3, starting transfers between devices, local_resplit(): received[step] = lax.ppermute(pieces[step], 'bl', partners(tiles, step))  4.44 us
    ppermute x3, waiting for transfers between devices, local_resplit(): received[step] = lax.ppermute(pieces[step], 'bl', partners(tiles, step))  3.64 us
    ppermute x3, starting transfers between devices, local_resplit(): moment_parts.append(lax.ppermute(moments, 'ch', partners(groups, step)))  1.92 us
    ppermute x3, waiting for transfers between devices, local_resplit(): moment_parts.append(lax.ppermute(moments, 'ch', partners(groups, step)))  1.23 us
  transfers between devices with their start and end apart: 10, of which 4 were waited for; matrix products, arithmetic and copies ran while one was open for 2% of the time, Pallas kernels for 9%

profile of v5, /device:TPU:0, one launch (start us, length us, event | category | flops | bytes accessed | tf_op | source)
XLA Modules:
  0.0 36.8 jit_solution(48710109000084761)
XLA Ops:
  1.3 1.2 %shard_map.78 = (bf16[65,8,128]{2,1,0:T(8,128)(2,1)S(1)}, bf16[65,8,128]{2,1,0:T(8,128)(2,1)S(1)}, bf16[65,8,128]{2,1,0:T(8,128)(2,1)S(1)}, bf16[1,8,128]{2,1,0:T(8,128)(2,1)S(1)}) custom-call(s32[1]{0:T(128)S(6)} %copy.8.counts_ref, bf16[8,32,512]{2,1,0:T(8,128)(2,1)} %vis_hbm.3, bf16[8,32,512]{2,1,0:T(8,128)(2,1)} %sky_hbm.3, s32[32,512]{1,0:T(8,128)} %mask_hbm.3, ...), custom_call_target="tpu_custom_call" | custom-call | tf_op jit(solution)/shard_map/pallas_call | solution.py:408
  2.5 3.1 %collective-permute-start.1 = (bf16[65,8,128]{2,1,0:T(8,128)(2,1)S(1)}, bf16[65,8,128]{2,1,0:T(8,128)(2,1)S(1)}, u32[]{:S(2)}, u32[]{:S(2)}) collective-permute-start(bf16[65,8,128]{2,1,0:T(8,128)(2,1)S(1)} %get-tuple-element.24), channel_id=1, source_target_pairs={{0,4},{4,0},{8,12},{12,8},{1,5},{5,1},{9,13},{13,9},{2,6},{6,2},{1... | collective-permute-start | bytes 399368 | tf_op jit(solution)/shard_map/ppermute | solution.py:479
  5.6 2.5 %collective-permute-start = (bf16[65,8,128]{2,1,0:T(8,128)(2,1)S(1)}, bf16[65,8,128]{2,1,0:T(8,128)(2,1)S(1)}, u32[]{:S(2)}, u32[]{:S(2)}) collective-permute-start(bf16[65,8,128]{2,1,0:T(8,128)(2,1)S(1)} %get-tuple-element.22), channel_id=1, source_target_pairs={{0,12},{4,8},{8,4},{12,0},{1,13},{5,9},{9,5},{13,1},{2,14},{6,10},... | collective-permute-start | bytes 399368 | tf_op jit(solution)/shard_map/ppermute | solution.py:479
  8.1 0.9 %shard_map.77 = bf16[64,8,128]{2,1,0:T(8,128)(2,1)S(1)} custom-call(bf16[8,32,512]{2,1,0:T(8,128)(2,1)} %vis_hbm.3, bf16[8,32,512]{2,1,0:T(8,128)(2,1)} %sky_hbm.3, s32[32,512]{1,0:T(8,128)} %mask_hbm.3), custom_call_target="tpu_custom_call" | custom-call | tf_op jit(solution)/shard_map/pallas_call | solution.py:408
  9.1 0.2 collective-permute-start.3
  9.2 2.8 %collective-permute-start.2 = (bf16[1,8,128]{2,1,0:T(8,128)(2,1)S(1)}, bf16[1,8,128]{2,1,0:T(8,128)(2,1)S(1)}, u32[]{:S(2)}, u32[]{:S(2)}) collective-permute-start(bf16[1,8,128]{2,1,0:T(8,128)(2,1)S(1)} %get-tuple-element.25), channel_id=1, source_target_pairs={{0,8},{4,12},{8,0},{12,4},{1,9},{5,13},{9,1},{13,5},{2,10},{6,14},... | collective-permute-start | bytes 6152 | tf_op jit(solution)/shard_map/ppermute | solution.py:479
  12.0 0.5 %shard_map.79 = (f32[12,8,512]{2,1,0:T(8,128)S(1)}, bf16[512,1024]{1,0:T(8,128)(2,1)S(1)}, f32[48,512]{1,0:T(8,128)S(1)}) custom-call(bf16[65,8,128]{2,1,0:T(8,128)(2,1)S(1)} %get-tuple-element.23.chunk_ref.ends_ref.refs_1_, bf16[65,8,128]{2,1,0:T(8,128)(2,1)S(1)} %get-tuple-element.23.chunk_ref.ends_ref.refs_1_), custom_call_target="tpu_custom_call" | custom-call | tf_op jit(solution)/shard_map/pallas_call | solution.py:408
  12.6 7.5 %collective-permute-done.2.ends_ref.refs_3_ = bf16[1,8,128]{2,1,0:T(8,128)(2,1)S(1)} collective-permute-done((bf16[1,8,128]{2,1,0:T(8,128)(2,1)S(1)}, bf16[1,8,128]{2,1,0:T(8,128)(2,1)S(1)}, u32[]{:S(2)}, u32[]{:S(2)}) %collective-permute-start.2) | collective-permute-done | bytes 2080 | tf_op jit(solution)/shard_map/ppermute | solution.py:479
  20.1 0.0 collective-permute-done.3.chunk_ref
  20.1 0.5 %shard_map.81 = (f32[12,8,512]{2,1,0:T(8,128)S(1)}, bf16[512,1024]{1,0:T(8,128)(2,1)S(1)}, f32[48,512]{1,0:T(8,128)S(1)}) custom-call(bf16[64,8,128]{2,1,0:T(8,128)(2,1)S(1)} %collective-permute-done.3.chunk_ref, bf16[1,8,128]{2,1,0:T(8,128)(2,1)S(1)} %collective-permute-done.2.ends_ref.refs_3_), custom_call_target="tpu_custom_call" | custom-call | tf_op jit(solution)/shard_map/pallas_call | solution.py:408
  20.6 0.0 collective-permute-done.1.chunk_ref.ends_ref.refs_2_
  20.6 0.5 %shard_map.80 = (f32[12,8,512]{2,1,0:T(8,128)S(1)}, bf16[512,1024]{1,0:T(8,128)(2,1)S(1)}, f32[48,512]{1,0:T(8,128)S(1)}) custom-call(bf16[65,8,128]{2,1,0:T(8,128)(2,1)S(1)} %collective-permute-done.1.chunk_ref.ends_ref.refs_2_, bf16[65,8,128]{2,1,0:T(8,128)(2,1)S(1)} %collective-permute-done.1.chunk_ref.ends_ref.refs_2_), custom_call_target="tpu_custom_call" | custom-call | tf_op jit(solution)/shard_map/pallas_call | solution.py:408
  21.2 0.0 collective-permute-done.refs_0_.refs_4_
  21.2 2.1 %shard_map.82 = (f32[32,128]{1,0:T(8,128)S(1)}, f32[32,128]{1,0:T(8,128)S(1)}, f32[32,128]{1,0:T(8,128)S(1)}, f32[32,128]{1,0:T(8,128)S(1)}) custom-call(bf16[65,8,128]{2,1,0:T(8,128)(2,1)S(1)} %collective-permute-done.refs_0_.refs_4_, bf16[65,8,128]{2,1,0:T(8,128)(2,1)S(1)} %get-tuple-element.23.chunk_ref.ends_ref.refs_1_, ...), custom_call_target="tpu_custom_call" | custom-call | tf_op jit(solution)/shard_map/pallas_call | solution.py:408
  23.3 0.1 collective-permute-start.4
  23.4 3.2 %collective-permute-start.5 = (f32[32,128]{1,0:T(8,128)S(1)}, f32[32,128]{1,0:T(8,128)S(1)}, u32[]{:S(2)}, u32[]{:S(2)}) collective-permute-start(f32[32,128]{1,0:T(8,128)S(1)} %get-tuple-element.38), channel_id=1, source_target_pairs={{0,8},{4,12},{8,0},{12,4},{1,9},{5,13},{9,1},{13,5},{2,10},{6,14},... | collective-permute-start | bytes 49160 | tf_op jit(solution)/shard_map/ppermute | solution.py:514
  26.6 1.2 %collective-permute-start.6 = (f32[32,128]{1,0:T(8,128)S(1)}, f32[32,128]{1,0:T(8,128)S(1)}, u32[]{:S(2)}, u32[]{:S(2)}) collective-permute-start(f32[32,128]{1,0:T(8,128)S(1)} %get-tuple-element.39), channel_id=1, source_target_pairs={{0,12},{4,8},{8,4},{12,0},{1,13},{5,9},{9,5},{13,1},{2,14},{6,10},... | collective-permute-start | bytes 49160 | tf_op jit(solution)/shard_map/ppermute | solution.py:514
  27.7 0.7 %constant_dynamic-slice_fusion.basis_ref = f32[32,4]{1,0:T(8,128)S(1)} fusion(f32[128,4]{1,0:T(8,128)} %constant.12.clone, s32[]{:T(128)S(6)} %select_n.3), kind=kLoop, calls=%fused_computation | loop fusion | bytes 1028 | tf_op jit(solution)/shard_map/dynamic_slice | solution.py:516
  28.5 0.0 collective-permute-done.4.refs_1_
  28.5 0.0 collective-permute-done.5.refs_2_
  28.5 3.6 %collective-permute-done.6.refs_3_ = f32[32,128]{1,0:T(8,128)S(1)} collective-permute-done((f32[32,128]{1,0:T(8,128)S(1)}, f32[32,128]{1,0:T(8,128)S(1)}, u32[]{:S(2)}, u32[]{:S(2)}) %collective-permute-start.6) | collective-permute-done | bytes 16416 | tf_op jit(solution)/shard_map/ppermute | solution.py:514
  32.1 0.1 shard_map.84.refs_0_
  32.2 0.1 collective-permute-start.9
  32.3 1.6 %collective-permute-start.8 = (f32[16,128]{1,0:T(8,128)S(1)}, f32[16,128]{1,0:T(8,128)S(1)}, u32[]{:S(2)}, u32[]{:S(2)}) collective-permute-start(f32[16,128]{1,0:T(8,128)S(1)} %shard_map.84.refs_0_), channel_id=1, source_target_pairs={{0,2},{1,3},{2,0},{3,1},{4,6},{5,7},{6,4},{7,5},{8,10},{9,11},{10,... | collective-permute-start | bytes 24584 | tf_op jit(solution)/shard_map/ppermute | solution.py:526
  33.9 0.3 collective-permute-start.7
  34.1 0.6 %shard_map.83 = f32[4,32,128]{2,1,0:T(8,128)} custom-call(f32[32,128]{1,0:T(8,128)S(1)} %get-tuple-element.36.refs_0_, f32[32,128]{1,0:T(8,128)S(1)} %collective-permute-done.4.refs_1_, f32[32,128]{1,0:T(8,128)S(1)} %collective-permute-done.5.refs_2_, f32[32,128]{1,0:T(8,128)S(1)} %collective-permute-done.6.refs_3_), custom_call_target="tpu_custom_call" | custom-call | tf_op jit(solution)/shard_map/pallas_call | solution.py:408
  34.8 0.6 %collective-permute-done.9.refs_3_ = f32[16,128]{1,0:T(8,128)S(1)} collective-permute-done((f32[16,128]{1,0:T(8,128)S(1)}, f32[16,128]{1,0:T(8,128)S(1)}, u32[]{:S(2)}, u32[]{:S(2)}) %collective-permute-start.9) | collective-permute-done | bytes 8224 | tf_op jit(solution)/shard_map/ppermute | solution.py:526
  35.4 0.6 %collective-permute-done.8.refs_2_ = f32[16,128]{1,0:T(8,128)S(1)} collective-permute-done((f32[16,128]{1,0:T(8,128)S(1)}, f32[16,128]{1,0:T(8,128)S(1)}, u32[]{:S(2)}, u32[]{:S(2)}) %collective-permute-start.8) | collective-permute-done | bytes 8224 | tf_op jit(solution)/shard_map/ppermute | solution.py:526
  36.0 0.0 collective-permute-done.7.refs_1_
  36.0 0.8 %shard_map.85 = f32[4,32,128]{2,1,0:T(8,128)} custom-call(f32[32,4]{1,0:T(8,128)S(1)} %constant_dynamic-slice_fusion.basis_ref, f32[16,128]{1,0:T(8,128)S(1)} %shard_map.84.refs_0_, f32[16,128]{1,0:T(8,128)S(1)} %collective-permute-done.7.refs_1_, f32[16,128]{1,0:T(8,128)S(1)} %collective-permute-done.8.refs_2_, f32[16,128]{1,0:T(8,128)S(1)} %collective-permute-done.9.refs_3_), custom_call_target="tpu_custom_call" | custom-call | tf_op jit(solution)/shard_map/pallas_call | solution.py:408
Async XLA Ops:
  2.5 18.1 %collective-permute-start.1 = (bf16[65,8,128]{2,1,0:T(8,128)(2,1)S(1)}, bf16[65,8,128]{2,1,0:T(8,128)(2,1)S(1)}, u32[]{:S(2)}, u32[]{:S(2)}) collective-permute-start(bf16[65,8,128]{2,1,0:T(8,128)(2,1)S(1)} %get-tuple-element.24), channel_id=1, source_target_pairs={{0,4},{4,0},{8,12},{12,8},{1,5},{5,1},{9,13},{13,9},{2,6},{6,2},{1... | collective-permute-start | bytes 399368 | tf_op jit(solution)/shard_map/ppermute | solution.py:479
  5.6 15.5 %collective-permute-start = (bf16[65,8,128]{2,1,0:T(8,128)(2,1)S(1)}, bf16[65,8,128]{2,1,0:T(8,128)(2,1)S(1)}, u32[]{:S(2)}, u32[]{:S(2)}) collective-permute-start(bf16[65,8,128]{2,1,0:T(8,128)(2,1)S(1)} %get-tuple-element.22), channel_id=1, source_target_pairs={{0,12},{4,8},{8,4},{12,0},{1,13},{5,9},{9,5},{13,1},{2,14},{6,10},... | collective-permute-start | bytes 399368 | tf_op jit(solution)/shard_map/ppermute | solution.py:479
  9.1 11.0 %collective-permute-start.3 = (bf16[64,8,128]{2,1,0:T(8,128)(2,1)S(1)}, bf16[64,8,128]{2,1,0:T(8,128)(2,1)S(1)}, u32[]{:S(2)}, u32[]{:S(2)}) collective-permute-start(bf16[64,8,128]{2,1,0:T(8,128)(2,1)S(1)} %shard_map.77), channel_id=1, source_target_pairs={{0,8},{4,12},{8,0},{12,4},{1,9},{5,13},{9,1},{13,5},{2,10},{6,14},... | collective-permute-start | bytes 393224 | tf_op jit(solution)/shard_map/ppermute | solution.py:479
  9.2 10.8 %collective-permute-start.2 = (bf16[1,8,128]{2,1,0:T(8,128)(2,1)S(1)}, bf16[1,8,128]{2,1,0:T(8,128)(2,1)S(1)}, u32[]{:S(2)}, u32[]{:S(2)}) collective-permute-start(bf16[1,8,128]{2,1,0:T(8,128)(2,1)S(1)} %get-tuple-element.25), channel_id=1, source_target_pairs={{0,8},{4,12},{8,0},{12,4},{1,9},{5,13},{9,1},{13,5},{2,10},{6,14},... | collective-permute-start | bytes 6152 | tf_op jit(solution)/shard_map/ppermute | solution.py:479
  23.3 5.2 %collective-permute-start.4 = (f32[32,128]{1,0:T(8,128)S(1)}, f32[32,128]{1,0:T(8,128)S(1)}, u32[]{:S(2)}, u32[]{:S(2)}) collective-permute-start(f32[32,128]{1,0:T(8,128)S(1)} %get-tuple-element.37), channel_id=1, source_target_pairs={{0,4},{4,0},{8,12},{12,8},{1,5},{5,1},{9,13},{13,9},{2,6},{6,2},{1... | collective-permute-start | bytes 49160 | tf_op jit(solution)/shard_map/ppermute | solution.py:514
  23.4 5.1 %collective-permute-start.5 = (f32[32,128]{1,0:T(8,128)S(1)}, f32[32,128]{1,0:T(8,128)S(1)}, u32[]{:S(2)}, u32[]{:S(2)}) collective-permute-start(f32[32,128]{1,0:T(8,128)S(1)} %get-tuple-element.38), channel_id=1, source_target_pairs={{0,8},{4,12},{8,0},{12,4},{1,9},{5,13},{9,1},{13,5},{2,10},{6,14},... | collective-permute-start | bytes 49160 | tf_op jit(solution)/shard_map/ppermute | solution.py:514
  26.6 5.5 %collective-permute-start.6 = (f32[32,128]{1,0:T(8,128)S(1)}, f32[32,128]{1,0:T(8,128)S(1)}, u32[]{:S(2)}, u32[]{:S(2)}) collective-permute-start(f32[32,128]{1,0:T(8,128)S(1)} %get-tuple-element.39), channel_id=1, source_target_pairs={{0,12},{4,8},{8,4},{12,0},{1,13},{5,9},{9,5},{13,1},{2,14},{6,10},... | collective-permute-start | bytes 49160 | tf_op jit(solution)/shard_map/ppermute | solution.py:514
  32.2 3.2 %collective-permute-start.9 = (f32[16,128]{1,0:T(8,128)S(1)}, f32[16,128]{1,0:T(8,128)S(1)}, u32[]{:S(2)}, u32[]{:S(2)}) collective-permute-start(f32[16,128]{1,0:T(8,128)S(1)} %shard_map.84.refs_0_), channel_id=1, source_target_pairs={{0,3},{1,2},{2,1},{3,0},{4,7},{5,6},{6,5},{7,4},{8,11},{9,10},{10,... | collective-permute-start | bytes 24584 | tf_op jit(solution)/shard_map/ppermute | solution.py:526
  32.3 3.7 %collective-permute-start.8 = (f32[16,128]{1,0:T(8,128)S(1)}, f32[16,128]{1,0:T(8,128)S(1)}, u32[]{:S(2)}, u32[]{:S(2)}) collective-permute-start(f32[16,128]{1,0:T(8,128)S(1)} %shard_map.84.refs_0_), channel_id=1, source_target_pairs={{0,2},{1,3},{2,0},{3,1},{4,6},{5,7},{6,4},{7,5},{8,10},{9,11},{10,... | collective-permute-start | bytes 24584 | tf_op jit(solution)/shard_map/ppermute | solution.py:526
  33.9 2.2 %collective-permute-start.7 = (f32[16,128]{1,0:T(8,128)S(1)}, f32[16,128]{1,0:T(8,128)S(1)}, u32[]{:S(2)}, u32[]{:S(2)}) collective-permute-start(f32[16,128]{1,0:T(8,128)S(1)} %shard_map.84.refs_0_), channel_id=1, source_target_pairs={{0,1},{1,0},{2,3},{3,2},{4,5},{5,4},{6,7},{7,6},{8,9},{9,8},{10,11... | collective-permute-start | bytes 24584 | tf_op jit(solution)/shard_map/ppermute | solution.py:526

commit v6 on v5

--- a/solution.py
+++ b/solution.py
@@ -206,27 +206,31 @@
     return jnp.concatenate([high, low], axis=0)
 
 
-def station_sums(first, second, table):
+def station_sums(first, second, table_ref):
     rows = first.shape[0]
-    both = lax.dot_general(
+    both = jnp.dot(
         pieces_of(jnp.concatenate([first, second], axis=1)),
-        table,
-        (((1,), (1,)), ((), ())),
+        jnp.concatenate([table_ref[group] for group in range(table_ref.shape[0])], axis=1),
         preferred_element_type=jnp.float32,
     )
     return both[:rows] + both[rows:]
 
 
 def end_table(ends_ref, table_ref):
-    ends = ends_ref[ends_ref.shape[0] - 1]
-    station = lax.broadcasted_iota(jnp.int32, (STATION_COUNT, LANES), 0).astype(jnp.float32)
-    station = (station - INDEX_SHIFT).astype(jnp.bfloat16)
+    ends = ends_ref[ends_ref.shape[0] - 1].astype(jnp.float32).T
+    lane = lax.broadcasted_iota(jnp.int32, (LANES, LANES), 1).astype(jnp.float32)
     one = jnp.ones((), jnp.bfloat16)
     zero = jnp.zeros((), jnp.bfloat16)
+    stations = [
+        (lane + (group * LANES - INDEX_SHIFT)).astype(jnp.bfloat16)
+        for group in range(table_ref.shape[0])
+    ]
     for row in range(table_ref.shape[1] // LANES):
-        table_ref[:, row * LANES : (row + 1) * LANES] = jnp.where(
-            station == ends[row : row + 1, :], one, zero
-        )
+        column = jnp.broadcast_to(ends[:, row : row + 1], (LANES, LANES)).astype(jnp.bfloat16)
+        for group, station in enumerate(stations):
+            table_ref[group, row * LANES : (row + 1) * LANES, :] = jnp.where(
+                station == column, one, zero
+            )
 
 
 def unit_terms(chunk_ref, products_ref):
@@ -263,7 +267,7 @@
 
 def tile_kernel(chunk_ref, ends_ref, products_ref, table_ref, sums_ref):
     end_table(ends_ref, table_ref)
-    sums_ref[...] = station_sums(*unit_terms(chunk_ref, products_ref), table_ref[...])
+    sums_ref[...] = station_sums(*unit_terms(chunk_ref, products_ref), table_ref)
 
 
 def end_gains(gains, ends_ref, share, blocks):
@@ -344,7 +348,7 @@
         chunks, ends[early:], late_products, late_tables
     ):
         end_table(ends_ref, table_ref)
-        total = total + station_sums(*unit_terms(chunk_ref, products_ref), table_ref[...])
+        total = total + station_sums(*unit_terms(chunk_ref, products_ref), table_ref)
     rows = 2 * share
     divisor = total[2 * rows :] + damping
     gains = jnp.concatenate([(total[:rows] + damping) / divisor, total[rows : 2 * rows] / divisor])
@@ -352,7 +356,7 @@
     for ends_ref, products_ref, table_ref in zip(
         ends, products + late_products, tables + late_tables
     ):
-        total = total + station_sums(*gain_terms(gains, ends_ref, products_ref), table_ref[...])
+        total = total + station_sums(*gain_terms(gains, ends_ref, products_ref), table_ref)
     divisor = total[2 * rows :] + damping
     renewed = (total[: 2 * rows] + damping * gains) / jnp.concatenate([divisor, divisor])
     solved_ref[...] = 0.5 * (renewed + gains)
@@ -485,7 +489,8 @@
     ends[first] = exchange(own_ends, first)
 
     products_shape = shape((12, share, slots), f32)
-    table_shape = shape((STATION_COUNT, 2 * slots), bf16)
+    table_dims = (STATION_COUNT // LANES, 2 * slots, LANES)
+    table_shape = shape(table_dims, bf16)
     sums_shape = shape((6 * share, STATION_COUNT), f32)
     tile_outs = (products_shape, table_shape, sums_shape)
     late = [steps[-1]]
@@ -499,7 +504,7 @@
         tuple(shape((4 * share, owned), f32) for _ in range(tiles)),
         scratch=[
             *[pltpu.VMEM((12, share, slots), f32) for _ in late],
-            *[pltpu.VMEM((STATION_COUNT, 2 * slots), bf16) for _ in late],
+            *[pltpu.VMEM(table_dims, bf16) for _ in late],
             pltpu.VMEM((4 * share, STATION_COUNT), f32),
         ],
     )(

time: 37.2 us -> 37 us (level)
  no operation moved by 1% of the time
where the time goes in v6:
time: 37 us; the launch traced here: 36.6 us
  starting transfers between devices  14.9 us (40%)
  waiting for transfers between devices  12.3 us (33%)
  Pallas kernels  7.28 us (20%)
  between operations  1.35 us (4%)
  local copies, waits for them, and re-layouts  0.72 us (2%)
    ppermute x4, starting transfers between devices, exchange(): return lax.ppermute(piece, 'bl', partners(tiles, step))  8.58 us
    ppermute x4, waiting for transfers between devices, exchange(): return lax.ppermute(piece, 'bl', partners(tiles, step))  7.47 us
    pallas_call x9, Pallas kernels, call(): pl.pallas_call(kernel, out_shape=outs, in_specs=[pl.BlockSpec(memory_spac...  7.28 us
    ppermute x3, starting transfers between devices, local_resplit(): received[step] = lax.ppermute(pieces[step], 'bl', partners(tiles, step))  4.44 us
    ppermute x3, waiting for transfers between devices, local_resplit(): received[step] = lax.ppermute(pieces[step], 'bl', partners(tiles, step))  3.64 us
    ppermute x3, starting transfers between devices, local_resplit(): moment_parts.append(lax.ppermute(moments, 'ch', partners(groups, step)))  1.92 us
    ppermute x3, waiting for transfers between devices, local_resplit(): moment_parts.append(lax.ppermute(moments, 'ch', partners(groups, step)))  1.23 us
  transfers between devices with their start and end apart: 10, of which 4 were waited for; matrix products, arithmetic and copies ran while one was open for 2% of the time, Pallas kernels for 9%

profile of v6, /device:TPU:0, one launch (start us, length us, event | category | flops | bytes accessed | tf_op | source)
XLA Modules:
  0.0 36.6 jit_solution(17062878460574823740)
XLA Ops:
  1.3 1.2 %shard_map.78 = (bf16[65,8,128]{2,1,0:T(8,128)(2,1)S(1)}, bf16[65,8,128]{2,1,0:T(8,128)(2,1)S(1)}, bf16[65,8,128]{2,1,0:T(8,128)(2,1)S(1)}, bf16[1,8,128]{2,1,0:T(8,128)(2,1)S(1)}) custom-call(s32[1]{0:T(128)S(6)} %copy.8.counts_ref, bf16[8,32,512]{2,1,0:T(8,128)(2,1)} %vis_hbm.3, bf16[8,32,512]{2,1,0:T(8,128)(2,1)} %sky_hbm.3, s32[32,512]{1,0:T(8,128)} %mask_hbm.3, ...), custom_call_target="tpu_custom_call" | custom-call | tf_op jit(solution)/shard_map/pallas_call | solution.py:412
  2.5 3.1 %collective-permute-start.1 = (bf16[65,8,128]{2,1,0:T(8,128)(2,1)S(1)}, bf16[65,8,128]{2,1,0:T(8,128)(2,1)S(1)}, u32[]{:S(2)}, u32[]{:S(2)}) collective-permute-start(bf16[65,8,128]{2,1,0:T(8,128)(2,1)S(1)} %get-tuple-element.24), channel_id=1, source_target_pairs={{0,4},{4,0},{8,12},{12,8},{1,5},{5,1},{9,13},{13,9},{2,6},{6,2},{1... | collective-permute-start | bytes 399368 | tf_op jit(solution)/shard_map/ppermute | solution.py:483
  5.6 2.5 %collective-permute-start = (bf16[65,8,128]{2,1,0:T(8,128)(2,1)S(1)}, bf16[65,8,128]{2,1,0:T(8,128)(2,1)S(1)}, u32[]{:S(2)}, u32[]{:S(2)}) collective-permute-start(bf16[65,8,128]{2,1,0:T(8,128)(2,1)S(1)} %get-tuple-element.22), channel_id=1, source_target_pairs={{0,12},{4,8},{8,4},{12,0},{1,13},{5,9},{9,5},{13,1},{2,14},{6,10},... | collective-permute-start | bytes 399368 | tf_op jit(solution)/shard_map/ppermute | solution.py:483
  8.1 0.9 %shard_map.77 = bf16[64,8,128]{2,1,0:T(8,128)(2,1)S(1)} custom-call(bf16[8,32,512]{2,1,0:T(8,128)(2,1)} %vis_hbm.3, bf16[8,32,512]{2,1,0:T(8,128)(2,1)} %sky_hbm.3, s32[32,512]{1,0:T(8,128)} %mask_hbm.3), custom_call_target="tpu_custom_call" | custom-call | tf_op jit(solution)/shard_map/pallas_call | solution.py:412
  9.1 0.2 collective-permute-start.3
  9.2 2.8 %collective-permute-start.2 = (bf16[1,8,128]{2,1,0:T(8,128)(2,1)S(1)}, bf16[1,8,128]{2,1,0:T(8,128)(2,1)S(1)}, u32[]{:S(2)}, u32[]{:S(2)}) collective-permute-start(bf16[1,8,128]{2,1,0:T(8,128)(2,1)S(1)} %get-tuple-element.25), channel_id=1, source_target_pairs={{0,8},{4,12},{8,0},{12,4},{1,9},{5,13},{9,1},{13,5},{2,10},{6,14},... | collective-permute-start | bytes 6152 | tf_op jit(solution)/shard_map/ppermute | solution.py:483
  12.0 0.6 %shard_map.79 = (f32[12,8,512]{2,1,0:T(8,128)S(1)}, bf16[4,1024,128]{2,1,0:T(8,128)(2,1)S(1)}, f32[48,512]{1,0:T(8,128)S(1)}) custom-call(bf16[65,8,128]{2,1,0:T(8,128)(2,1)S(1)} %get-tuple-element.23.chunk_ref.ends_ref.refs_1_, bf16[65,8,128]{2,1,0:T(8,128)(2,1)S(1)} %get-tuple-element.23.chunk_ref.ends_ref.refs_1_), custom_call_target="tpu_custom_call" | custom-call | tf_op jit(solution)/shard_map/pallas_call | solution.py:412
  12.6 7.4 %collective-permute-done.2.ends_ref.refs_3_ = bf16[1,8,128]{2,1,0:T(8,128)(2,1)S(1)} collective-permute-done((bf16[1,8,128]{2,1,0:T(8,128)(2,1)S(1)}, bf16[1,8,128]{2,1,0:T(8,128)(2,1)S(1)}, u32[]{:S(2)}, u32[]{:S(2)}) %collective-permute-start.2) | collective-permute-done | bytes 2080 | tf_op jit(solution)/shard_map/ppermute | solution.py:483
  20.1 0.0 collective-permute-done.3.chunk_ref
  20.1 0.6 %shard_map.81 = (f32[12,8,512]{2,1,0:T(8,128)S(1)}, bf16[4,1024,128]{2,1,0:T(8,128)(2,1)S(1)}, f32[48,512]{1,0:T(8,128)S(1)}) custom-call(bf16[64,8,128]{2,1,0:T(8,128)(2,1)S(1)} %collective-permute-done.3.chunk_ref, bf16[1,8,128]{2,1,0:T(8,128)(2,1)S(1)} %collective-permute-done.2.ends_ref.refs_3_), custom_call_target="tpu_custom_call" | custom-call | tf_op jit(solution)/shard_map/pallas_call | solution.py:412
  20.6 0.0 collective-permute-done.1.chunk_ref.ends_ref.refs_2_
  20.7 0.6 %shard_map.80 = (f32[12,8,512]{2,1,0:T(8,128)S(1)}, bf16[4,1024,128]{2,1,0:T(8,128)(2,1)S(1)}, f32[48,512]{1,0:T(8,128)S(1)}) custom-call(bf16[65,8,128]{2,1,0:T(8,128)(2,1)S(1)} %collective-permute-done.1.chunk_ref.ends_ref.refs_2_, bf16[65,8,128]{2,1,0:T(8,128)(2,1)S(1)} %collective-permute-done.1.chunk_ref.ends_ref.refs_2_), custom_call_target="tpu_custom_call" | custom-call | tf_op jit(solution)/shard_map/pallas_call | solution.py:412
  21.2 0.0 collective-permute-done.refs_0_.refs_4_
  21.3 1.8 %shard_map.82 = (f32[32,128]{1,0:T(8,128)S(1)}, f32[32,128]{1,0:T(8,128)S(1)}, f32[32,128]{1,0:T(8,128)S(1)}, f32[32,128]{1,0:T(8,128)S(1)}) custom-call(bf16[65,8,128]{2,1,0:T(8,128)(2,1)S(1)} %collective-permute-done.refs_0_.refs_4_, bf16[65,8,128]{2,1,0:T(8,128)(2,1)S(1)} %get-tuple-element.23.chunk_ref.ends_ref.refs_1_, ...), custom_call_target="tpu_custom_call" | custom-call | tf_op jit(solution)/shard_map/pallas_call | solution.py:412
  23.1 0.1 collective-permute-start.4
  23.2 3.2 %collective-permute-start.5 = (f32[32,128]{1,0:T(8,128)S(1)}, f32[32,128]{1,0:T(8,128)S(1)}, u32[]{:S(2)}, u32[]{:S(2)}) collective-permute-start(f32[32,128]{1,0:T(8,128)S(1)} %get-tuple-element.38), channel_id=1, source_target_pairs={{0,8},{4,12},{8,0},{12,4},{1,9},{5,13},{9,1},{13,5},{2,10},{6,14},... | collective-permute-start | bytes 49160 | tf_op jit(solution)/shard_map/ppermute | solution.py:519
  26.4 1.2 %collective-permute-start.6 = (f32[32,128]{1,0:T(8,128)S(1)}, f32[32,128]{1,0:T(8,128)S(1)}, u32[]{:S(2)}, u32[]{:S(2)}) collective-permute-start(f32[32,128]{1,0:T(8,128)S(1)} %get-tuple-element.39), channel_id=1, source_target_pairs={{0,12},{4,8},{8,4},{12,0},{1,13},{5,9},{9,5},{13,1},{2,14},{6,10},... | collective-permute-start | bytes 49160 | tf_op jit(solution)/shard_map/ppermute | solution.py:519
  27.6 0.7 %constant_dynamic-slice_fusion.basis_ref = f32[32,4]{1,0:T(8,128)S(1)} fusion(f32[128,4]{1,0:T(8,128)} %constant.12.clone, s32[]{:T(128)S(6)} %select_n.3), kind=kLoop, calls=%fused_computation | loop fusion | bytes 1028 | tf_op jit(solution)/shard_map/dynamic_slice | solution.py:521
  28.3 0.0 collective-permute-done.4.refs_1_
  28.3 0.0 collective-permute-done.5.refs_2_
  28.3 3.6 %collective-permute-done.6.refs_3_ = f32[32,128]{1,0:T(8,128)S(1)} collective-permute-done((f32[32,128]{1,0:T(8,128)S(1)}, f32[32,128]{1,0:T(8,128)S(1)}, u32[]{:S(2)}, u32[]{:S(2)}) %collective-permute-start.6) | collective-permute-done | bytes 16416 | tf_op jit(solution)/shard_map/ppermute | solution.py:519
  31.9 0.1 shard_map.84.refs_0_
  32.0 0.1 collective-permute-start.9
  32.1 1.6 %collective-permute-start.8 = (f32[16,128]{1,0:T(8,128)S(1)}, f32[16,128]{1,0:T(8,128)S(1)}, u32[]{:S(2)}, u32[]{:S(2)}) collective-permute-start(f32[16,128]{1,0:T(8,128)S(1)} %shard_map.84.refs_0_), channel_id=1, source_target_pairs={{0,2},{1,3},{2,0},{3,1},{4,6},{5,7},{6,4},{7,5},{8,10},{9,11},{10,... | collective-permute-start | bytes 24584 | tf_op jit(solution)/shard_map/ppermute | solution.py:531
  33.7 0.3 collective-permute-start.7
  34.0 0.6 %shard_map.83 = f32[4,32,128]{2,1,0:T(8,128)} custom-call(f32[32,128]{1,0:T(8,128)S(1)} %get-tuple-element.36.refs_0_, f32[32,128]{1,0:T(8,128)S(1)} %collective-permute-done.4.refs_1_, f32[32,128]{1,0:T(8,128)S(1)} %collective-permute-done.5.refs_2_, f32[32,128]{1,0:T(8,128)S(1)} %collective-permute-done.6.refs_3_), custom_call_target="tpu_custom_call" | custom-call | tf_op jit(solution)/shard_map/pallas_call | solution.py:412
  34.6 0.6 %collective-permute-done.9.refs_3_ = f32[16,128]{1,0:T(8,128)S(1)} collective-permute-done((f32[16,128]{1,0:T(8,128)S(1)}, f32[16,128]{1,0:T(8,128)S(1)}, u32[]{:S(2)}, u32[]{:S(2)}) %collective-permute-start.9) | collective-permute-done | bytes 8224 | tf_op jit(solution)/shard_map/ppermute | solution.py:531
  35.2 0.6 %collective-permute-done.8.refs_2_ = f32[16,128]{1,0:T(8,128)S(1)} collective-permute-done((f32[16,128]{1,0:T(8,128)S(1)}, f32[16,128]{1,0:T(8,128)S(1)}, u32[]{:S(2)}, u32[]{:S(2)}) %collective-permute-start.8) | collective-permute-done | bytes 8224 | tf_op jit(solution)/shard_map/ppermute | solution.py:531
  35.8 0.0 collective-permute-done.7.refs_1_
  35.8 0.8 %shard_map.85 = f32[4,32,128]{2,1,0:T(8,128)} custom-call(f32[32,4]{1,0:T(8,128)S(1)} %constant_dynamic-slice_fusion.basis_ref, f32[16,128]{1,0:T(8,128)S(1)} %shard_map.84.refs_0_, f32[16,128]{1,0:T(8,128)S(1)} %collective-permute-done.7.refs_1_, f32[16,128]{1,0:T(8,128)S(1)} %collective-permute-done.8.refs_2_, f32[16,128]{1,0:T(8,128)S(1)} %collective-permute-done.9.refs_3_), custom_call_target="tpu_custom_call" | custom-call | tf_op jit(solution)/shard_map/pallas_call | solution.py:412
Async XLA Ops:
  2.5 18.1 %collective-permute-start.1 = (bf16[65,8,128]{2,1,0:T(8,128)(2,1)S(1)}, bf16[65,8,128]{2,1,0:T(8,128)(2,1)S(1)}, u32[]{:S(2)}, u32[]{:S(2)}) collective-permute-start(bf16[65,8,128]{2,1,0:T(8,128)(2,1)S(1)} %get-tuple-element.24), channel_id=1, source_target_pairs={{0,4},{4,0},{8,12},{12,8},{1,5},{5,1},{9,13},{13,9},{2,6},{6,2},{1... | collective-permute-start | bytes 399368 | tf_op jit(solution)/shard_map/ppermute | solution.py:483
  5.6 15.6 %collective-permute-start = (bf16[65,8,128]{2,1,0:T(8,128)(2,1)S(1)}, bf16[65,8,128]{2,1,0:T(8,128)(2,1)S(1)}, u32[]{:S(2)}, u32[]{:S(2)}) collective-permute-start(bf16[65,8,128]{2,1,0:T(8,128)(2,1)S(1)} %get-tuple-element.22), channel_id=1, source_target_pairs={{0,12},{4,8},{8,4},{12,0},{1,13},{5,9},{9,5},{13,1},{2,14},{6,10},... | collective-permute-start | bytes 399368 | tf_op jit(solution)/shard_map/ppermute | solution.py:483
  9.1 11.0 %collective-permute-start.3 = (bf16[64,8,128]{2,1,0:T(8,128)(2,1)S(1)}, bf16[64,8,128]{2,1,0:T(8,128)(2,1)S(1)}, u32[]{:S(2)}, u32[]{:S(2)}) collective-permute-start(bf16[64,8,128]{2,1,0:T(8,128)(2,1)S(1)} %shard_map.77), channel_id=1, source_target_pairs={{0,8},{4,12},{8,0},{12,4},{1,9},{5,13},{9,1},{13,5},{2,10},{6,14},... | collective-permute-start | bytes 393224 | tf_op jit(solution)/shard_map/ppermute | solution.py:483
  9.2 10.8 %collective-permute-start.2 = (bf16[1,8,128]{2,1,0:T(8,128)(2,1)S(1)}, bf16[1,8,128]{2,1,0:T(8,128)(2,1)S(1)}, u32[]{:S(2)}, u32[]{:S(2)}) collective-permute-start(bf16[1,8,128]{2,1,0:T(8,128)(2,1)S(1)} %get-tuple-element.25), channel_id=1, source_target_pairs={{0,8},{4,12},{8,0},{12,4},{1,9},{5,13},{9,1},{13,5},{2,10},{6,14},... | collective-permute-start | bytes 6152 | tf_op jit(solution)/shard_map/ppermute | solution.py:483
  23.1 5.2 %collective-permute-start.4 = (f32[32,128]{1,0:T(8,128)S(1)}, f32[32,128]{1,0:T(8,128)S(1)}, u32[]{:S(2)}, u32[]{:S(2)}) collective-permute-start(f32[32,128]{1,0:T(8,128)S(1)} %get-tuple-element.37), channel_id=1, source_target_pairs={{0,4},{4,0},{8,12},{12,8},{1,5},{5,1},{9,13},{13,9},{2,6},{6,2},{1... | collective-permute-start | bytes 49160 | tf_op jit(solution)/shard_map/ppermute | solution.py:519
  23.2 5.1 %collective-permute-start.5 = (f32[32,128]{1,0:T(8,128)S(1)}, f32[32,128]{1,0:T(8,128)S(1)}, u32[]{:S(2)}, u32[]{:S(2)}) collective-permute-start(f32[32,128]{1,0:T(8,128)S(1)} %get-tuple-element.38), channel_id=1, source_target_pairs={{0,8},{4,12},{8,0},{12,4},{1,9},{5,13},{9,1},{13,5},{2,10},{6,14},... | collective-permute-start | bytes 49160 | tf_op jit(solution)/shard_map/ppermute | solution.py:519
  26.4 5.5 %collective-permute-start.6 = (f32[32,128]{1,0:T(8,128)S(1)}, f32[32,128]{1,0:T(8,128)S(1)}, u32[]{:S(2)}, u32[]{:S(2)}) collective-permute-start(f32[32,128]{1,0:T(8,128)S(1)} %get-tuple-element.39), channel_id=1, source_target_pairs={{0,12},{4,8},{8,4},{12,0},{1,13},{5,9},{9,5},{13,1},{2,14},{6,10},... | collective-permute-start | bytes 49160 | tf_op jit(solution)/shard_map/ppermute | solution.py:519
  32.0 3.2 %collective-permute-start.9 = (f32[16,128]{1,0:T(8,128)S(1)}, f32[16,128]{1,0:T(8,128)S(1)}, u32[]{:S(2)}, u32[]{:S(2)}) collective-permute-start(f32[16,128]{1,0:T(8,128)S(1)} %shard_map.84.refs_0_), channel_id=1, source_target_pairs={{0,3},{1,2},{2,1},{3,0},{4,7},{5,6},{6,5},{7,4},{8,11},{9,10},{10,... | collective-permute-start | bytes 24584 | tf_op jit(solution)/shard_map/ppermute | solution.py:531
  32.1 3.7 %collective-permute-start.8 = (f32[16,128]{1,0:T(8,128)S(1)}, f32[16,128]{1,0:T(8,128)S(1)}, u32[]{:S(2)}, u32[]{:S(2)}) collective-permute-start(f32[16,128]{1,0:T(8,128)S(1)} %shard_map.84.refs_0_), channel_id=1, source_target_pairs={{0,2},{1,3},{2,0},{3,1},{4,6},{5,7},{6,4},{7,5},{8,10},{9,11},{10,... | collective-permute-start | bytes 24584 | tf_op jit(solution)/shard_map/ppermute | solution.py:531
  33.7 2.2 %collective-permute-start.7 = (f32[16,128]{1,0:T(8,128)S(1)}, f32[16,128]{1,0:T(8,128)S(1)}, u32[]{:S(2)}, u32[]{:S(2)}) collective-permute-start(f32[16,128]{1,0:T(8,128)S(1)} %shard_map.84.refs_0_), channel_id=1, source_target_pairs={{0,1},{1,0},{2,3},{3,2},{4,5},{5,4},{6,7},{7,6},{8,9},{9,8},{10,11... | collective-permute-start | bytes 24584 | tf_op jit(solution)/shard_map/ppermute | solution.py:531

commit v7 on v6

--- a/solution.py
+++ b/solution.py
@@ -206,30 +206,47 @@
     return jnp.concatenate([high, low], axis=0)
 
 
-def station_sums(first, second, table_ref):
-    rows = first.shape[0]
-    both = jnp.dot(
-        pieces_of(jnp.concatenate([first, second], axis=1)),
-        jnp.concatenate([table_ref[group] for group in range(table_ref.shape[0])], axis=1),
-        preferred_element_type=jnp.float32,
-    )
+def split_dot(values, table):
+    rows = values.shape[0]
+    both = jnp.dot(pieces_of(values), table, preferred_element_type=jnp.float32)
     return both[:rows] + both[rows:]
 
 
-def end_table(ends_ref, table_ref):
-    ends = ends_ref[ends_ref.shape[0] - 1].astype(jnp.float32).T
-    lane = lax.broadcasted_iota(jnp.int32, (LANES, LANES), 1).astype(jnp.float32)
+def station_sums(first, second, table):
+    return split_dot(jnp.concatenate([first, second], axis=1), table)
+
+
+def read_table(table_ref):
+    return jnp.concatenate([table_ref[group] for group in range(table_ref.shape[0])], axis=1)
+
+
+def shifted_stations(axis):
+    station = lax.broadcasted_iota(jnp.int32, (LANES, LANES), axis).astype(jnp.float32)
+    return [
+        (station + (group * LANES - INDEX_SHIFT)).astype(jnp.bfloat16)
+        for group in range(STATION_COUNT // LANES)
+    ]
+
+
+def end_table(ends):
+    columns = ends.astype(jnp.float32).T
     one = jnp.ones((), jnp.bfloat16)
     zero = jnp.zeros((), jnp.bfloat16)
-    stations = [
-        (lane + (group * LANES - INDEX_SHIFT)).astype(jnp.bfloat16)
-        for group in range(table_ref.shape[0])
-    ]
-    for row in range(table_ref.shape[1] // LANES):
-        column = jnp.broadcast_to(ends[:, row : row + 1], (LANES, LANES)).astype(jnp.bfloat16)
-        for group, station in enumerate(stations):
-            table_ref[group, row * LANES : (row + 1) * LANES, :] = jnp.where(
-                station == column, one, zero
+    blocks = [[] for _ in range(STATION_COUNT // LANES)]
+    for row in range(ends.shape[0]):
+        column = jnp.broadcast_to(columns[:, row : row + 1], (LANES, LANES)).astype(jnp.bfloat16)
+        for block, station in zip(blocks, shifted_stations(1)):
+            block.append(jnp.where(station == column, one, zero))
+    return [jnp.concatenate(block, axis=0) for block in blocks]
+
+
+def look_up_table(ends, table_ref):
+    one = jnp.ones((), jnp.bfloat16)
+    zero = jnp.zeros((), jnp.bfloat16)
+    for row in range(ends.shape[0]):
+        for group, station in enumerate(shifted_stations(0)):
+            table_ref[row, group * LANES : (group + 1) * LANES, :] = jnp.where(
+                station == ends[row : row + 1, :], one, zero
             )
 
 
@@ -265,9 +282,25 @@
     return jnp.concatenate(first, 0), jnp.concatenate(second, 0)
 
 
-def tile_kernel(chunk_ref, ends_ref, products_ref, table_ref, sums_ref):
-    end_table(ends_ref, table_ref)
-    sums_ref[...] = station_sums(*unit_terms(chunk_ref, products_ref), table_ref)
+def tile_kernel(chunk_ref, ends_ref, products_ref, table_ref, sums_ref, *look_up_ref):
+    ends = ends_ref[ends_ref.shape[0] - 1]
+    for group, block in enumerate(end_table(ends)):
+        table_ref[group] = block
+    sums_ref[...] = station_sums(*unit_terms(chunk_ref, products_ref), read_table(table_ref))
+    for ref in look_up_ref:
+        look_up_table(ends, ref)
+
+
+def dot_gains(gains, look_up_ref, share):
+    found = split_dot(gains, read_table(look_up_ref))
+    slots = found.shape[1] // 2
+    return [
+        [
+            found[part * share : (part + 1) * share, end * slots : (end + 1) * slots]
+            for part in range(4)
+        ]
+        for end in range(2)
+    ]
 
 
 def end_gains(gains, ends_ref, share, blocks):
@@ -296,10 +329,7 @@
     return result
 
 
-def gain_terms(gains, ends_ref, products_ref):
-    share = products_ref.shape[1]
-    blocks = products_ref.shape[2] // LANES
-    at = end_gains(gains, ends_ref, share, blocks)
+def gain_terms(at, products_ref):
     gain = lambda part, feed, end: at[end][2 * part + feed]
     size = {
         (feed, end): gain(0, feed, end) * gain(0, feed, end)
@@ -338,25 +368,27 @@
     products, refs = refs[:early], refs[early:]
     tables, refs = refs[:early], refs[early:]
     sums, refs = refs[:early], refs[early:]
+    look_up_ref, refs = refs[0], refs[1:]
     outs, refs = refs[:tiles], refs[tiles:]
     late_products, refs = refs[:late], refs[late:]
-    late_tables, refs = refs[:late], refs[late:]
     (solved_ref,) = refs
     share = products[0].shape[1]
     total = sum(part[...] for part in sums)
-    for chunk_ref, ends_ref, products_ref, table_ref in zip(
-        chunks, ends[early:], late_products, late_tables
-    ):
-        end_table(ends_ref, table_ref)
-        total = total + station_sums(*unit_terms(chunk_ref, products_ref), table_ref)
+    tables = [read_table(table_ref) for table_ref in tables]
+    for chunk_ref, ends_ref, products_ref in zip(chunks, ends[early:], late_products):
+        tables.append(jnp.concatenate(end_table(ends_ref[ends_ref.shape[0] - 1]), axis=1))
+        total = total + station_sums(*unit_terms(chunk_ref, products_ref), tables[-1])
     rows = 2 * share
     divisor = total[2 * rows :] + damping
     gains = jnp.concatenate([(total[:rows] + damping) / divisor, total[rows : 2 * rows] / divisor])
     total = 0.0
-    for ends_ref, products_ref, table_ref in zip(
-        ends, products + late_products, tables + late_tables
-    ):
-        total = total + station_sums(*gain_terms(gains, ends_ref, products_ref), table_ref)
+    blocks = products[0].shape[2] // LANES
+    for tile, products_ref in enumerate(products + late_products):
+        if tile < 0:
+            at = dot_gains(gains, look_up_ref, share)
+        else:
+            at = end_gains(gains, ends[tile], share, blocks)
+        total = total + station_sums(*gain_terms(at, products_ref), tables[tile])
     divisor = total[2 * rows :] + damping
     renewed = (total[: 2 * rows] + damping * gains) / jnp.concatenate([divisor, divisor])
     solved_ref[...] = 0.5 * (renewed + gains)
@@ -393,18 +425,6 @@
         start = pl.multiple_of((here ^ step) * share, share)
         for part in range(4):
             solved_ref[part, pl.ds(start, share), :] = piece[part * share : (part + 1) * share, :]
-
-
-def fit_kernel(basis_ref, *refs):
-    total = refs[0][...]
-    for part in refs[1:-1]:
-        total = total + part[...]
-    fitted_ref = refs[-1]
-    for part in range(4):
-        fitted_ref[part] = sum(
-            basis_ref[:, degree : degree + 1] * total[4 * degree + part : 4 * degree + part + 1, :]
-            for degree in range(4)
-        )
 
 
 def vmem_call(kernel, outs, scratch=(), spaces=None, **options):
@@ -492,10 +512,13 @@
     table_dims = (STATION_COUNT // LANES, 2 * slots, LANES)
     table_shape = shape(table_dims, bf16)
     sums_shape = shape((6 * share, STATION_COUNT), f32)
+    look_up_shape = shape((2 * blocks, STATION_COUNT, LANES), bf16)
     tile_outs = (products_shape, table_shape, sums_shape)
     late = [steps[-1]]
     done = {
-        step: vmem_call(tile_kernel, tile_outs)(chunks[step], ends[step])
+        step: vmem_call(tile_kernel, tile_outs + ((look_up_shape,) if step == 0 else ()))(
+            chunks[step], ends[step]
+        )
         for step in range(tiles)
         if step not in late
     }
@@ -504,7 +527,6 @@
         tuple(shape((4 * share, owned), f32) for _ in range(tiles)),
         scratch=[
             *[pltpu.VMEM((12, share, slots), f32) for _ in late],
-            *[pltpu.VMEM(table_dims, bf16) for _ in late],
             pltpu.VMEM((4 * share, STATION_COUNT), f32),
         ],
     )(
@@ -513,6 +535,7 @@
         *[parts[0] for parts in done.values()],
         *[parts[1] for parts in done.values()],
         *[parts[2] for parts in done.values()],
+        done[0][3],
     )
     received = {0: pieces[0]}
     for step in steps:
@@ -529,7 +552,8 @@
     moment_parts = [moments]
     for step in range(1, groups):
         moment_parts.append(lax.ppermute(moments, "ch", partners(groups, step)))
-    fitted = vmem_call(fit_kernel, shape((4, channel_local, owned), f32))(basis, *moment_parts)
+    total = sum(moment_parts).reshape(4, 4, owned)
+    fitted = sum(basis[None, :, k, None] * total[k][:, None, :] for k in range(4))
     out_shape = (2, 2, channel_local, owned)
     return solved.reshape(out_shape), fitted.reshape(out_shape)
 

time: 37 us -> 36.7 us (level)
  Pallas kernels: 7.28 us -> 6.47 us
  other arithmetic: 0 us -> 0.72 us
  local copies, waits for them, and re-layouts: 0.72 us -> 0.24 us
  waiting for transfers between devices: 12.3 us -> 12.7 us
    pallas_call x9 -> x8, Pallas kernels: 7.28 us -> 6.47 us  [call(): pl.pallas_call(kernel, out_shape=outs, in_specs=[pl.BlockSpec(memory_spac...]
    add x0 -> x2, other arithmetic: none -> 0.72 us  [the longest x1 0.72 us: local_resplit(): sum((basis[None, :, k, None] * total[k][:, None, :] for k in range(4)))]
    dynamic_slice x1, local copies, waits for them, and re-layouts: 0.72 us -> 0.01 us  [local_resplit(): lax.dynamic_slice_in_dim(jnp.asarray(poly_basis(channel_local * groups).T...]
    ppermute x3, waiting for transfers between devices: 3.64 us -> 4.34 us  [local_resplit(): received[step] = lax.ppermute(pieces[step], 'bl', partners(tiles, step))]
  transfers between devices with their start and end apart: 10 -> 10, of which waited for: 4 -> 5; matrix products, arithmetic and copies ran while one was open for 2% -> 1% of each run, Pallas kernels for 9% -> 9%
where the time goes in v7:
time: 36.7 us; the launch traced here: 36.5 us
  starting transfers between devices  14.9 us (41%)
  waiting for transfers between devices  12.7 us (35%)
  Pallas kernels  6.47 us (18%)
  between operations  1.39 us (4%)
  other arithmetic  0.72 us (2%)
    ppermute x4, starting transfers between devices, exchange(): return lax.ppermute(piece, 'bl', partners(tiles, step))  8.58 us
    ppermute x4, waiting for transfers between devices, exchange(): return lax.ppermute(piece, 'bl', partners(tiles, step))  7.35 us
    pallas_call x8, Pallas kernels, call(): pl.pallas_call(kernel, out_shape=outs, in_specs=[pl.BlockSpec(memory_spac...  6.47 us
    ppermute x3, starting transfers between devices, local_resplit(): received[step] = lax.ppermute(pieces[step], 'bl', partners(tiles, step))  4.44 us
    ppermute x3, waiting for transfers between devices, local_resplit(): received[step] = lax.ppermute(pieces[step], 'bl', partners(tiles, step))  4.34 us
    ppermute x3, starting transfers between devices, local_resplit(): moment_parts.append(lax.ppermute(moments, 'ch', partners(groups, step)))  1.92 us
    ppermute x3, waiting for transfers between devices, local_resplit(): moment_parts.append(lax.ppermute(moments, 'ch', partners(groups, step)))  1 us
  transfers between devices with their start and end apart: 10, of which 5 were waited for; matrix products, arithmetic and copies ran while one was open for 1% of the time, Pallas kernels for 9%

profile of v7, /device:TPU:0, one launch (start us, length us, event | category | flops | bytes accessed | tf_op | source)
XLA Modules:
  0.0 36.5 jit_solution(12429939502556555273)
XLA Ops:
  1.3 1.2 %shard_map.78 = (bf16[65,8,128]{2,1,0:T(8,128)(2,1)S(1)}, bf16[65,8,128]{2,1,0:T(8,128)(2,1)S(1)}, bf16[65,8,128]{2,1,0:T(8,128)(2,1)S(1)}, bf16[1,8,128]{2,1,0:T(8,128)(2,1)S(1)}) custom-call(s32[1]{0:T(128)S(6)} %copy.8.counts_ref, bf16[8,32,512]{2,1,0:T(8,128)(2,1)} %vis_hbm.3, bf16[8,32,512]{2,1,0:T(8,128)(2,1)} %sky_hbm.3, s32[32,512]{1,0:T(8,128)} %mask_hbm.3, ...), custom_call_target="tpu_custom_call" | custom-call | tf_op jit(solution)/shard_map/pallas_call | solution.py:432
  2.5 3.1 %collective-permute-start.1 = (bf16[65,8,128]{2,1,0:T(8,128)(2,1)S(1)}, bf16[65,8,128]{2,1,0:T(8,128)(2,1)S(1)}, u32[]{:S(2)}, u32[]{:S(2)}) collective-permute-start(bf16[65,8,128]{2,1,0:T(8,128)(2,1)S(1)} %get-tuple-element.25), channel_id=1, source_target_pairs={{0,4},{4,0},{8,12},{12,8},{1,5},{5,1},{9,13},{13,9},{2,6},{6,2},{1... | collective-permute-start | bytes 399368 | tf_op jit(solution)/shard_map/ppermute | solution.py:503
  5.6 2.5 %collective-permute-start = (bf16[65,8,128]{2,1,0:T(8,128)(2,1)S(1)}, bf16[65,8,128]{2,1,0:T(8,128)(2,1)S(1)}, u32[]{:S(2)}, u32[]{:S(2)}) collective-permute-start(bf16[65,8,128]{2,1,0:T(8,128)(2,1)S(1)} %get-tuple-element.23), channel_id=1, source_target_pairs={{0,12},{4,8},{8,4},{12,0},{1,13},{5,9},{9,5},{13,1},{2,14},{6,10},... | collective-permute-start | bytes 399368 | tf_op jit(solution)/shard_map/ppermute | solution.py:503
  8.1 0.9 %shard_map.77 = bf16[64,8,128]{2,1,0:T(8,128)(2,1)S(1)} custom-call(bf16[8,32,512]{2,1,0:T(8,128)(2,1)} %vis_hbm.3, bf16[8,32,512]{2,1,0:T(8,128)(2,1)} %sky_hbm.3, s32[32,512]{1,0:T(8,128)} %mask_hbm.3), custom_call_target="tpu_custom_call" | custom-call | tf_op jit(solution)/shard_map/pallas_call | solution.py:432
  9.1 0.2 collective-permute-start.3
  9.2 2.8 %collective-permute-start.2 = (bf16[1,8,128]{2,1,0:T(8,128)(2,1)S(1)}, bf16[1,8,128]{2,1,0:T(8,128)(2,1)S(1)}, u32[]{:S(2)}, u32[]{:S(2)}) collective-permute-start(bf16[1,8,128]{2,1,0:T(8,128)(2,1)S(1)} %get-tuple-element.26), channel_id=1, source_target_pairs={{0,8},{4,12},{8,0},{12,4},{1,9},{5,13},{9,1},{13,5},{2,10},{6,14},... | collective-permute-start | bytes 6152 | tf_op jit(solution)/shard_map/ppermute | solution.py:503
  12.0 0.7 %shard_map.79 = (f32[12,8,512]{2,1,0:T(8,128)S(1)}, bf16[4,1024,128]{2,1,0:T(8,128)(2,1)S(1)}, f32[48,512]{1,0:T(8,128)S(1)}, bf16[8,512,128]{2,1,0:T(8,128)(2,1)S(1)}) custom-call(bf16[65,8,128]{2,1,0:T(8,128)(2,1)S(1)} %get-tuple-element.24.chunk_ref.ends_ref.refs_1_, bf16[65,8,128]{2,1,0:T(8,128)(2,1)S(1)} %get-tuple-element.24.chunk_ref.ends_ref.refs_1_), custom_call_target="tpu_custom_call" | custom-call | tf_op jit(solution)/shard_map/pallas_call | solution.py:432
  12.7 7.3 %collective-permute-done.2.ends_ref.refs_3_ = bf16[1,8,128]{2,1,0:T(8,128)(2,1)S(1)} collective-permute-done((bf16[1,8,128]{2,1,0:T(8,128)(2,1)S(1)}, bf16[1,8,128]{2,1,0:T(8,128)(2,1)S(1)}, u32[]{:S(2)}, u32[]{:S(2)}) %collective-permute-start.2) | collective-permute-done | bytes 2080 | tf_op jit(solution)/shard_map/ppermute | solution.py:503
  20.1 0.0 collective-permute-done.3.chunk_ref
  20.1 0.6 %shard_map.81 = (f32[12,8,512]{2,1,0:T(8,128)S(1)}, bf16[4,1024,128]{2,1,0:T(8,128)(2,1)S(1)}, f32[48,512]{1,0:T(8,128)S(1)}) custom-call(bf16[64,8,128]{2,1,0:T(8,128)(2,1)S(1)} %collective-permute-done.3.chunk_ref, bf16[1,8,128]{2,1,0:T(8,128)(2,1)S(1)} %collective-permute-done.2.ends_ref.refs_3_), custom_call_target="tpu_custom_call" | custom-call | tf_op jit(solution)/shard_map/pallas_call | solution.py:432
  20.7 0.0 collective-permute-done.1.chunk_ref.ends_ref.refs_2_
  20.7 0.6 %shard_map.80 = (f32[12,8,512]{2,1,0:T(8,128)S(1)}, bf16[4,1024,128]{2,1,0:T(8,128)(2,1)S(1)}, f32[48,512]{1,0:T(8,128)S(1)}) custom-call(bf16[65,8,128]{2,1,0:T(8,128)(2,1)S(1)} %collective-permute-done.1.chunk_ref.ends_ref.refs_2_, bf16[65,8,128]{2,1,0:T(8,128)(2,1)S(1)} %collective-permute-done.1.chunk_ref.ends_ref.refs_2_), custom_call_target="tpu_custom_call" | custom-call | tf_op jit(solution)/shard_map/pallas_call | solution.py:432
  21.3 0.0 collective-permute-done.refs_0_.refs_4_
  21.3 0.0 copy-start
  21.3 1.7 %shard_map.82 = (f32[32,128]{1,0:T(8,128)S(1)}, f32[32,128]{1,0:T(8,128)S(1)}, f32[32,128]{1,0:T(8,128)S(1)}, f32[32,128]{1,0:T(8,128)S(1)}) custom-call(bf16[65,8,128]{2,1,0:T(8,128)(2,1)S(1)} %collective-permute-done.refs_0_.refs_4_, bf16[65,8,128]{2,1,0:T(8,128)(2,1)S(1)} %get-tuple-element.24.chunk_ref.ends_ref.refs_1_, ...), custom_call_target="tpu_custom_call" | custom-call | tf_op jit(solution)/shard_map/pallas_call | solution.py:432
  23.0 0.1 collective-permute-start.4
  23.1 3.2 %collective-permute-start.5 = (f32[32,128]{1,0:T(8,128)S(1)}, f32[32,128]{1,0:T(8,128)S(1)}, u32[]{:S(2)}, u32[]{:S(2)}) collective-permute-start(f32[32,128]{1,0:T(8,128)S(1)} %get-tuple-element.40), channel_id=1, source_target_pairs={{0,8},{4,12},{8,0},{12,4},{1,9},{5,13},{9,1},{13,5},{2,10},{6,14},... | collective-permute-start | bytes 49160 | tf_op jit(solution)/shard_map/ppermute | solution.py:542
  26.3 1.2 %collective-permute-start.6 = (f32[32,128]{1,0:T(8,128)S(1)}, f32[32,128]{1,0:T(8,128)S(1)}, u32[]{:S(2)}, u32[]{:S(2)}) collective-permute-start(f32[32,128]{1,0:T(8,128)S(1)} %get-tuple-element.41), channel_id=1, source_target_pairs={{0,12},{4,8},{8,4},{12,0},{1,13},{5,9},{9,5},{13,1},{2,14},{6,10},... | collective-permute-start | bytes 49160 | tf_op jit(solution)/shard_map/ppermute | solution.py:542
  27.5 0.0 copy-done
  27.5 0.0 collective-permute-done.4.refs_1_
  27.5 0.5 %collective-permute-done.5.refs_2_ = f32[32,128]{1,0:T(8,128)S(1)} collective-permute-done((f32[32,128]{1,0:T(8,128)S(1)}, f32[32,128]{1,0:T(8,128)S(1)}, u32[]{:S(2)}, u32[]{:S(2)}) %collective-permute-start.5) | collective-permute-done | bytes 16416 | tf_op jit(solution)/shard_map/ppermute | solution.py:542
  28.0 3.8 %collective-permute-done.6.refs_3_ = f32[32,128]{1,0:T(8,128)S(1)} collective-permute-done((f32[32,128]{1,0:T(8,128)S(1)}, f32[32,128]{1,0:T(8,128)S(1)}, u32[]{:S(2)}, u32[]{:S(2)}) %collective-permute-start.6) | collective-permute-done | bytes 16416 | tf_op jit(solution)/shard_map/ppermute | solution.py:542
  31.8 0.1 shard_map.84
  31.9 0.1 collective-permute-start.9
  32.0 1.6 %collective-permute-start.8 = (f32[16,128]{1,0:T(8,128)S(1)}, f32[16,128]{1,0:T(8,128)S(1)}, u32[]{:S(2)}, u32[]{:S(2)}) collective-permute-start(f32[16,128]{1,0:T(8,128)S(1)} %shard_map.84), channel_id=1, source_target_pairs={{0,2},{1,3},{2,0},{3,1},{4,6},{5,7},{6,4},{7,5},{8,10},{9,11},{10,... | collective-permute-start | bytes 24584 | tf_op jit(solution)/shard_map/ppermute | solution.py:554
  33.6 0.3 collective-permute-start.7
  33.9 0.2 dynamic-slice_reduce_fusion.3
  34.1 0.6 %shard_map.83 = f32[4,32,128]{2,1,0:T(8,128)} custom-call(f32[32,128]{1,0:T(8,128)S(1)} %get-tuple-element.38.refs_0_, f32[32,128]{1,0:T(8,128)S(1)} %collective-permute-done.4.refs_1_, f32[32,128]{1,0:T(8,128)S(1)} %collective-permute-done.5.refs_2_, f32[32,128]{1,0:T(8,128)S(1)} %collective-permute-done.6.refs_3_), custom_call_target="tpu_custom_call" | custom-call | tf_op jit(solution)/shard_map/pallas_call | solution.py:432
  34.7 0.4 %collective-permute-done.9 = f32[16,128]{1,0:T(8,128)S(1)} collective-permute-done((f32[16,128]{1,0:T(8,128)S(1)}, f32[16,128]{1,0:T(8,128)S(1)}, u32[]{:S(2)}, u32[]{:S(2)}) %collective-permute-start.9) | collective-permute-done | bytes 8224 | tf_op jit(solution)/shard_map/ppermute | solution.py:554
  35.1 0.6 %collective-permute-done.8 = f32[16,128]{1,0:T(8,128)S(1)} collective-permute-done((f32[16,128]{1,0:T(8,128)S(1)}, f32[16,128]{1,0:T(8,128)S(1)}, u32[]{:S(2)}, u32[]{:S(2)}) %collective-permute-start.8) | collective-permute-done | bytes 8224 | tf_op jit(solution)/shard_map/ppermute | solution.py:554
  35.7 0.0 collective-permute-done.7
  35.7 0.7 %multiply_add_fusion = f32[2,2,32,128]{3,2,1,0:T(8,128)} fusion(f32[2,2,128]{2,1,0:T(2,128)S(1)} %bitcast.7, f32[32]{0:T(128)S(1)} %get-tuple-element.43, f32[2,2,128]{2,1,0:T(2,128)S(1)} %bitcast.8, f32[32]{0:T(128)S(1)} %get-tuple-element.44, f32[2,2,128]{2,1,0:T(2,128)S(1)} %bitcast.9, f32[32]{0:T(128)S(1)} %get-tuple-element.45, ...), kind=kLoop, calls=%fused_computation | loop fusion | flops 114688 | bytes 74240 | tf_op jit(solution)/shard_map/add | solution.py:556
  (3 shorter events, 0.0 us)
Async XLA Ops:
  2.5 18.1 %collective-permute-start.1 = (bf16[65,8,128]{2,1,0:T(8,128)(2,1)S(1)}, bf16[65,8,128]{2,1,0:T(8,128)(2,1)S(1)}, u32[]{:S(2)}, u32[]{:S(2)}) collective-permute-start(bf16[65,8,128]{2,1,0:T(8,128)(2,1)S(1)} %get-tuple-element.25), channel_id=1, source_target_pairs={{0,4},{4,0},{8,12},{12,8},{1,5},{5,1},{9,13},{13,9},{2,6},{6,2},{1... | collective-permute-start | bytes 399368 | tf_op jit(solution)/shard_map/ppermute | solution.py:503
  5.6 15.6 %collective-permute-start = (bf16[65,8,128]{2,1,0:T(8,128)(2,1)S(1)}, bf16[65,8,128]{2,1,0:T(8,128)(2,1)S(1)}, u32[]{:S(2)}, u32[]{:S(2)}) collective-permute-start(bf16[65,8,128]{2,1,0:T(8,128)(2,1)S(1)} %get-tuple-element.23), channel_id=1, source_target_pairs={{0,12},{4,8},{8,4},{12,0},{1,13},{5,9},{9,5},{13,1},{2,14},{6,10},... | collective-permute-start | bytes 399368 | tf_op jit(solution)/shard_map/ppermute | solution.py:503
  9.1 11.0 %collective-permute-start.3 = (bf16[64,8,128]{2,1,0:T(8,128)(2,1)S(1)}, bf16[64,8,128]{2,1,0:T(8,128)(2,1)S(1)}, u32[]{:S(2)}, u32[]{:S(2)}) collective-permute-start(bf16[64,8,128]{2,1,0:T(8,128)(2,1)S(1)} %shard_map.77), channel_id=1, source_target_pairs={{0,8},{4,12},{8,0},{12,4},{1,9},{5,13},{9,1},{13,5},{2,10},{6,14},... | collective-permute-start | bytes 393224 | tf_op jit(solution)/shard_map/ppermute | solution.py:503
  9.2 10.8 %collective-permute-start.2 = (bf16[1,8,128]{2,1,0:T(8,128)(2,1)S(1)}, bf16[1,8,128]{2,1,0:T(8,128)(2,1)S(1)}, u32[]{:S(2)}, u32[]{:S(2)}) collective-permute-start(bf16[1,8,128]{2,1,0:T(8,128)(2,1)S(1)} %get-tuple-element.26), channel_id=1, source_target_pairs={{0,8},{4,12},{8,0},{12,4},{1,9},{5,13},{9,1},{13,5},{2,10},{6,14},... | collective-permute-start | bytes 6152 | tf_op jit(solution)/shard_map/ppermute | solution.py:503
  21.3 6.2 %copy-start = (f32[128,4]{1,0:T(8,128)S(1)}, f32[128,4]{1,0:T(8,128)}, u32[]{:S(2)}) copy-start(f32[128,4]{1,0:T(8,128)} %constant.12.clone) | copy-start | bytes 6148
  23.0 4.5 %collective-permute-start.4 = (f32[32,128]{1,0:T(8,128)S(1)}, f32[32,128]{1,0:T(8,128)S(1)}, u32[]{:S(2)}, u32[]{:S(2)}) collective-permute-start(f32[32,128]{1,0:T(8,128)S(1)} %get-tuple-element.39), channel_id=1, source_target_pairs={{0,4},{4,0},{8,12},{12,8},{1,5},{5,1},{9,13},{13,9},{2,6},{6,2},{1... | collective-permute-start | bytes 49160 | tf_op jit(solution)/shard_map/ppermute | solution.py:542
  23.1 4.9 %collective-permute-start.5 = (f32[32,128]{1,0:T(8,128)S(1)}, f32[32,128]{1,0:T(8,128)S(1)}, u32[]{:S(2)}, u32[]{:S(2)}) collective-permute-start(f32[32,128]{1,0:T(8,128)S(1)} %get-tuple-element.40), channel_id=1, source_target_pairs={{0,8},{4,12},{8,0},{12,4},{1,9},{5,13},{9,1},{13,5},{2,10},{6,14},... | collective-permute-start | bytes 49160 | tf_op jit(solution)/shard_map/ppermute | solution.py:542
  26.3 5.5 %collective-permute-start.6 = (f32[32,128]{1,0:T(8,128)S(1)}, f32[32,128]{1,0:T(8,128)S(1)}, u32[]{:S(2)}, u32[]{:S(2)}) collective-permute-start(f32[32,128]{1,0:T(8,128)S(1)} %get-tuple-element.41), channel_id=1, source_target_pairs={{0,12},{4,8},{8,4},{12,0},{1,13},{5,9},{9,5},{13,1},{2,14},{6,10},... | collective-permute-start | bytes 49160 | tf_op jit(solution)/shard_map/ppermute | solution.py:542
  31.9 3.2 %collective-permute-start.9 = (f32[16,128]{1,0:T(8,128)S(1)}, f32[16,128]{1,0:T(8,128)S(1)}, u32[]{:S(2)}, u32[]{:S(2)}) collective-permute-start(f32[16,128]{1,0:T(8,128)S(1)} %shard_map.84), channel_id=1, source_target_pairs={{0,3},{1,2},{2,1},{3,0},{4,7},{5,6},{6,5},{7,4},{8,11},{9,10},{10,... | collective-permute-start | bytes 24584 | tf_op jit(solution)/shard_map/ppermute | solution.py:554
  32.0 3.7 %collective-permute-start.8 = (f32[16,128]{1,0:T(8,128)S(1)}, f32[16,128]{1,0:T(8,128)S(1)}, u32[]{:S(2)}, u32[]{:S(2)}) collective-permute-start(f32[16,128]{1,0:T(8,128)S(1)} %shard_map.84), channel_id=1, source_target_pairs={{0,2},{1,3},{2,0},{3,1},{4,6},{5,7},{6,4},{7,5},{8,10},{9,11},{10,... | collective-permute-start | bytes 24584 | tf_op jit(solution)/shard_map/ppermute | solution.py:554
  33.6 2.2 %collective-permute-start.7 = (f32[16,128]{1,0:T(8,128)S(1)}, f32[16,128]{1,0:T(8,128)S(1)}, u32[]{:S(2)}, u32[]{:S(2)}) collective-permute-start(f32[16,128]{1,0:T(8,128)S(1)} %shard_map.84), channel_id=1, source_target_pairs={{0,1},{1,0},{2,3},{3,2},{4,5},{5,4},{6,7},{7,6},{8,9},{9,8},{10,11... | collective-permute-start | bytes 24584 | tf_op jit(solution)/shard_map/ppermute | solution.py:554

commit v8 on v7

--- a/solution.py
+++ b/solution.py
@@ -129,10 +129,16 @@
 INDEX_SHIFT = 256.0
 
 
+def partner_step(slot, column, table):
+    even, odd = table
+    return even[slot] + (column % 2) * (odd[slot] - even[slot])
+
+
 def chunk_copies(step, vis_hbm, sky_hbm, mask_hbm, out, sky, mask, sems):
     share, slots = mask.shape
     blocks = slots // LANES
-    channels = pl.ds(pl.multiple_of((lax.axis_index("bl") ^ step) * share, share), share)
+    partner = lax.axis_index("bl") ^ partner_step(step, lax.axis_index("ch"), RAW_STEPS)
+    channels = pl.ds(pl.multiple_of(partner * share, share), share)
     copies = [
         pltpu.make_async_copy(mask_hbm.at[channels], mask, sems.at[0]),
         pltpu.make_async_copy(sky_hbm.at[:, channels], sky, sems.at[1]),
@@ -395,7 +401,7 @@
     owned = STATION_COUNT // tiles
     here = lax.axis_index("bl")
     for step in range(tiles):
-        start = pl.multiple_of((here ^ step) * owned, owned)
+        start = pl.multiple_of(((here + tiles - step) % tiles) * owned, owned)
         outs[step][...] = solved_ref[:, pl.ds(start, owned)]
 
 
@@ -405,7 +411,7 @@
     here = lax.axis_index("bl")
     columns = []
     for step in range(len(pieces)):
-        start = pl.multiple_of((here ^ step) * share, share)
+        start = pl.multiple_of(((here + step) % len(pieces)) * share, share)
         columns.append(basis_ref[pl.ds(start, share), :])
     for degree in range(4):
         for part in range(4):
@@ -422,7 +428,7 @@
     share = pieces[0].shape[0] // 4
     here = lax.axis_index("bl")
     for step, piece in enumerate(pieces):
-        start = pl.multiple_of((here ^ step) * share, share)
+        start = pl.multiple_of(((here + step) % len(pieces)) * share, share)
         for part in range(4):
             solved_ref[part, pl.ds(start, share), :] = piece[part * share : (part + 1) * share, :]
 
@@ -446,6 +452,14 @@
 
 def in_hbm(value):
     return pltpu.with_memory_space_constraint(value, pltpu.HBM)
+
+
+def mesh_partners(tiles, groups, step, table):
+    return [
+        (row * groups + column, (row ^ partner_step(step, column, table)) * groups + column)
+        for row in range(tiles)
+        for column in range(groups)
+    ]
 
 
 def partners(count, step):
@@ -500,7 +514,7 @@
     )
 
     def exchange(piece, step):
-        return lax.ppermute(piece, "bl", partners(tiles, step))
+        return lax.ppermute(piece, ("bl", "ch"), mesh_partners(tiles, groups, step, RAW_STEPS))
 
     chunks = {0: packed[-1], first: exchange(lead, first)}
     for piece, step in zip(packed[:-1], others):
@@ -539,7 +553,9 @@
     )
     received = {0: pieces[0]}
     for step in steps:
-        received[step] = lax.ppermute(pieces[step], "bl", partners(tiles, step))
+        received[step] = lax.ppermute(
+            pieces[step], "bl", [(row, (row - step) % tiles) for row in range(tiles)]
+        )
     received = [received[step] for step in range(tiles)]
     basis = lax.dynamic_slice_in_dim(
         jnp.asarray(poly_basis(channel_local * groups).T),
@@ -559,17 +575,15 @@
 
 
 FIRST = 2
+RAW_STEPS = ((0, 1, 2, 3), (0, 1, 3, 2))
 
 
 def local(visibilities, sky_model, antenna_pairs, tile_counts, usable_mask):
     tiles = lax.axis_size("bl")
     groups = lax.axis_size("ch")
-    power_of_two = lambda count: count & (count - 1) == 0
     resplit = (
-        power_of_two(tiles)
-        and power_of_two(groups)
-        and 1 < tiles <= 4
-        and groups <= 8
+        tiles == 4
+        and groups == 4
         and visibilities.shape[1] == 8 * tiles
         and STATION_COUNT % (128 * tiles) == 0
         and STATION_COUNT <= 2 * INDEX_SHIFT

time: 36.7 us -> 36.1 us (0.984)
  starting transfers between devices: 14.9 us -> 13.7 us
  waiting for transfers between devices: 12.7 us -> 13.3 us
    ppermute x7, starting transfers between devices: 13 us -> 11.7 us  [the longest x4 8.58 us: exchange(): lax.ppermute(piece, ('bl', 'ch'), mesh_partners(tiles, groups, step, RAW_...]
    ppermute x7, waiting for transfers between devices: 11.7 us -> 12.3 us  [the longest x4 7.46 us: exchange(): lax.ppermute(piece, ('bl', 'ch'), mesh_partners(tiles, groups, step, RAW_...]
  transfers between devices with their start and end apart: 10 -> 10, of which waited for: 5 -> 6; matrix products, arithmetic and copies ran while one was open for 1% -> 1% of each run, Pallas kernels for 9% -> 10%
where the time goes in v8:
time: 36.1 us; the launch traced here: 35.8 us
  starting transfers between devices  13.7 us (38%)
  waiting for transfers between devices  13.3 us (37%)
  Pallas kernels  6.48 us (18%)
  between operations  1.38 us (4%)
  other arithmetic  0.72 us (2%)
    ppermute x4, starting transfers between devices, exchange(): lax.ppermute(piece, ('bl', 'ch'), mesh_partners(tiles, groups, step, RAW_...  8.58 us
    ppermute x4, waiting for transfers between devices, exchange(): lax.ppermute(piece, ('bl', 'ch'), mesh_partners(tiles, groups, step, RAW_...  7.46 us
    pallas_call x8, Pallas kernels, call(): pl.pallas_call(kernel, out_shape=outs, in_specs=[pl.BlockSpec(memory_spac...  6.48 us
    ppermute x3, waiting for transfers between devices, local_resplit(): lax.ppermute(pieces[step], 'bl', [(row, (row - step) % tiles) for row in...  4.89 us
    ppermute x3, starting transfers between devices, local_resplit(): lax.ppermute(pieces[step], 'bl', [(row, (row - step) % tiles) for row in...  3.16 us
    ppermute x3, starting transfers between devices, local_resplit(): moment_parts.append(lax.ppermute(moments, 'ch', partners(groups, step)))  1.92 us
    ppermute x3, waiting for transfers between devices, local_resplit(): moment_parts.append(lax.ppermute(moments, 'ch', partners(groups, step)))  0.99 us
  transfers between devices with their start and end apart: 10, of which 6 were waited for; matrix products, arithmetic and copies ran while one was open for 1% of the time, Pallas kernels for 10%

profile of v8, /device:TPU:0, one launch (start us, length us, event | category | flops | bytes accessed | tf_op | source)
XLA Modules:
  0.0 35.8 jit_solution(13038576394211379489)
XLA Ops:
  1.3 1.2 %shard_map.78 = (bf16[65,8,128]{2,1,0:T(8,128)(2,1)S(1)}, bf16[65,8,128]{2,1,0:T(8,128)(2,1)S(1)}, bf16[65,8,128]{2,1,0:T(8,128)(2,1)S(1)}, bf16[1,8,128]{2,1,0:T(8,128)(2,1)S(1)}) custom-call(s32[1]{0:T(128)S(6)} %copy.8.counts_ref, bf16[8,32,512]{2,1,0:T(8,128)(2,1)} %vis_hbm.3, bf16[8,32,512]{2,1,0:T(8,128)(2,1)} %sky_hbm.3, s32[32,512]{1,0:T(8,128)} %mask_hbm.3, ...), custom_call_target="tpu_custom_call" | custom-call | tf_op jit(solution)/shard_map/pallas_call | solution.py:438
  2.5 3.1 %collective-permute-start.1 = (bf16[65,8,128]{2,1,0:T(8,128)(2,1)S(1)}, bf16[65,8,128]{2,1,0:T(8,128)(2,1)S(1)}, u32[]{:S(2)}, u32[]{:S(2)}) collective-permute-start(bf16[65,8,128]{2,1,0:T(8,128)(2,1)S(1)} %get-tuple-element.25), channel_id=1, source_target_pairs={{0,4},{1,5},{2,6},{3,7},{4,0},{5,1},{6,2},{7,3},{8,12},{9,13},{10,... | collective-permute-start | bytes 399368 | tf_op jit(solution)/shard_map/ppermute | solution.py:517
  5.6 2.5 %collective-permute-start = (bf16[65,8,128]{2,1,0:T(8,128)(2,1)S(1)}, bf16[65,8,128]{2,1,0:T(8,128)(2,1)S(1)}, u32[]{:S(2)}, u32[]{:S(2)}) collective-permute-start(bf16[65,8,128]{2,1,0:T(8,128)(2,1)S(1)} %get-tuple-element.23), channel_id=1, source_target_pairs={{0,12},{1,9},{2,14},{3,11},{4,8},{5,13},{6,10},{7,15},{8,4},{9,1},... | collective-permute-start | bytes 399368 | tf_op jit(solution)/shard_map/ppermute | solution.py:517
  8.1 0.9 %shard_map.77 = bf16[64,8,128]{2,1,0:T(8,128)(2,1)S(1)} custom-call(bf16[8,32,512]{2,1,0:T(8,128)(2,1)} %vis_hbm.3, bf16[8,32,512]{2,1,0:T(8,128)(2,1)} %sky_hbm.3, s32[32,512]{1,0:T(8,128)} %mask_hbm.3), custom_call_target="tpu_custom_call" | custom-call | tf_op jit(solution)/shard_map/pallas_call | solution.py:438
  9.1 0.2 collective-permute-start.3
  9.2 2.8 %collective-permute-start.2 = (bf16[1,8,128]{2,1,0:T(8,128)(2,1)S(1)}, bf16[1,8,128]{2,1,0:T(8,128)(2,1)S(1)}, u32[]{:S(2)}, u32[]{:S(2)}) collective-permute-start(bf16[1,8,128]{2,1,0:T(8,128)(2,1)S(1)} %get-tuple-element.26), channel_id=1, source_target_pairs={{0,8},{1,13},{2,10},{3,15},{4,12},{5,9},{6,14},{7,11},{8,0},{9,5},... | collective-permute-start | bytes 6152 | tf_op jit(solution)/shard_map/ppermute | solution.py:517
  12.0 0.7 %shard_map.79 = (f32[12,8,512]{2,1,0:T(8,128)S(1)}, bf16[4,1024,128]{2,1,0:T(8,128)(2,1)S(1)}, f32[48,512]{1,0:T(8,128)S(1)}, bf16[8,512,128]{2,1,0:T(8,128)(2,1)S(1)}) custom-call(bf16[65,8,128]{2,1,0:T(8,128)(2,1)S(1)} %get-tuple-element.24.chunk_ref.ends_ref.refs_1_, bf16[65,8,128]{2,1,0:T(8,128)(2,1)S(1)} %get-tuple-element.24.chunk_ref.ends_ref.refs_1_), custom_call_target="tpu_custom_call" | custom-call | tf_op jit(solution)/shard_map/pallas_call | solution.py:438
  12.7 7.4 %collective-permute-done.2.ends_ref.refs_3_ = bf16[1,8,128]{2,1,0:T(8,128)(2,1)S(1)} collective-permute-done((bf16[1,8,128]{2,1,0:T(8,128)(2,1)S(1)}, bf16[1,8,128]{2,1,0:T(8,128)(2,1)S(1)}, u32[]{:S(2)}, u32[]{:S(2)}) %collective-permute-start.2) | collective-permute-done | bytes 2080 | tf_op jit(solution)/shard_map/ppermute | solution.py:517
  20.2 0.0 collective-permute-done.3.chunk_ref
  20.2 0.6 %shard_map.81 = (f32[12,8,512]{2,1,0:T(8,128)S(1)}, bf16[4,1024,128]{2,1,0:T(8,128)(2,1)S(1)}, f32[48,512]{1,0:T(8,128)S(1)}) custom-call(bf16[64,8,128]{2,1,0:T(8,128)(2,1)S(1)} %collective-permute-done.3.chunk_ref, bf16[1,8,128]{2,1,0:T(8,128)(2,1)S(1)} %collective-permute-done.2.ends_ref.refs_3_), custom_call_target="tpu_custom_call" | custom-call | tf_op jit(solution)/shard_map/pallas_call | solution.py:438
  20.8 0.0 collective-permute-done.1.chunk_ref.ends_ref.refs_2_
  20.8 0.6 %shard_map.80 = (f32[12,8,512]{2,1,0:T(8,128)S(1)}, bf16[4,1024,128]{2,1,0:T(8,128)(2,1)S(1)}, f32[48,512]{1,0:T(8,128)S(1)}) custom-call(bf16[65,8,128]{2,1,0:T(8,128)(2,1)S(1)} %collective-permute-done.1.chunk_ref.ends_ref.refs_2_, bf16[65,8,128]{2,1,0:T(8,128)(2,1)S(1)} %collective-permute-done.1.chunk_ref.ends_ref.refs_2_), custom_call_target="tpu_custom_call" | custom-call | tf_op jit(solution)/shard_map/pallas_call | solution.py:438
  21.4 0.0 collective-permute-done.refs_0_.refs_4_
  21.4 0.0 copy-start
  21.4 1.7 %shard_map.82 = (f32[32,128]{1,0:T(8,128)S(1)}, f32[32,128]{1,0:T(8,128)S(1)}, f32[32,128]{1,0:T(8,128)S(1)}, f32[32,128]{1,0:T(8,128)S(1)}) custom-call(bf16[65,8,128]{2,1,0:T(8,128)(2,1)S(1)} %collective-permute-done.refs_0_.refs_4_, bf16[65,8,128]{2,1,0:T(8,128)(2,1)S(1)} %get-tuple-element.24.chunk_ref.ends_ref.refs_1_, ...), custom_call_target="tpu_custom_call" | custom-call | tf_op jit(solution)/shard_map/pallas_call | solution.py:438
  23.1 2.5 %collective-permute-start.4 = (f32[32,128]{1,0:T(8,128)S(1)}, f32[32,128]{1,0:T(8,128)S(1)}, u32[]{:S(2)}, u32[]{:S(2)}) collective-permute-start(f32[32,128]{1,0:T(8,128)S(1)} %get-tuple-element.39), channel_id=1, source_target_pairs={{0,12},{4,0},{8,4},{12,8},{1,13},{5,1},{9,5},{13,9},{2,14},{6,2},{... | collective-permute-start | bytes 49160 | tf_op jit(solution)/shard_map/ppermute | solution.py:556
  25.6 0.0 collective-permute-start.5
  25.6 0.6 %collective-permute-start.6 = (f32[32,128]{1,0:T(8,128)S(1)}, f32[32,128]{1,0:T(8,128)S(1)}, u32[]{:S(2)}, u32[]{:S(2)}) collective-permute-start(f32[32,128]{1,0:T(8,128)S(1)} %get-tuple-element.41), channel_id=1, source_target_pairs={{0,4},{4,8},{8,12},{12,0},{1,5},{5,9},{9,13},{13,1},{2,6},{6,10},{... | collective-permute-start | bytes 49160 | tf_op jit(solution)/shard_map/ppermute | solution.py:556
  26.3 0.0 copy-done
  26.3 0.8 %collective-permute-done.4.refs_1_ = f32[32,128]{1,0:T(8,128)S(1)} collective-permute-done((f32[32,128]{1,0:T(8,128)S(1)}, f32[32,128]{1,0:T(8,128)S(1)}, u32[]{:S(2)}, u32[]{:S(2)}) %collective-permute-start.4) | collective-permute-done | bytes 16416 | tf_op jit(solution)/shard_map/ppermute | solution.py:556
  27.1 3.2 %collective-permute-done.5.refs_2_ = f32[32,128]{1,0:T(8,128)S(1)} collective-permute-done((f32[32,128]{1,0:T(8,128)S(1)}, f32[32,128]{1,0:T(8,128)S(1)}, u32[]{:S(2)}, u32[]{:S(2)}) %collective-permute-start.5) | collective-permute-done | bytes 16416 | tf_op jit(solution)/shard_map/ppermute | solution.py:556
  30.3 0.9 %collective-permute-done.6.refs_3_ = f32[32,128]{1,0:T(8,128)S(1)} collective-permute-done((f32[32,128]{1,0:T(8,128)S(1)}, f32[32,128]{1,0:T(8,128)S(1)}, u32[]{:S(2)}, u32[]{:S(2)}) %collective-permute-start.6) | collective-permute-done | bytes 16416 | tf_op jit(solution)/shard_map/ppermute | solution.py:556
  31.2 0.1 shard_map.84
  31.3 0.1 collective-permute-start.9
  31.4 1.6 %collective-permute-start.8 = (f32[16,128]{1,0:T(8,128)S(1)}, f32[16,128]{1,0:T(8,128)S(1)}, u32[]{:S(2)}, u32[]{:S(2)}) collective-permute-start(f32[16,128]{1,0:T(8,128)S(1)} %shard_map.84), channel_id=1, source_target_pairs={{0,2},{1,3},{2,0},{3,1},{4,6},{5,7},{6,4},{7,5},{8,10},{9,11},{10,... | collective-permute-start | bytes 24584 | tf_op jit(solution)/shard_map/ppermute | solution.py:570
  32.9 0.3 collective-permute-start.7
  33.2 0.2 dynamic-slice_reduce_fusion.3
  33.4 0.7 %shard_map.83 = f32[4,32,128]{2,1,0:T(8,128)} custom-call(f32[32,128]{1,0:T(8,128)S(1)} %get-tuple-element.38.refs_0_, f32[32,128]{1,0:T(8,128)S(1)} %collective-permute-done.4.refs_1_, f32[32,128]{1,0:T(8,128)S(1)} %collective-permute-done.5.refs_2_, f32[32,128]{1,0:T(8,128)S(1)} %collective-permute-done.6.refs_3_), custom_call_target="tpu_custom_call" | custom-call | tf_op jit(solution)/shard_map/pallas_call | solution.py:438
  34.1 0.4 %collective-permute-done.9 = f32[16,128]{1,0:T(8,128)S(1)} collective-permute-done((f32[16,128]{1,0:T(8,128)S(1)}, f32[16,128]{1,0:T(8,128)S(1)}, u32[]{:S(2)}, u32[]{:S(2)}) %collective-permute-start.9) | collective-permute-done | bytes 8224 | tf_op jit(solution)/shard_map/ppermute | solution.py:570
  34.5 0.6 %collective-permute-done.8 = f32[16,128]{1,0:T(8,128)S(1)} collective-permute-done((f32[16,128]{1,0:T(8,128)S(1)}, f32[16,128]{1,0:T(8,128)S(1)}, u32[]{:S(2)}, u32[]{:S(2)}) %collective-permute-start.8) | collective-permute-done | bytes 8224 | tf_op jit(solution)/shard_map/ppermute | solution.py:570
  35.1 0.0 collective-permute-done.7
  35.1 0.7 %multiply_add_fusion = f32[2,2,32,128]{3,2,1,0:T(8,128)} fusion(f32[2,2,128]{2,1,0:T(2,128)S(1)} %bitcast.7, f32[32]{0:T(128)S(1)} %get-tuple-element.43, f32[2,2,128]{2,1,0:T(2,128)S(1)} %bitcast.8, f32[32]{0:T(128)S(1)} %get-tuple-element.44, f32[2,2,128]{2,1,0:T(2,128)S(1)} %bitcast.9, f32[32]{0:T(128)S(1)} %get-tuple-element.45, ...), kind=kLoop, calls=%fused_computation | loop fusion | flops 114688 | bytes 74240 | tf_op jit(solution)/shard_map/add | solution.py:572
  (3 shorter events, 0.0 us)
Async XLA Ops:
  2.5 18.2 %collective-permute-start.1 = (bf16[65,8,128]{2,1,0:T(8,128)(2,1)S(1)}, bf16[65,8,128]{2,1,0:T(8,128)(2,1)S(1)}, u32[]{:S(2)}, u32[]{:S(2)}) collective-permute-start(bf16[65,8,128]{2,1,0:T(8,128)(2,1)S(1)} %get-tuple-element.25), channel_id=1, source_target_pairs={{0,4},{1,5},{2,6},{3,7},{4,0},{5,1},{6,2},{7,3},{8,12},{9,13},{10,... | collective-permute-start | bytes 399368 | tf_op jit(solution)/shard_map/ppermute | solution.py:517
  5.6 15.7 %collective-permute-start = (bf16[65,8,128]{2,1,0:T(8,128)(2,1)S(1)}, bf16[65,8,128]{2,1,0:T(8,128)(2,1)S(1)}, u32[]{:S(2)}, u32[]{:S(2)}) collective-permute-start(bf16[65,8,128]{2,1,0:T(8,128)(2,1)S(1)} %get-tuple-element.23), channel_id=1, source_target_pairs={{0,12},{1,9},{2,14},{3,11},{4,8},{5,13},{6,10},{7,15},{8,4},{9,1},... | collective-permute-start | bytes 399368 | tf_op jit(solution)/shard_map/ppermute | solution.py:517
  9.1 11.1 %collective-permute-start.3 = (bf16[64,8,128]{2,1,0:T(8,128)(2,1)S(1)}, bf16[64,8,128]{2,1,0:T(8,128)(2,1)S(1)}, u32[]{:S(2)}, u32[]{:S(2)}) collective-permute-start(bf16[64,8,128]{2,1,0:T(8,128)(2,1)S(1)} %shard_map.77), channel_id=1, source_target_pairs={{0,8},{1,13},{2,10},{3,15},{4,12},{5,9},{6,14},{7,11},{8,0},{9,5},... | collective-permute-start | bytes 393224 | tf_op jit(solution)/shard_map/ppermute | solution.py:517
  9.2 10.9 %collective-permute-start.2 = (bf16[1,8,128]{2,1,0:T(8,128)(2,1)S(1)}, bf16[1,8,128]{2,1,0:T(8,128)(2,1)S(1)}, u32[]{:S(2)}, u32[]{:S(2)}) collective-permute-start(bf16[1,8,128]{2,1,0:T(8,128)(2,1)S(1)} %get-tuple-element.26), channel_id=1, source_target_pairs={{0,8},{1,13},{2,10},{3,15},{4,12},{5,9},{6,14},{7,11},{8,0},{9,5},... | collective-permute-start | bytes 6152 | tf_op jit(solution)/shard_map/ppermute | solution.py:517
  21.4 4.9 %copy-start = (f32[128,4]{1,0:T(8,128)S(1)}, f32[128,4]{1,0:T(8,128)}, u32[]{:S(2)}) copy-start(f32[128,4]{1,0:T(8,128)} %constant.12.clone) | copy-start | bytes 6148
  23.1 4.0 %collective-permute-start.4 = (f32[32,128]{1,0:T(8,128)S(1)}, f32[32,128]{1,0:T(8,128)S(1)}, u32[]{:S(2)}, u32[]{:S(2)}) collective-permute-start(f32[32,128]{1,0:T(8,128)S(1)} %get-tuple-element.39), channel_id=1, source_target_pairs={{0,12},{4,0},{8,4},{12,8},{1,13},{5,1},{9,5},{13,9},{2,14},{6,2},{... | collective-permute-start | bytes 49160 | tf_op jit(solution)/shard_map/ppermute | solution.py:556
  25.6 4.6 %collective-permute-start.5 = (f32[32,128]{1,0:T(8,128)S(1)}, f32[32,128]{1,0:T(8,128)S(1)}, u32[]{:S(2)}, u32[]{:S(2)}) collective-permute-start(f32[32,128]{1,0:T(8,128)S(1)} %get-tuple-element.40), channel_id=1, source_target_pairs={{0,8},{4,12},{8,0},{12,4},{1,9},{5,13},{9,1},{13,5},{2,10},{6,14},... | collective-permute-start | bytes 49160 | tf_op jit(solution)/shard_map/ppermute | solution.py:556
  25.6 5.5 %collective-permute-start.6 = (f32[32,128]{1,0:T(8,128)S(1)}, f32[32,128]{1,0:T(8,128)S(1)}, u32[]{:S(2)}, u32[]{:S(2)}) collective-permute-start(f32[32,128]{1,0:T(8,128)S(1)} %get-tuple-element.41), channel_id=1, source_target_pairs={{0,4},{4,8},{8,12},{12,0},{1,5},{5,9},{9,13},{13,1},{2,6},{6,10},{... | collective-permute-start | bytes 49160 | tf_op jit(solution)/shard_map/ppermute | solution.py:556
  31.3 3.2 %collective-permute-start.9 = (f32[16,128]{1,0:T(8,128)S(1)}, f32[16,128]{1,0:T(8,128)S(1)}, u32[]{:S(2)}, u32[]{:S(2)}) collective-permute-start(f32[16,128]{1,0:T(8,128)S(1)} %shard_map.84), channel_id=1, source_target_pairs={{0,3},{1,2},{2,1},{3,0},{4,7},{5,6},{6,5},{7,4},{8,11},{9,10},{10,... | collective-permute-start | bytes 24584 | tf_op jit(solution)/shard_map/ppermute | solution.py:570
  31.4 3.7 %collective-permute-start.8 = (f32[16,128]{1,0:T(8,128)S(1)}, f32[16,128]{1,0:T(8,128)S(1)}, u32[]{:S(2)}, u32[]{:S(2)}) collective-permute-start(f32[16,128]{1,0:T(8,128)S(1)} %shard_map.84), channel_id=1, source_target_pairs={{0,2},{1,3},{2,0},{3,1},{4,6},{5,7},{6,4},{7,5},{8,10},{9,11},{10,... | collective-permute-start | bytes 24584 | tf_op jit(solution)/shard_map/ppermute | solution.py:570
  32.9 2.2 %collective-permute-start.7 = (f32[16,128]{1,0:T(8,128)S(1)}, f32[16,128]{1,0:T(8,128)S(1)}, u32[]{:S(2)}, u32[]{:S(2)}) collective-permute-start(f32[16,128]{1,0:T(8,128)S(1)} %shard_map.84), channel_id=1, source_target_pairs={{0,1},{1,0},{2,3},{3,2},{4,5},{5,4},{6,7},{7,6},{8,9},{9,8},{10,11... | collective-permute-start | bytes 24584 | tf_op jit(solution)/shard_map/ppermute | solution.py:570

commit v9 on v8

--- a/solution.py
+++ b/solution.py
@@ -401,7 +401,7 @@
     owned = STATION_COUNT // tiles
     here = lax.axis_index("bl")
     for step in range(tiles):
-        start = pl.multiple_of(((here + tiles - step) % tiles) * owned, owned)
+        start = pl.multiple_of((here ^ partner_step(step, lax.axis_index("ch"), BACK_STEPS)) * owned, owned)
         outs[step][...] = solved_ref[:, pl.ds(start, owned)]
 
 
@@ -411,7 +411,7 @@
     here = lax.axis_index("bl")
     columns = []
     for step in range(len(pieces)):
-        start = pl.multiple_of(((here + step) % len(pieces)) * share, share)
+        start = pl.multiple_of((here ^ partner_step(step, lax.axis_index("ch"), BACK_STEPS)) * share, share)
         columns.append(basis_ref[pl.ds(start, share), :])
     for degree in range(4):
         for part in range(4):
@@ -428,7 +428,7 @@
     share = pieces[0].shape[0] // 4
     here = lax.axis_index("bl")
     for step, piece in enumerate(pieces):
-        start = pl.multiple_of(((here + step) % len(pieces)) * share, share)
+        start = pl.multiple_of((here ^ partner_step(step, lax.axis_index("ch"), BACK_STEPS)) * share, share)
         for part in range(4):
             solved_ref[part, pl.ds(start, share), :] = piece[part * share : (part + 1) * share, :]
 
@@ -554,7 +554,7 @@
     received = {0: pieces[0]}
     for step in steps:
         received[step] = lax.ppermute(
-            pieces[step], "bl", [(row, (row - step) % tiles) for row in range(tiles)]
+            pieces[step], ("bl", "ch"), mesh_partners(tiles, groups, step, BACK_STEPS)
         )
     received = [received[step] for step in range(tiles)]
     basis = lax.dynamic_slice_in_dim(
@@ -576,6 +576,7 @@
 
 FIRST = 2
 RAW_STEPS = ((0, 1, 2, 3), (0, 1, 3, 2))
+BACK_STEPS = ((0, 1, 2, 3), (0, 2, 1, 3))
 
 
 def local(visibilities, sky_model, antenna_pairs, tile_counts, usable_mask):

time: 36.1 us -> 36.7 us (1.017)
  starting transfers between devices: 13.7 us -> 14.9 us
  waiting for transfers between devices: 13.3 us -> 12.6 us
    ppermute x3, starting transfers between devices: 3.16 us -> 4.44 us  [local_resplit(): lax.ppermute(pieces[step], ('bl', 'ch'), mesh_partners(tiles, groups, ste...]
    ppermute x3, waiting for transfers between devices: 4.89 us -> 4.17 us  [local_resplit(): lax.ppermute(pieces[step], ('bl', 'ch'), mesh_partners(tiles, groups, ste...]
  transfers between devices with their start and end apart: 10 -> 10, of which waited for: 6 -> 5; matrix products, arithmetic and copies ran while one was open for 1% -> 1% of each run, Pallas kernels for 10% -> 9%
where the time goes in v9:
time: 36.7 us; the launch traced here: 36.4 us
  starting transfers between devices  14.9 us (41%)
  waiting for transfers between devices  12.6 us (34%)
  Pallas kernels  6.48 us (18%)
  between operations  1.39 us (4%)
  other arithmetic  0.72 us (2%)
    ppermute x4, starting transfers between devices, exchange(): lax.ppermute(piece, ('bl', 'ch'), mesh_partners(tiles, groups, step, RAW_...  8.58 us
    ppermute x4, waiting for transfers between devices, exchange(): lax.ppermute(piece, ('bl', 'ch'), mesh_partners(tiles, groups, step, RAW_...  7.46 us
    pallas_call x8, Pallas kernels, call(): pl.pallas_call(kernel, out_shape=outs, in_specs=[pl.BlockSpec(memory_spac...  6.48 us
    ppermute x3, starting transfers between devices, local_resplit(): lax.ppermute(pieces[step], ('bl', 'ch'), mesh_partners(tiles, groups, ste...  4.44 us
    ppermute x3, waiting for transfers between devices, local_resplit(): lax.ppermute(pieces[step], ('bl', 'ch'), mesh_partners(tiles, groups, ste...  4.17 us
    ppermute x3, starting transfers between devices, local_resplit(): moment_parts.append(lax.ppermute(moments, 'ch', partners(groups, step)))  1.92 us
    ppermute x3, waiting for transfers between devices, local_resplit(): moment_parts.append(lax.ppermute(moments, 'ch', partners(groups, step)))  1 us
  transfers between devices with their start and end apart: 10, of which 5 were waited for; matrix products, arithmetic and copies ran while one was open for 1% of the time, Pallas kernels for 9%

profile of v9, /device:TPU:0, one launch (start us, length us, event | category | flops | bytes accessed | tf_op | source)
XLA Modules:
  0.0 36.4 jit_solution(9917840809091444205)
XLA Ops:
  1.3 1.2 %shard_map.78 = (bf16[65,8,128]{2,1,0:T(8,128)(2,1)S(1)}, bf16[65,8,128]{2,1,0:T(8,128)(2,1)S(1)}, bf16[65,8,128]{2,1,0:T(8,128)(2,1)S(1)}, bf16[1,8,128]{2,1,0:T(8,128)(2,1)S(1)}) custom-call(s32[1]{0:T(128)S(6)} %copy.8.counts_ref, bf16[8,32,512]{2,1,0:T(8,128)(2,1)} %vis_hbm.3, bf16[8,32,512]{2,1,0:T(8,128)(2,1)} %sky_hbm.3, s32[32,512]{1,0:T(8,128)} %mask_hbm.3, ...), custom_call_target="tpu_custom_call" | custom-call | tf_op jit(solution)/shard_map/pallas_call | solution.py:438
  2.5 3.1 %collective-permute-start.1 = (bf16[65,8,128]{2,1,0:T(8,128)(2,1)S(1)}, bf16[65,8,128]{2,1,0:T(8,128)(2,1)S(1)}, u32[]{:S(2)}, u32[]{:S(2)}) collective-permute-start(bf16[65,8,128]{2,1,0:T(8,128)(2,1)S(1)} %get-tuple-element.25), channel_id=1, source_target_pairs={{0,4},{1,5},{2,6},{3,7},{4,0},{5,1},{6,2},{7,3},{8,12},{9,13},{10,... | collective-permute-start | bytes 399368 | tf_op jit(solution)/shard_map/ppermute | solution.py:517
  5.6 2.5 %collective-permute-start = (bf16[65,8,128]{2,1,0:T(8,128)(2,1)S(1)}, bf16[65,8,128]{2,1,0:T(8,128)(2,1)S(1)}, u32[]{:S(2)}, u32[]{:S(2)}) collective-permute-start(bf16[65,8,128]{2,1,0:T(8,128)(2,1)S(1)} %get-tuple-element.23), channel_id=1, source_target_pairs={{0,12},{1,9},{2,14},{3,11},{4,8},{5,13},{6,10},{7,15},{8,4},{9,1},... | collective-permute-start | bytes 399368 | tf_op jit(solution)/shard_map/ppermute | solution.py:517
  8.1 0.9 %shard_map.77 = bf16[64,8,128]{2,1,0:T(8,128)(2,1)S(1)} custom-call(bf16[8,32,512]{2,1,0:T(8,128)(2,1)} %vis_hbm.3, bf16[8,32,512]{2,1,0:T(8,128)(2,1)} %sky_hbm.3, s32[32,512]{1,0:T(8,128)} %mask_hbm.3), custom_call_target="tpu_custom_call" | custom-call | tf_op jit(solution)/shard_map/pallas_call | solution.py:438
  9.1 0.2 collective-permute-start.3
  9.2 2.8 %collective-permute-start.2 = (bf16[1,8,128]{2,1,0:T(8,128)(2,1)S(1)}, bf16[1,8,128]{2,1,0:T(8,128)(2,1)S(1)}, u32[]{:S(2)}, u32[]{:S(2)}) collective-permute-start(bf16[1,8,128]{2,1,0:T(8,128)(2,1)S(1)} %get-tuple-element.26), channel_id=1, source_target_pairs={{0,8},{1,13},{2,10},{3,15},{4,12},{5,9},{6,14},{7,11},{8,0},{9,5},... | collective-permute-start | bytes 6152 | tf_op jit(solution)/shard_map/ppermute | solution.py:517
  12.0 0.7 %shard_map.79 = (f32[12,8,512]{2,1,0:T(8,128)S(1)}, bf16[4,1024,128]{2,1,0:T(8,128)(2,1)S(1)}, f32[48,512]{1,0:T(8,128)S(1)}, bf16[8,512,128]{2,1,0:T(8,128)(2,1)S(1)}) custom-call(bf16[65,8,128]{2,1,0:T(8,128)(2,1)S(1)} %get-tuple-element.24.chunk_ref.ends_ref.refs_1_, bf16[65,8,128]{2,1,0:T(8,128)(2,1)S(1)} %get-tuple-element.24.chunk_ref.ends_ref.refs_1_), custom_call_target="tpu_custom_call" | custom-call | tf_op jit(solution)/shard_map/pallas_call | solution.py:438
  12.7 7.4 %collective-permute-done.2.ends_ref.refs_3_ = bf16[1,8,128]{2,1,0:T(8,128)(2,1)S(1)} collective-permute-done((bf16[1,8,128]{2,1,0:T(8,128)(2,1)S(1)}, bf16[1,8,128]{2,1,0:T(8,128)(2,1)S(1)}, u32[]{:S(2)}, u32[]{:S(2)}) %collective-permute-start.2) | collective-permute-done | bytes 2080 | tf_op jit(solution)/shard_map/ppermute | solution.py:517
  20.2 0.0 collective-permute-done.3.chunk_ref
  20.2 0.6 %shard_map.81 = (f32[12,8,512]{2,1,0:T(8,128)S(1)}, bf16[4,1024,128]{2,1,0:T(8,128)(2,1)S(1)}, f32[48,512]{1,0:T(8,128)S(1)}) custom-call(bf16[64,8,128]{2,1,0:T(8,128)(2,1)S(1)} %collective-permute-done.3.chunk_ref, bf16[1,8,128]{2,1,0:T(8,128)(2,1)S(1)} %collective-permute-done.2.ends_ref.refs_3_), custom_call_target="tpu_custom_call" | custom-call | tf_op jit(solution)/shard_map/pallas_call | solution.py:438
  20.8 0.0 collective-permute-done.1.chunk_ref.ends_ref.refs_2_
  20.8 0.6 %shard_map.80 = (f32[12,8,512]{2,1,0:T(8,128)S(1)}, bf16[4,1024,128]{2,1,0:T(8,128)(2,1)S(1)}, f32[48,512]{1,0:T(8,128)S(1)}) custom-call(bf16[65,8,128]{2,1,0:T(8,128)(2,1)S(1)} %collective-permute-done.1.chunk_ref.ends_ref.refs_2_, bf16[65,8,128]{2,1,0:T(8,128)(2,1)S(1)} %collective-permute-done.1.chunk_ref.ends_ref.refs_2_), custom_call_target="tpu_custom_call" | custom-call | tf_op jit(solution)/shard_map/pallas_call | solution.py:438
  21.4 0.0 collective-permute-done.refs_0_.refs_4_
  21.4 0.0 copy-start
  21.4 1.7 %shard_map.82 = (f32[32,128]{1,0:T(8,128)S(1)}, f32[32,128]{1,0:T(8,128)S(1)}, f32[32,128]{1,0:T(8,128)S(1)}, f32[32,128]{1,0:T(8,128)S(1)}) custom-call(bf16[65,8,128]{2,1,0:T(8,128)(2,1)S(1)} %collective-permute-done.refs_0_.refs_4_, bf16[65,8,128]{2,1,0:T(8,128)(2,1)S(1)} %get-tuple-element.24.chunk_ref.ends_ref.refs_1_, ...), custom_call_target="tpu_custom_call" | custom-call | tf_op jit(solution)/shard_map/pallas_call | solution.py:438
  23.1 0.1 collective-permute-start.4
  23.2 3.0 %collective-permute-start.5 = (f32[32,128]{1,0:T(8,128)S(1)}, f32[32,128]{1,0:T(8,128)S(1)}, u32[]{:S(2)}, u32[]{:S(2)}) collective-permute-start(f32[32,128]{1,0:T(8,128)S(1)} %get-tuple-element.40), channel_id=1, source_target_pairs={{0,8},{1,5},{2,10},{3,7},{4,12},{5,1},{6,14},{7,3},{8,0},{9,13},{1... | collective-permute-start | bytes 49160 | tf_op jit(solution)/shard_map/ppermute | solution.py:556
  26.2 1.4 %collective-permute-start.6 = (f32[32,128]{1,0:T(8,128)S(1)}, f32[32,128]{1,0:T(8,128)S(1)}, u32[]{:S(2)}, u32[]{:S(2)}) collective-permute-start(f32[32,128]{1,0:T(8,128)S(1)} %get-tuple-element.41), channel_id=1, source_target_pairs={{0,12},{1,13},{2,14},{3,15},{4,8},{5,9},{6,10},{7,11},{8,4},{9,5},... | collective-permute-start | bytes 49160 | tf_op jit(solution)/shard_map/ppermute | solution.py:556
  27.6 0.0 copy-done
  27.6 0.0 collective-permute-done.4.refs_1_
  27.6 0.3 collective-permute-done.5.refs_2_
  27.9 3.8 %collective-permute-done.6.refs_3_ = f32[32,128]{1,0:T(8,128)S(1)} collective-permute-done((f32[32,128]{1,0:T(8,128)S(1)}, f32[32,128]{1,0:T(8,128)S(1)}, u32[]{:S(2)}, u32[]{:S(2)}) %collective-permute-start.6) | collective-permute-done | bytes 16416 | tf_op jit(solution)/shard_map/ppermute | solution.py:556
  31.8 0.1 shard_map.84
  31.9 0.1 collective-permute-start.9
  31.9 1.6 %collective-permute-start.8 = (f32[16,128]{1,0:T(8,128)S(1)}, f32[16,128]{1,0:T(8,128)S(1)}, u32[]{:S(2)}, u32[]{:S(2)}) collective-permute-start(f32[16,128]{1,0:T(8,128)S(1)} %shard_map.84), channel_id=1, source_target_pairs={{0,2},{1,3},{2,0},{3,1},{4,6},{5,7},{6,4},{7,5},{8,10},{9,11},{10,... | collective-permute-start | bytes 24584 | tf_op jit(solution)/shard_map/ppermute | solution.py:570
  33.5 0.3 collective-permute-start.7
  33.8 0.2 dynamic-slice_reduce_fusion.3
  34.0 0.6 %shard_map.83 = f32[4,32,128]{2,1,0:T(8,128)} custom-call(f32[32,128]{1,0:T(8,128)S(1)} %get-tuple-element.38.refs_0_, f32[32,128]{1,0:T(8,128)S(1)} %collective-permute-done.4.refs_1_, f32[32,128]{1,0:T(8,128)S(1)} %collective-permute-done.5.refs_2_, f32[32,128]{1,0:T(8,128)S(1)} %collective-permute-done.6.refs_3_), custom_call_target="tpu_custom_call" | custom-call | tf_op jit(solution)/shard_map/pallas_call | solution.py:438
  34.7 0.4 %collective-permute-done.9 = f32[16,128]{1,0:T(8,128)S(1)} collective-permute-done((f32[16,128]{1,0:T(8,128)S(1)}, f32[16,128]{1,0:T(8,128)S(1)}, u32[]{:S(2)}, u32[]{:S(2)}) %collective-permute-start.9) | collective-permute-done | bytes 8224 | tf_op jit(solution)/shard_map/ppermute | solution.py:570
  35.0 0.6 %collective-permute-done.8 = f32[16,128]{1,0:T(8,128)S(1)} collective-permute-done((f32[16,128]{1,0:T(8,128)S(1)}, f32[16,128]{1,0:T(8,128)S(1)}, u32[]{:S(2)}, u32[]{:S(2)}) %collective-permute-start.8) | collective-permute-done | bytes 8224 | tf_op jit(solution)/shard_map/ppermute | solution.py:570
  35.7 0.0 collective-permute-done.7
  35.7 0.7 %multiply_add_fusion = f32[2,2,32,128]{3,2,1,0:T(8,128)} fusion(f32[2,2,128]{2,1,0:T(2,128)S(1)} %bitcast.7, f32[32]{0:T(128)S(1)} %get-tuple-element.43, f32[2,2,128]{2,1,0:T(2,128)S(1)} %bitcast.8, f32[32]{0:T(128)S(1)} %get-tuple-element.44, f32[2,2,128]{2,1,0:T(2,128)S(1)} %bitcast.9, f32[32]{0:T(128)S(1)} %get-tuple-element.45, ...), kind=kLoop, calls=%fused_computation | loop fusion | flops 114688 | bytes 74240 | tf_op jit(solution)/shard_map/add | solution.py:572
  (3 shorter events, 0.0 us)
Async XLA Ops:
  2.5 18.2 %collective-permute-start.1 = (bf16[65,8,128]{2,1,0:T(8,128)(2,1)S(1)}, bf16[65,8,128]{2,1,0:T(8,128)(2,1)S(1)}, u32[]{:S(2)}, u32[]{:S(2)}) collective-permute-start(bf16[65,8,128]{2,1,0:T(8,128)(2,1)S(1)} %get-tuple-element.25), channel_id=1, source_target_pairs={{0,4},{1,5},{2,6},{3,7},{4,0},{5,1},{6,2},{7,3},{8,12},{9,13},{10,... | collective-permute-start | bytes 399368 | tf_op jit(solution)/shard_map/ppermute | solution.py:517
  5.6 15.7 %collective-permute-start = (bf16[65,8,128]{2,1,0:T(8,128)(2,1)S(1)}, bf16[65,8,128]{2,1,0:T(8,128)(2,1)S(1)}, u32[]{:S(2)}, u32[]{:S(2)}) collective-permute-start(bf16[65,8,128]{2,1,0:T(8,128)(2,1)S(1)} %get-tuple-element.23), channel_id=1, source_target_pairs={{0,12},{1,9},{2,14},{3,11},{4,8},{5,13},{6,10},{7,15},{8,4},{9,1},... | collective-permute-start | bytes 399368 | tf_op jit(solution)/shard_map/ppermute | solution.py:517
  9.1 11.1 %collective-permute-start.3 = (bf16[64,8,128]{2,1,0:T(8,128)(2,1)S(1)}, bf16[64,8,128]{2,1,0:T(8,128)(2,1)S(1)}, u32[]{:S(2)}, u32[]{:S(2)}) collective-permute-start(bf16[64,8,128]{2,1,0:T(8,128)(2,1)S(1)} %shard_map.77), channel_id=1, source_target_pairs={{0,8},{1,13},{2,10},{3,15},{4,12},{5,9},{6,14},{7,11},{8,0},{9,5},... | collective-permute-start | bytes 393224 | tf_op jit(solution)/shard_map/ppermute | solution.py:517
  9.2 10.9 %collective-permute-start.2 = (bf16[1,8,128]{2,1,0:T(8,128)(2,1)S(1)}, bf16[1,8,128]{2,1,0:T(8,128)(2,1)S(1)}, u32[]{:S(2)}, u32[]{:S(2)}) collective-permute-start(bf16[1,8,128]{2,1,0:T(8,128)(2,1)S(1)} %get-tuple-element.26), channel_id=1, source_target_pairs={{0,8},{1,13},{2,10},{3,15},{4,12},{5,9},{6,14},{7,11},{8,0},{9,5},... | collective-permute-start | bytes 6152 | tf_op jit(solution)/shard_map/ppermute | solution.py:517
  21.4 6.2 %copy-start = (f32[128,4]{1,0:T(8,128)S(1)}, f32[128,4]{1,0:T(8,128)}, u32[]{:S(2)}) copy-start(f32[128,4]{1,0:T(8,128)} %constant.12.clone) | copy-start | bytes 6148
  23.1 4.5 %collective-permute-start.4 = (f32[32,128]{1,0:T(8,128)S(1)}, f32[32,128]{1,0:T(8,128)S(1)}, u32[]{:S(2)}, u32[]{:S(2)}) collective-permute-start(f32[32,128]{1,0:T(8,128)S(1)} %get-tuple-element.39), channel_id=1, source_target_pairs={{0,4},{1,9},{2,6},{3,11},{4,0},{5,13},{6,2},{7,15},{8,12},{9,1},{1... | collective-permute-start | bytes 49160 | tf_op jit(solution)/shard_map/ppermute | solution.py:556
  23.2 4.7 %collective-permute-start.5 = (f32[32,128]{1,0:T(8,128)S(1)}, f32[32,128]{1,0:T(8,128)S(1)}, u32[]{:S(2)}, u32[]{:S(2)}) collective-permute-start(f32[32,128]{1,0:T(8,128)S(1)} %get-tuple-element.40), channel_id=1, source_target_pairs={{0,8},{1,5},{2,10},{3,7},{4,12},{5,1},{6,14},{7,3},{8,0},{9,13},{1... | collective-permute-start | bytes 49160 | tf_op jit(solution)/shard_map/ppermute | solution.py:556
  26.2 5.5 %collective-permute-start.6 = (f32[32,128]{1,0:T(8,128)S(1)}, f32[32,128]{1,0:T(8,128)S(1)}, u32[]{:S(2)}, u32[]{:S(2)}) collective-permute-start(f32[32,128]{1,0:T(8,128)S(1)} %get-tuple-element.41), channel_id=1, source_target_pairs={{0,12},{1,13},{2,14},{3,15},{4,8},{5,9},{6,10},{7,11},{8,4},{9,5},... | collective-permute-start | bytes 49160 | tf_op jit(solution)/shard_map/ppermute | solution.py:556
  31.9 3.2 %collective-permute-start.9 = (f32[16,128]{1,0:T(8,128)S(1)}, f32[16,128]{1,0:T(8,128)S(1)}, u32[]{:S(2)}, u32[]{:S(2)}) collective-permute-start(f32[16,128]{1,0:T(8,128)S(1)} %shard_map.84), channel_id=1, source_target_pairs={{0,3},{1,2},{2,1},{3,0},{4,7},{5,6},{6,5},{7,4},{8,11},{9,10},{10,... | collective-permute-start | bytes 24584 | tf_op jit(solution)/shard_map/ppermute | solution.py:570
  31.9 3.7 %collective-permute-start.8 = (f32[16,128]{1,0:T(8,128)S(1)}, f32[16,128]{1,0:T(8,128)S(1)}, u32[]{:S(2)}, u32[]{:S(2)}) collective-permute-start(f32[16,128]{1,0:T(8,128)S(1)} %shard_map.84), channel_id=1, source_target_pairs={{0,2},{1,3},{2,0},{3,1},{4,6},{5,7},{6,4},{7,5},{8,10},{9,11},{10,... | collective-permute-start | bytes 24584 | tf_op jit(solution)/shard_map/ppermute | solution.py:570
  33.5 2.2 %collective-permute-start.7 = (f32[16,128]{1,0:T(8,128)S(1)}, f32[16,128]{1,0:T(8,128)S(1)}, u32[]{:S(2)}, u32[]{:S(2)}) collective-permute-start(f32[16,128]{1,0:T(8,128)S(1)} %shard_map.84), channel_id=1, source_target_pairs={{0,1},{1,0},{2,3},{3,2},{4,5},{5,4},{6,7},{7,6},{8,9},{9,8},{10,11... | collective-permute-start | bytes 24584 | tf_op jit(solution)/shard_map/ppermute | solution.py:570
